TPU v7x, 128 devices: a whole 4x4x4 slice. The times are simulated.
128 devices in a mesh: draw: 8 (over z_lo, y), width: 8 (over x, core), cores: 2 (over z_hi).
Axes of the slice: x: 4, y: 4, z: 4 (z_hi: 2, z_lo: 2; z = z_hi * 2 + z_lo), core: 2. Of those that a mesh axis runs over, the one named last changes fastest.
Arguments:
- warmth_history: float32 [10, 4096, 2048], P(None, ('draw', 'width', 'cores')), may hold values from 0.9 to 1.1
- fictitious_warmth: float32 [4096, 2048], P('draw', ('width', 'cores')), may hold values from 0.9 to 1.1
- vertex_velocity: float32 [2, 4096, 2048], P(None, 'draw', ('width', 'cores')), may hold values from -6 to 6
- branch_load_tensors: float32 [12, 3, 4096, 2048], P(None, None, 'draw', ('width', 'cores')), may hold values from -2 to 2
- mechanism_lifetimes: float32 [12], replicated, may hold values from 0.3 to 30
- branch_stiffness: float32 [12], replicated, may hold values from 0.005 to 0.025
Outputs:
- fictive_final: float32 [4096, 2048], P('draw', ('width', 'cores'))
- velocity_final: float32 [2, 4096, 2048], P(None, 'draw', ('width', 'cores'))
- modes_final: float32 [12, 3, 4096, 2048], P(None, None, 'draw', ('width', 'cores'))
All inputs are finite; a program needn't handle non-finite values.
Results may differ from a plain program's by a relative error of at most 0.0001.
Values sent between devices are 32-bit elements; how exact they have to be, the bound alone decides.
No kernel may reach another device: no remote copies, remote signals or barrier semaphores. Data moves between devices by JAX's collectives and lax.ppermute only.
A program may use at most 128 MiB of HBM per device.

v0:
```python
import jax
import jax.numpy as jnp
from jax import lax
from jax.sharding import PartitionSpec as P

clock_increment = 1.0
arrhenius_energy = 20.0
coupling_exponent = 0.5
reduced_clock = 3.0


def shifted(shard, axis, by):
    peers = lax.axis_size(axis)
    pairs = [(i, i + by) for i in range(peers) if 0 <= i + by < peers]
    return lax.ppermute(shard, axis, pairs)


def heat_terms(heat_block):
    return (heat_block, arrhenius_energy * coupling_exponent / heat_block - arrhenius_energy)


def strain_field(motion):
    next_row = shifted(motion[:, :1, :], "draw", -1)
    below = jnp.concatenate([motion[:, 1:, :], next_row], axis=1)
    right_here, right_below = shifted((motion[:, :, 0], below[:, :, 0]), ("width", "cores"), -1)
    beside = jnp.concatenate([motion[:, :, 1:], right_here[:, :, None]], axis=2)
    corner = jnp.concatenate([below[:, :, 1:], right_below[:, :, None]], axis=2)
    grad_len = 0.5 * (below + corner - (motion + beside))
    grad_wid = 0.5 * (beside + corner - (motion + below))
    return jnp.stack([grad_len[0], grad_wid[1], 0.5 * (grad_wid[0] + grad_len[1])])


def nodal_field(stress):
    along_len = -0.5 * jnp.stack([stress[0], stress[2]])
    along_wid = -0.5 * jnp.stack([stress[2], stress[1]])
    node_base = -along_len - along_wid
    node_down = along_len - along_wid
    node_right = along_wid - along_len
    node_diag = along_len + along_wid
    left_base, left_diag = shifted(
        (node_right[:, :, -1], node_diag[:, :, -1]), ("width", "cores"), 1
    )
    row_here = node_base + jnp.concatenate([left_base[:, :, None], node_right[:, :, :-1]], axis=2)
    row_next = node_down + jnp.concatenate([left_diag[:, :, None], node_diag[:, :, :-1]], axis=2)
    from_above = shifted(row_next[:, -1:, :], "draw", 1)
    return row_here + jnp.concatenate([from_above, row_next[:, :-1, :]], axis=1)


def relax_mode(stress_mode, relax_time, modulus, strain, multiplier):
    rate_ratio = clock_increment / (relax_time * multiplier)
    kept = jnp.exp(-rate_ratio)
    weight = -jnp.expm1(-rate_ratio) / rate_ratio
    return kept * stress_mode + 2.0 * clock_increment * modulus * weight * strain


def shards(
    warmth_history,
    fictitious_warmth,
    vertex_velocity,
    branch_load_tensors,
    mechanism_lifetimes,
    branch_stiffness,
):
    tick_ordinal = warmth_history.shape[0]
    piece_lines = warmth_history.shape[1]
    entire_breadth = warmth_history.shape[2]
    row_count = vertex_velocity.shape[1]
    col_count = vertex_velocity.shape[2]
    sheet_pieces = warmth_history.reshape(tick_ordinal, 1, piece_lines, entire_breadth)
    arrived_block = lax.all_to_all(
        sheet_pieces, ("width", "cores"), split_axis=3, concat_axis=1, tiled=True
    )
    heat_all, term_all = heat_terms(
        arrived_block.reshape(arrived_block.shape[0], row_count, col_count)
    )
    update_modes = jax.vmap(relax_mode, in_axes=(0, 0, 0, None, None))

    def march_forward(locator_now, state_now):
        fictive_now, motion, mode_state = state_now
        warmth_now = lax.dynamic_index_in_dim(heat_all, locator_now, 0, keepdims=False)
        warming_contribution = lax.dynamic_index_in_dim(term_all, locator_now, 0, keepdims=False)
        multiplier = jnp.exp(
            warming_contribution + arrhenius_energy * (1.0 - coupling_exponent) / fictive_now
        )
        fictive_next = warmth_now + (fictive_now - warmth_now) * jnp.exp(
            -clock_increment / (reduced_clock * multiplier)
        )
        strain = strain_field(motion)
        mode_next = update_modes(
            mode_state, mechanism_lifetimes, branch_stiffness, strain, multiplier
        )
        stress = jnp.sum(mode_next, axis=0)
        motion_next = motion + clock_increment * nodal_field(stress)
        return (fictive_next, motion_next, mode_next)

    return lax.fori_loop(
        0, tick_ordinal, march_forward, (fictitious_warmth, vertex_velocity, branch_load_tensors)
    )


def solution(mesh):
    in_specs = (
        P(None, ("draw", "width", "cores"), None),
        P("draw", ("width", "cores")),
        P(None, "draw", ("width", "cores")),
        P(None, None, "draw", ("width", "cores")),
        P(),
        P(),
    )
    out_specs = (
        P("draw", ("width", "cores")),
        P(None, "draw", ("width", "cores")),
        P(None, None, "draw", ("width", "cores")),
    )
    return jax.shard_map(shards, mesh=mesh, in_specs=in_specs, out_specs=out_specs, check_vma=False)
```

profile of v0, /device:TPU:5, one launch (start us, length us, event | category | flops | bytes accessed | tf_op | source)
XLA Modules:
  0.0 753.7 jit_solution(2050167849661055217)
XLA Ops:
  0.7 8.6 %copy.74 = f32[12,3,512,128]{3,2,1,0:T(8,128)} copy(f32[12,3,512,128]{3,2,1,0:T(8,128)} %param.11) | data formatting | bytes 18874368
  9.9 15.1 %copy.45 = f32[10,1,32,2048]{2,1,0,3:T(1,128)} copy(f32[10,1,32,2048]{3,2,0,1:T(8,128)S(1)} %bitcast.49) | data formatting | bytes 5242880 | tf_op jit(solution)/shard_map/reshape | solution.py:69
  25.6 94.9 %reduce.8 = f32[2048,10,32]{2,1,0:T(8,128)} reduce(f32[2048,10,1,32]{3,2,1,0:T(1,128)} %bitcast.46, f32[]{:T(128)} %broadcast.140), dimensions={2}, to_apply=%bitcast.22.reduce_sub_computation | reduce | bytes 5242884
  120.5 15.1 %reshape.35 = f32[16,1,40960]{2,1,0:T(1,128)} reshape(f32[2048,10,32]{2,1,0:T(8,128)} %reduce.8) | data formatting | bytes 5242880
  135.6 8.4 %all-to-all-start = ((f32[16,1,40960]{2,1,0:T(1,128)}), f32[16,1,40960]{2,1,0:T(1,128)S(1)}, u32[]{:S(2)}, u32[]{:S(2)}) async-start(f32[16,1,40960]{2,1,0:T(1,128)} %reshape.35), calls=%async_computation | async-start | bytes 5242880 | tf_op jit(solution)/shard_map/all_to_all | solution.py:70
  144.1 41.4 %all-to-all-done = f32[16,1,40960]{2,1,0:T(1,128)S(1)} async-done(((f32[16,1,40960]{2,1,0:T(1,128)}), f32[16,1,40960]{2,1,0:T(1,128)S(1)}, u32[]{:S(2)}, u32[]{:S(2)}) %all-to-all-start) | async-done | bytes 2621472 | tf_op jit(solution)/shard_map/all_to_all | solution.py:70
  185.5 9.2 %reduce.9 = f32[16,40960]{1,0:T(8,128)} reduce(f32[16,1,40960]{2,1,0:T(1,128)S(1)} %all-to-all-done, f32[]{:T(128)} %broadcast.140), dimensions={1}, to_apply=%all_to_all.11.reduce_sub_computation | reduce | bytes 5242884 | tf_op jit(solution)/shard_map/all_to_all | solution.py:70
  194.7 24.0 %reshape.36 = f32[2048,10,1,32]{3,2,1,0:T(1,128)} reshape(f32[16,40960]{1,0:T(8,128)} %reduce.9) | data formatting | bytes 5242880
  218.6 22.0 %copy.46 = f32[10,1,32,2048]{3,1,2,0:T(1,128)S(1)} copy(f32[10,1,32,2048]{2,1,0,3:T(1,128)} %bitcast.47) | data formatting | bytes 5242880 | tf_op jit(solution)/shard_map/all_to_all | solution.py:70
  246.7 506.1 %while.17 = (s32[]{:T(128)}, f32[512,128]{1,0:T(8,128)}, f32[2,512,128]{2,1,0:T(8,128)S(1)}, f32[12,3,512,128]{3,2,1,0:T(8,128)}, f32[10,512,128]{2,1,0:T(8,128)...) while((s32[]{:T(128)}, f32[512,128]{1,0:T(8,128)}, ...), condition=%wide.region_2.3_spmd, body=%wide.region_0.2_spmd.sunk | while | flops 19660812 | bytes 53078544 | solution.py:96
  252.4 4.2 fusion.29
  263.6 11.8 %fusion.30 = (f32[3,512,128]{2,1,0:T(8,128)S(1)}, f32[12,3,512,128]{3,2,1,0:T(8,128)}) fusion(f32[3,512,128]{2,1,0:T(8,128)S(1)} %pad_maximum_fusion.5, f32[12,512,128]{2,1,0:T(8,128)} %get-tuple-element.262, f32[12,3,512,128]{3,2,1,0:T(8,128)} %get-tuple-element.283, f32[12,512,128]{2,1,0:T(8,128)} %get-tuple-element.263), kind=kLoop, calls=%fused_computation.37.clone.1 | loop fusion | flops 9240576 | bytes 26738688 | tf_op jit(solution)/shard_map/while/body/eval_jaxpr/reduce_sum | solution.py:92
  276.0 6.3 collective-permute-start.3
  283.9 5.1 collective-permute-start.4
  300.5 4.2 fusion.29
  311.9 11.8 %fusion.30 = (f32[3,512,128]{2,1,0:T(8,128)S(1)}, f32[12,3,512,128]{3,2,1,0:T(8,128)}) fusion(f32[3,512,128]{2,1,0:T(8,128)S(1)} %pad_maximum_fusion.5, f32[12,512,128]{2,1,0:T(8,128)} %get-tuple-element.262, f32[12,3,512,128]{3,2,1,0:T(8,128)} %get-tuple-element.283, f32[12,512,128]{2,1,0:T(8,128)} %get-tuple-element.263), kind=kLoop, calls=%fused_computation.37.clone.1 | loop fusion | flops 9240576 | bytes 26738688 | tf_op jit(solution)/shard_map/while/body/eval_jaxpr/reduce_sum | solution.py:92
  324.3 5.2 collective-permute-start.3
  331.5 4.7 collective-permute-start.4
  336.2 4.2 collective-permute-start.5
  348.4 4.2 fusion.29
  353.1 5.2 collective-permute-start.2
  360.0 11.8 %fusion.30 = (f32[3,512,128]{2,1,0:T(8,128)S(1)}, f32[12,3,512,128]{3,2,1,0:T(8,128)}) fusion(f32[3,512,128]{2,1,0:T(8,128)S(1)} %pad_maximum_fusion.5, f32[12,512,128]{2,1,0:T(8,128)} %get-tuple-element.262, f32[12,3,512,128]{3,2,1,0:T(8,128)} %get-tuple-element.283, f32[12,512,128]{2,1,0:T(8,128)} %get-tuple-element.263), kind=kLoop, calls=%fused_computation.37.clone.1 | loop fusion | flops 9240576 | bytes 26738688 | tf_op jit(solution)/shard_map/while/body/eval_jaxpr/reduce_sum | solution.py:92
  372.3 6.3 collective-permute-start.3
  380.2 5.7 collective-permute-start.4
  386.0 4.2 collective-permute-start.5
  397.5 4.2 fusion.29
  402.2 5.4 collective-permute-start.2
  409.8 11.8 %fusion.30 = (f32[3,512,128]{2,1,0:T(8,128)S(1)}, f32[12,3,512,128]{3,2,1,0:T(8,128)}) fusion(f32[3,512,128]{2,1,0:T(8,128)S(1)} %pad_maximum_fusion.5, f32[12,512,128]{2,1,0:T(8,128)} %get-tuple-element.262, f32[12,3,512,128]{3,2,1,0:T(8,128)} %get-tuple-element.283, f32[12,512,128]{2,1,0:T(8,128)} %get-tuple-element.263), kind=kLoop, calls=%fused_computation.37.clone.1 | loop fusion | flops 9240576 | bytes 26738688 | tf_op jit(solution)/shard_map/while/body/eval_jaxpr/reduce_sum | solution.py:92
  422.1 6.3 collective-permute-start.3
  430.0 5.7 collective-permute-start.4
  435.7 4.8 collective-permute-start.5
  447.5 4.2 fusion.29
  452.1 4.9 collective-permute-start.2
  460.1 11.8 %fusion.30 = (f32[3,512,128]{2,1,0:T(8,128)S(1)}, f32[12,3,512,128]{3,2,1,0:T(8,128)}) fusion(f32[3,512,128]{2,1,0:T(8,128)S(1)} %pad_maximum_fusion.5, f32[12,512,128]{2,1,0:T(8,128)} %get-tuple-element.262, f32[12,3,512,128]{3,2,1,0:T(8,128)} %get-tuple-element.283, f32[12,512,128]{2,1,0:T(8,128)} %get-tuple-element.263), kind=kLoop, calls=%fused_computation.37.clone.1 | loop fusion | flops 9240576 | bytes 26738688 | tf_op jit(solution)/shard_map/while/body/eval_jaxpr/reduce_sum | solution.py:92
  472.5 6.3 collective-permute-start.3
  480.4 5.7 collective-permute-start.4
  486.1 6.3 collective-permute-start.5
  499.3 4.2 fusion.29
  504.0 4.6 collective-permute-start.2
  512.0 11.8 %fusion.30 = (f32[3,512,128]{2,1,0:T(8,128)S(1)}, f32[12,3,512,128]{3,2,1,0:T(8,128)}) fusion(f32[3,512,128]{2,1,0:T(8,128)S(1)} %pad_maximum_fusion.5, f32[12,512,128]{2,1,0:T(8,128)} %get-tuple-element.262, f32[12,3,512,128]{3,2,1,0:T(8,128)} %get-tuple-element.283, f32[12,512,128]{2,1,0:T(8,128)} %get-tuple-element.263), kind=kLoop, calls=%fused_computation.37.clone.1 | loop fusion | flops 9240576 | bytes 26738688 | tf_op jit(solution)/shard_map/while/body/eval_jaxpr/reduce_sum | solution.py:92
  524.3 6.3 collective-permute-start.3
  532.2 5.7 collective-permute-start.4
  537.9 6.3 collective-permute-start.5
  551.2 4.2 fusion.29
  555.8 4.6 collective-permute-start.2
  563.8 11.8 %fusion.30 = (f32[3,512,128]{2,1,0:T(8,128)S(1)}, f32[12,3,512,128]{3,2,1,0:T(8,128)}) fusion(f32[3,512,128]{2,1,0:T(8,128)S(1)} %pad_maximum_fusion.5, f32[12,512,128]{2,1,0:T(8,128)} %get-tuple-element.262, f32[12,3,512,128]{3,2,1,0:T(8,128)} %get-tuple-element.283, f32[12,512,128]{2,1,0:T(8,128)} %get-tuple-element.263), kind=kLoop, calls=%fused_computation.37.clone.1 | loop fusion | flops 9240576 | bytes 26738688 | tf_op jit(solution)/shard_map/while/body/eval_jaxpr/reduce_sum | solution.py:92
  576.2 6.3 collective-permute-start.3
  584.1 5.7 collective-permute-start.4
  589.8 6.3 collective-permute-start.5
  607.7 4.6 collective-permute-start.2
  615.7 11.8 %fusion.30 = (f32[3,512,128]{2,1,0:T(8,128)S(1)}, f32[12,3,512,128]{3,2,1,0:T(8,128)}) fusion(f32[3,512,128]{2,1,0:T(8,128)S(1)} %pad_maximum_fusion.5, f32[12,512,128]{2,1,0:T(8,128)} %get-tuple-element.262, f32[12,3,512,128]{3,2,1,0:T(8,128)} %get-tuple-element.283, f32[12,512,128]{2,1,0:T(8,128)} %get-tuple-element.263), kind=kLoop, calls=%fused_computation.37.clone.1 | loop fusion | flops 9240576 | bytes 26738688 | tf_op jit(solution)/shard_map/while/body/eval_jaxpr/reduce_sum | solution.py:92
  628.0 6.3 collective-permute-start.3
  635.9 5.7 collective-permute-start.4
  641.6 6.3 collective-permute-start.5
  659.5 4.6 collective-permute-start.2
  667.5 11.8 %fusion.30 = (f32[3,512,128]{2,1,0:T(8,128)S(1)}, f32[12,3,512,128]{3,2,1,0:T(8,128)}) fusion(f32[3,512,128]{2,1,0:T(8,128)S(1)} %pad_maximum_fusion.5, f32[12,512,128]{2,1,0:T(8,128)} %get-tuple-element.262, f32[12,3,512,128]{3,2,1,0:T(8,128)} %get-tuple-element.283, f32[12,512,128]{2,1,0:T(8,128)} %get-tuple-element.263), kind=kLoop, calls=%fused_computation.37.clone.1 | loop fusion | flops 9240576 | bytes 26738688 | tf_op jit(solution)/shard_map/while/body/eval_jaxpr/reduce_sum | solution.py:92
  679.9 6.3 collective-permute-start.3
  687.8 5.7 collective-permute-start.4
  693.5 6.3 collective-permute-start.5
  711.4 4.6 collective-permute-start.2
  719.4 11.8 %fusion.30 = (f32[3,512,128]{2,1,0:T(8,128)S(1)}, f32[12,3,512,128]{3,2,1,0:T(8,128)}) fusion(f32[3,512,128]{2,1,0:T(8,128)S(1)} %pad_maximum_fusion.5, f32[12,512,128]{2,1,0:T(8,128)} %get-tuple-element.262, f32[12,3,512,128]{3,2,1,0:T(8,128)} %get-tuple-element.283, f32[12,512,128]{2,1,0:T(8,128)} %get-tuple-element.263), kind=kLoop, calls=%fused_computation.37.clone.1 | loop fusion | flops 9240576 | bytes 26738688 | tf_op jit(solution)/shard_map/while/body/eval_jaxpr/reduce_sum | solution.py:92
  731.7 6.3 collective-permute-start.3
  739.6 5.7 collective-permute-start.4
  745.4 6.3 collective-permute-start.5
  (322 shorter events, 156.8 us)
Async XLA Ops:
  0.6 8.6 %copy-start.3 = (f32[512,128]{1,0:T(8,128)S(1)}, f32[512,128]{1,0:T(8,128)}, u32[]{:S(2)}) copy-start(f32[512,128]{1,0:T(8,128)} %param.9) | copy-start | bytes 786436
  0.6 9.3 %copy-start.2 = (f32[10,32,2048]{2,1,0:T(8,128)S(1)}, f32[10,32,2048]{2,1,0:T(8,128)}, u32[]{:S(2)}) copy-start(f32[10,32,2048]{2,1,0:T(8,128)} %param.8) | copy-start | bytes 7864324
  135.6 49.9 %all-to-all-start = ((f32[16,1,40960]{2,1,0:T(1,128)}), f32[16,1,40960]{2,1,0:T(1,128)S(1)}, u32[]{:S(2)}, u32[]{:S(2)}) async-start(f32[16,1,40960]{2,1,0:T(1,128)} %reshape.35), calls=%async_computation | async-start | bytes 5242880 | tf_op jit(solution)/shard_map/all_to_all | solution.py:70
  243.0 3.7 copy-start.5
  247.0 9.9 %collective-permute-start = (f32[2,1,128]{2,1,0:T(1,128)S(1)}, f32[2,1,128]{2,1,0:T(1,128)S(1)}, u32[]{:S(2)}, u32[]{:S(2)}) collective-permute-start(f32[2,1,128]{2,1,0:T(1,128)S(1)} %slice.201), channel_id=1, source_target_pairs={{16,0},{32,16},{48,32},{64,48},{80,64},{96,80},{112,96},{17,1},{33... | collective-permute-start | bytes 3080 | tf_op jit(solution)/shard_map/while/body/eval_jaxpr/ppermute | solution.py:15
  248.5 11.5 %collective-permute-start.1 = (f32[2,512]{1,0:T(2,128)S(1)}, f32[2,512]{1,0:T(2,128)S(1)}, u32[]{:S(2)}, u32[]{:S(2)}) collective-permute-start(f32[2,512]{1,0:T(2,128)S(1)} %slice_reduce_fusion.6), channel_id=1, source_target_pairs={{1,0},{2,1},{3,2},{4,3},{5,4},{6,5},{7,6},{8,7},{9,8},{10,9},{11,1... | collective-permute-start | bytes 12296 | tf_op jit(solution)/shard_map/while/body/eval_jaxpr/ppermute | solution.py:15
  257.1 5.9 collective-permute-start.2
  276.0 7.1 collective-permute-start.3
  283.9 9.1 %collective-permute-start.4 = (f32[2,512]{1,0:T(2,128)S(1)}, f32[2,512]{1,0:T(2,128)S(1)}, u32[]{:S(2)}, u32[]{:S(2)}) collective-permute-start(f32[2,512]{1,0:T(2,128)S(1)} %slice_reduce_fusion.8), channel_id=1, source_target_pairs={{0,1},{1,2},{2,3},{3,4},{4,5},{5,6},{6,7},{7,8},{8,9},{9,10},{10,1... | collective-permute-start | bytes 12296 | tf_op jit(solution)/shard_map/while/body/eval_jaxpr/ppermute | solution.py:15
  289.0 4.7 collective-permute-start.5
  294.2 10.7 %collective-permute-start = (f32[2,1,128]{2,1,0:T(1,128)S(1)}, f32[2,1,128]{2,1,0:T(1,128)S(1)}, u32[]{:S(2)}, u32[]{:S(2)}) collective-permute-start(f32[2,1,128]{2,1,0:T(1,128)S(1)} %slice.201), channel_id=1, source_target_pairs={{16,0},{32,16},{48,32},{64,48},{80,64},{96,80},{112,96},{17,1},{33... | collective-permute-start | bytes 3080 | tf_op jit(solution)/shard_map/while/body/eval_jaxpr/ppermute | solution.py:15
  295.7 13.4 %collective-permute-start.1 = (f32[2,512]{1,0:T(2,128)S(1)}, f32[2,512]{1,0:T(2,128)S(1)}, u32[]{:S(2)}, u32[]{:S(2)}) collective-permute-start(f32[2,512]{1,0:T(2,128)S(1)} %slice_reduce_fusion.6), channel_id=1, source_target_pairs={{1,0},{2,1},{3,2},{4,3},{5,4},{6,5},{7,6},{8,7},{9,8},{10,9},{11,1... | collective-permute-start | bytes 12296 | tf_op jit(solution)/shard_map/while/body/eval_jaxpr/ppermute | solution.py:15
  305.1 6.1 collective-permute-start.2
  324.3 6.4 collective-permute-start.3
  331.5 9.0 %collective-permute-start.4 = (f32[2,512]{1,0:T(2,128)S(1)}, f32[2,512]{1,0:T(2,128)S(1)}, u32[]{:S(2)}, u32[]{:S(2)}) collective-permute-start(f32[2,512]{1,0:T(2,128)S(1)} %slice_reduce_fusion.8), channel_id=1, source_target_pairs={{0,1},{1,2},{2,3},{3,4},{4,5},{5,6},{6,7},{7,8},{8,9},{9,10},{10,1... | collective-permute-start | bytes 12296 | tf_op jit(solution)/shard_map/while/body/eval_jaxpr/ppermute | solution.py:15
  336.2 4.9 collective-permute-start.5
  341.6 11.2 %collective-permute-start = (f32[2,1,128]{2,1,0:T(1,128)S(1)}, f32[2,1,128]{2,1,0:T(1,128)S(1)}, u32[]{:S(2)}, u32[]{:S(2)}) collective-permute-start(f32[2,1,128]{2,1,0:T(1,128)S(1)} %slice.201), channel_id=1, source_target_pairs={{16,0},{32,16},{48,32},{64,48},{80,64},{96,80},{112,96},{17,1},{33... | collective-permute-start | bytes 3080 | tf_op jit(solution)/shard_map/while/body/eval_jaxpr/ppermute | solution.py:15
  343.2 15.3 %collective-permute-start.1 = (f32[2,512]{1,0:T(2,128)S(1)}, f32[2,512]{1,0:T(2,128)S(1)}, u32[]{:S(2)}, u32[]{:S(2)}) collective-permute-start(f32[2,512]{1,0:T(2,128)S(1)} %slice_reduce_fusion.6), channel_id=1, source_target_pairs={{1,0},{2,1},{3,2},{4,3},{5,4},{6,5},{7,6},{8,7},{9,8},{10,9},{11,1... | collective-permute-start | bytes 12296 | tf_op jit(solution)/shard_map/while/body/eval_jaxpr/ppermute | solution.py:15
  353.1 6.2 collective-permute-start.2
  372.3 7.1 collective-permute-start.3
  380.2 10.0 %collective-permute-start.4 = (f32[2,512]{1,0:T(2,128)S(1)}, f32[2,512]{1,0:T(2,128)S(1)}, u32[]{:S(2)}, u32[]{:S(2)}) collective-permute-start(f32[2,512]{1,0:T(2,128)S(1)} %slice_reduce_fusion.8), channel_id=1, source_target_pairs={{0,1},{1,2},{2,3},{3,4},{4,5},{5,6},{6,7},{7,8},{8,9},{9,10},{10,1... | collective-permute-start | bytes 12296 | tf_op jit(solution)/shard_map/while/body/eval_jaxpr/ppermute | solution.py:15
  386.0 4.9 collective-permute-start.5
  391.4 10.6 %collective-permute-start = (f32[2,1,128]{2,1,0:T(1,128)S(1)}, f32[2,1,128]{2,1,0:T(1,128)S(1)}, u32[]{:S(2)}, u32[]{:S(2)}) collective-permute-start(f32[2,1,128]{2,1,0:T(1,128)S(1)} %slice.201), channel_id=1, source_target_pairs={{16,0},{32,16},{48,32},{64,48},{80,64},{96,80},{112,96},{17,1},{33... | collective-permute-start | bytes 3080 | tf_op jit(solution)/shard_map/while/body/eval_jaxpr/ppermute | solution.py:15
  392.9 14.9 %collective-permute-start.1 = (f32[2,512]{1,0:T(2,128)S(1)}, f32[2,512]{1,0:T(2,128)S(1)}, u32[]{:S(2)}, u32[]{:S(2)}) collective-permute-start(f32[2,512]{1,0:T(2,128)S(1)} %slice_reduce_fusion.6), channel_id=1, source_target_pairs={{1,0},{2,1},{3,2},{4,3},{5,4},{6,5},{7,6},{8,7},{9,8},{10,9},{11,1... | collective-permute-start | bytes 12296 | tf_op jit(solution)/shard_map/while/body/eval_jaxpr/ppermute | solution.py:15
  402.2 6.9 collective-permute-start.2
  422.1 7.1 collective-permute-start.3
  430.0 10.6 %collective-permute-start.4 = (f32[2,512]{1,0:T(2,128)S(1)}, f32[2,512]{1,0:T(2,128)S(1)}, u32[]{:S(2)}, u32[]{:S(2)}) collective-permute-start(f32[2,512]{1,0:T(2,128)S(1)} %slice_reduce_fusion.8), channel_id=1, source_target_pairs={{0,1},{1,2},{2,3},{3,4},{4,5},{5,6},{6,7},{7,8},{8,9},{9,10},{10,1... | collective-permute-start | bytes 12296 | tf_op jit(solution)/shard_map/while/body/eval_jaxpr/ppermute | solution.py:15
  435.7 5.6 collective-permute-start.5
  441.8 10.1 %collective-permute-start = (f32[2,1,128]{2,1,0:T(1,128)S(1)}, f32[2,1,128]{2,1,0:T(1,128)S(1)}, u32[]{:S(2)}, u32[]{:S(2)}) collective-permute-start(f32[2,1,128]{2,1,0:T(1,128)S(1)} %slice.201), channel_id=1, source_target_pairs={{16,0},{32,16},{48,32},{64,48},{80,64},{96,80},{112,96},{17,1},{33... | collective-permute-start | bytes 3080 | tf_op jit(solution)/shard_map/while/body/eval_jaxpr/ppermute | solution.py:15
  443.3 14.0 %collective-permute-start.1 = (f32[2,512]{1,0:T(2,128)S(1)}, f32[2,512]{1,0:T(2,128)S(1)}, u32[]{:S(2)}, u32[]{:S(2)}) collective-permute-start(f32[2,512]{1,0:T(2,128)S(1)} %slice_reduce_fusion.6), channel_id=1, source_target_pairs={{1,0},{2,1},{3,2},{4,3},{5,4},{6,5},{7,6},{8,7},{9,8},{10,9},{11,1... | collective-permute-start | bytes 12296 | tf_op jit(solution)/shard_map/while/body/eval_jaxpr/ppermute | solution.py:15
  452.1 7.3 collective-permute-start.2
  472.5 7.1 collective-permute-start.3
  480.4 12.1 %collective-permute-start.4 = (f32[2,512]{1,0:T(2,128)S(1)}, f32[2,512]{1,0:T(2,128)S(1)}, u32[]{:S(2)}, u32[]{:S(2)}) collective-permute-start(f32[2,512]{1,0:T(2,128)S(1)} %slice_reduce_fusion.8), channel_id=1, source_target_pairs={{0,1},{1,2},{2,3},{3,4},{4,5},{5,6},{6,7},{7,8},{8,9},{9,10},{10,1... | collective-permute-start | bytes 12296 | tf_op jit(solution)/shard_map/while/body/eval_jaxpr/ppermute | solution.py:15
  486.1 7.1 collective-permute-start.5
  493.6 10.1 %collective-permute-start = (f32[2,1,128]{2,1,0:T(1,128)S(1)}, f32[2,1,128]{2,1,0:T(1,128)S(1)}, u32[]{:S(2)}, u32[]{:S(2)}) collective-permute-start(f32[2,1,128]{2,1,0:T(1,128)S(1)} %slice.201), channel_id=1, source_target_pairs={{16,0},{32,16},{48,32},{64,48},{80,64},{96,80},{112,96},{17,1},{33... | collective-permute-start | bytes 3080 | tf_op jit(solution)/shard_map/while/body/eval_jaxpr/ppermute | solution.py:15
  495.1 13.7 %collective-permute-start.1 = (f32[2,512]{1,0:T(2,128)S(1)}, f32[2,512]{1,0:T(2,128)S(1)}, u32[]{:S(2)}, u32[]{:S(2)}) collective-permute-start(f32[2,512]{1,0:T(2,128)S(1)} %slice_reduce_fusion.6), channel_id=1, source_target_pairs={{1,0},{2,1},{3,2},{4,3},{5,4},{6,5},{7,6},{8,7},{9,8},{10,9},{11,1... | collective-permute-start | bytes 12296 | tf_op jit(solution)/shard_map/while/body/eval_jaxpr/ppermute | solution.py:15
  504.0 7.3 collective-permute-start.2
  524.3 7.1 collective-permute-start.3
  532.2 12.1 %collective-permute-start.4 = (f32[2,512]{1,0:T(2,128)S(1)}, f32[2,512]{1,0:T(2,128)S(1)}, u32[]{:S(2)}, u32[]{:S(2)}) collective-permute-start(f32[2,512]{1,0:T(2,128)S(1)} %slice_reduce_fusion.8), channel_id=1, source_target_pairs={{0,1},{1,2},{2,3},{3,4},{4,5},{5,6},{6,7},{7,8},{8,9},{9,10},{10,1... | collective-permute-start | bytes 12296 | tf_op jit(solution)/shard_map/while/body/eval_jaxpr/ppermute | solution.py:15
  537.9 7.1 collective-permute-start.5
  545.5 10.1 %collective-permute-start = (f32[2,1,128]{2,1,0:T(1,128)S(1)}, f32[2,1,128]{2,1,0:T(1,128)S(1)}, u32[]{:S(2)}, u32[]{:S(2)}) collective-permute-start(f32[2,1,128]{2,1,0:T(1,128)S(1)} %slice.201), channel_id=1, source_target_pairs={{16,0},{32,16},{48,32},{64,48},{80,64},{96,80},{112,96},{17,1},{33... | collective-permute-start | bytes 3080 | tf_op jit(solution)/shard_map/while/body/eval_jaxpr/ppermute | solution.py:15
  547.0 13.7 %collective-permute-start.1 = (f32[2,512]{1,0:T(2,128)S(1)}, f32[2,512]{1,0:T(2,128)S(1)}, u32[]{:S(2)}, u32[]{:S(2)}) collective-permute-start(f32[2,512]{1,0:T(2,128)S(1)} %slice_reduce_fusion.6), channel_id=1, source_target_pairs={{1,0},{2,1},{3,2},{4,3},{5,4},{6,5},{7,6},{8,7},{9,8},{10,9},{11,1... | collective-permute-start | bytes 12296 | tf_op jit(solution)/shard_map/while/body/eval_jaxpr/ppermute | solution.py:15
  555.8 7.3 collective-permute-start.2
  576.2 7.1 collective-permute-start.3
  584.1 12.1 %collective-permute-start.4 = (f32[2,512]{1,0:T(2,128)S(1)}, f32[2,512]{1,0:T(2,128)S(1)}, u32[]{:S(2)}, u32[]{:S(2)}) collective-permute-start(f32[2,512]{1,0:T(2,128)S(1)} %slice_reduce_fusion.8), channel_id=1, source_target_pairs={{0,1},{1,2},{2,3},{3,4},{4,5},{5,6},{6,7},{7,8},{8,9},{9,10},{10,1... | collective-permute-start | bytes 12296 | tf_op jit(solution)/shard_map/while/body/eval_jaxpr/ppermute | solution.py:15
  589.8 7.1 collective-permute-start.5
  597.3 10.1 %collective-permute-start = (f32[2,1,128]{2,1,0:T(1,128)S(1)}, f32[2,1,128]{2,1,0:T(1,128)S(1)}, u32[]{:S(2)}, u32[]{:S(2)}) collective-permute-start(f32[2,1,128]{2,1,0:T(1,128)S(1)} %slice.201), channel_id=1, source_target_pairs={{16,0},{32,16},{48,32},{64,48},{80,64},{96,80},{112,96},{17,1},{33... | collective-permute-start | bytes 3080 | tf_op jit(solution)/shard_map/while/body/eval_jaxpr/ppermute | solution.py:15
  598.8 13.7 %collective-permute-start.1 = (f32[2,512]{1,0:T(2,128)S(1)}, f32[2,512]{1,0:T(2,128)S(1)}, u32[]{:S(2)}, u32[]{:S(2)}) collective-permute-start(f32[2,512]{1,0:T(2,128)S(1)} %slice_reduce_fusion.6), channel_id=1, source_target_pairs={{1,0},{2,1},{3,2},{4,3},{5,4},{6,5},{7,6},{8,7},{9,8},{10,9},{11,1... | collective-permute-start | bytes 12296 | tf_op jit(solution)/shard_map/while/body/eval_jaxpr/ppermute | solution.py:15
  607.7 7.3 collective-permute-start.2
  628.0 7.1 collective-permute-start.3
  635.9 12.1 %collective-permute-start.4 = (f32[2,512]{1,0:T(2,128)S(1)}, f32[2,512]{1,0:T(2,128)S(1)}, u32[]{:S(2)}, u32[]{:S(2)}) collective-permute-start(f32[2,512]{1,0:T(2,128)S(1)} %slice_reduce_fusion.8), channel_id=1, source_target_pairs={{0,1},{1,2},{2,3},{3,4},{4,5},{5,6},{6,7},{7,8},{8,9},{9,10},{10,1... | collective-permute-start | bytes 12296 | tf_op jit(solution)/shard_map/while/body/eval_jaxpr/ppermute | solution.py:15
  641.6 7.1 collective-permute-start.5
  649.2 10.1 %collective-permute-start = (f32[2,1,128]{2,1,0:T(1,128)S(1)}, f32[2,1,128]{2,1,0:T(1,128)S(1)}, u32[]{:S(2)}, u32[]{:S(2)}) collective-permute-start(f32[2,1,128]{2,1,0:T(1,128)S(1)} %slice.201), channel_id=1, source_target_pairs={{16,0},{32,16},{48,32},{64,48},{80,64},{96,80},{112,96},{17,1},{33... | collective-permute-start | bytes 3080 | tf_op jit(solution)/shard_map/while/body/eval_jaxpr/ppermute | solution.py:15
  650.7 13.7 %collective-permute-start.1 = (f32[2,512]{1,0:T(2,128)S(1)}, f32[2,512]{1,0:T(2,128)S(1)}, u32[]{:S(2)}, u32[]{:S(2)}) collective-permute-start(f32[2,512]{1,0:T(2,128)S(1)} %slice_reduce_fusion.6), channel_id=1, source_target_pairs={{1,0},{2,1},{3,2},{4,3},{5,4},{6,5},{7,6},{8,7},{9,8},{10,9},{11,1... | collective-permute-start | bytes 12296 | tf_op jit(solution)/shard_map/while/body/eval_jaxpr/ppermute | solution.py:15
  659.5 7.3 collective-permute-start.2
  679.9 7.1 collective-permute-start.3
  687.8 12.1 %collective-permute-start.4 = (f32[2,512]{1,0:T(2,128)S(1)}, f32[2,512]{1,0:T(2,128)S(1)}, u32[]{:S(2)}, u32[]{:S(2)}) collective-permute-start(f32[2,512]{1,0:T(2,128)S(1)} %slice_reduce_fusion.8), channel_id=1, source_target_pairs={{0,1},{1,2},{2,3},{3,4},{4,5},{5,6},{6,7},{7,8},{8,9},{9,10},{10,1... | collective-permute-start | bytes 12296 | tf_op jit(solution)/shard_map/while/body/eval_jaxpr/ppermute | solution.py:15
  693.5 7.1 collective-permute-start.5
  701.0 10.1 %collective-permute-start = (f32[2,1,128]{2,1,0:T(1,128)S(1)}, f32[2,1,128]{2,1,0:T(1,128)S(1)}, u32[]{:S(2)}, u32[]{:S(2)}) collective-permute-start(f32[2,1,128]{2,1,0:T(1,128)S(1)} %slice.201), channel_id=1, source_target_pairs={{16,0},{32,16},{48,32},{64,48},{80,64},{96,80},{112,96},{17,1},{33... | collective-permute-start | bytes 3080 | tf_op jit(solution)/shard_map/while/body/eval_jaxpr/ppermute | solution.py:15
  702.5 13.7 %collective-permute-start.1 = (f32[2,512]{1,0:T(2,128)S(1)}, f32[2,512]{1,0:T(2,128)S(1)}, u32[]{:S(2)}, u32[]{:S(2)}) collective-permute-start(f32[2,512]{1,0:T(2,128)S(1)} %slice_reduce_fusion.6), channel_id=1, source_target_pairs={{1,0},{2,1},{3,2},{4,3},{5,4},{6,5},{7,6},{8,7},{9,8},{10,9},{11,1... | collective-permute-start | bytes 12296 | tf_op jit(solution)/shard_map/while/body/eval_jaxpr/ppermute | solution.py:15
  711.4 7.3 collective-permute-start.2
  731.7 7.1 collective-permute-start.3
  739.6 12.1 %collective-permute-start.4 = (f32[2,512]{1,0:T(2,128)S(1)}, f32[2,512]{1,0:T(2,128)S(1)}, u32[]{:S(2)}, u32[]{:S(2)}) collective-permute-start(f32[2,512]{1,0:T(2,128)S(1)} %slice_reduce_fusion.8), channel_id=1, source_target_pairs={{0,1},{1,2},{2,3},{3,4},{4,5},{5,6},{6,7},{7,8},{8,9},{9,10},{10,1... | collective-permute-start | bytes 12296 | tf_op jit(solution)/shard_map/while/body/eval_jaxpr/ppermute | solution.py:15
  745.4 7.1 collective-permute-start.5
  (3 other events, 8.2 us)
where the time goes:
time: 769 us; the launch traced here: 754 us
  other arithmetic  304 us (40%)
  starting transfers between devices  263 us (34%)
  local copies, waits for them, and re-layouts  111 us (14%)
  waiting for transfers between devices  73.4 us (10%)
    ppermute x60, starting transfers between devices, shifted(): return lax.ppermute(shard, axis, pairs)  255 us
    reduce_sum x10, other arithmetic, march_forward(): stress = jnp.sum(mode_next, axis=0)  118 us
    unnamed x1, other arithmetic  94.9 us
    unnamed x17, local copies, waits for them, and re-layouts  49.7 us
    exp x10, other arithmetic, relax_mode(): kept = jnp.exp(-rate_ratio)  41.8 us
    all_to_all x1, waiting for transfers between devices, shards(): lax.all_to_all(sheet_pieces, ('width', 'cores'), split_axis=3, concat_axi...  41.4 us
    ppermute x60, waiting for transfers between devices, shifted(): return lax.ppermute(shard, axis, pairs)  32 us
    all_to_all x2, local copies, waits for them, and re-layouts, shards(): lax.all_to_all(sheet_pieces, ('width', 'cores'), split_axis=3, concat_axi...  24.4 us
  transfers between devices with their start and end apart: 61, of which 31 were waited for; matrix products, arithmetic and copies ran while one was open for 10% of the time, Pallas kernels for 0%

commit v1 on v0

v1 whole, which is shorter than its diff:
```python
import jax
import jax.numpy as jnp
from jax import lax
from jax.experimental import pallas as pl
from jax.experimental.pallas import tpu as pltpu
from jax.sharding import PartitionSpec as P

LOG2E = 1.4426950408889634
OUTSIDE = -1.0 / 3.0
TICKS = 10
MODES = 12
PIECES = 16
ROWS = 512
COLS = 128
HALO = 16
EXT = ROWS + 2 * HALO
DEEP = 10
LANES = 640
SUBS = 24
BLK = 32
F32 = jnp.float32
VMEM = pltpu.VMEM
ANY = pl.ANY
SMEM = pltpu.SMEM
WIDE = ("width", "cores")


def shifted(shard, axis, by):
    peers = lax.axis_size(axis)
    pairs = [(i, i + by) for i in range(peers) if 0 <= i + by < peers]
    return lax.ppermute(shard, axis, pairs)


def params(mb):
    return pltpu.CompilerParams(vmem_limit_bytes=mb << 20)


def iota(shape, axis):
    return lax.broadcasted_iota(jnp.int32, shape, axis)


def pack_heat_body(src, dst, buf, side, in_sem, out_sem, side_sem):
    def fetch(p):
        return pltpu.make_async_copy(src.at[:, :, pl.ds(p * COLS, COLS)], buf.at[p], in_sem.at[p])

    def put(p):
        return pltpu.make_async_copy(buf.at[p], dst.at[p, pl.ds(0, TICKS)], out_sem.at[p])

    def put_side(p):
        return pltpu.make_async_copy(side.at[p], dst.at[p, TICKS], side_sem.at[p])

    for p in range(PIECES):
        fetch(p).start()
    lane = iota((32, COLS), 1)
    for p in range(PIECES):
        fetch(p).wait()
        put(p).start()
        if p == 0:
            side[0] = jnp.full((32, COLS), OUTSIDE, F32)
            put_side(0).start()
        if p + 1 < PIECES:
            acc = jnp.full((32, COLS), 1.0, F32)
            for n in range(TICKS):
                moved = pltpu.roll(buf[p, n], (DEEP * n + DEEP) % COLS, 1)
                acc = jnp.where((lane >= DEEP * n) & (lane < DEEP * n + DEEP), moved, acc)
            side[p + 1] = acc
            put_side(p + 1).start()
    for p in range(PIECES):
        put(p).wait()
        put_side(p).wait()


def pack_heat(slab):
    return pl.pallas_call(
        pack_heat_body,
        out_shape=jax.ShapeDtypeStruct((PIECES, TICKS + 1, 32, COLS), F32),
        in_specs=[pl.BlockSpec(memory_space=ANY)],
        out_specs=pl.BlockSpec(memory_space=ANY),
        scratch_shapes=[
            VMEM((PIECES, TICKS, 32, COLS), F32),
            VMEM((PIECES, 32, COLS), F32),
            pltpu.SemaphoreType.DMA((PIECES,)),
            pltpu.SemaphoreType.DMA((PIECES,)),
            pltpu.SemaphoreType.DMA((PIECES,)),
        ],
        compiler_params=params(16),
        name="pack_heat",
    )(slab)


def turned(own, up, down, fill):
    last = jnp.concatenate([down, jnp.full((COLS - 2 * HALO, COLS), fill, F32), up], axis=0)
    return jnp.concatenate([own[i * COLS:(i + 1) * COLS].T for i in range(4)] + [last.T], axis=1)


def pack_state_body(flags, s_ref, vf_v, vf_f, up, down, first, last):
    i = pl.program_id(0)

    def edges(blocks):
        return (jnp.concatenate([b[:DEEP] for b in blocks], axis=0),
                jnp.concatenate([b[COLS - DEEP:] for b in blocks], axis=0))

    blocks = [turned(s_ref[q], up[4 * i + q], down[4 * i + q], 0.0) for q in range(4)]
    a, b = edges(blocks)
    at = pl.multiple_of(i * 40, 8)
    first[pl.ds(at, 40), :] = a
    last[pl.ds(at, 40), :] = b

    @pl.when(i == 8)
    def _():
        f_up = jnp.where(flags[0] == 1, OUTSIDE, up[38])
        f_down = jnp.where(flags[1] == 1, OUTSIDE, down[38])
        rest = [turned(vf_v[0], up[36], down[36], 0.0), turned(vf_v[1], up[37], down[37], 0.0),
                turned(vf_f[...], f_up, f_down, 1.0)]
        a, b = edges(rest)
        pad = jnp.zeros((2, LANES), F32)
        first[360:392, :] = jnp.concatenate([a, pad], axis=0)
        last[360:392, :] = jnp.concatenate([b, pad], axis=0)


def pack_state(flags, state, motion, fictive, up, down):
    whole = lambda shape: pl.BlockSpec(shape, lambda i: (0,) * len(shape))
    return pl.pallas_call(
        pack_state_body,
        out_shape=[jax.ShapeDtypeStruct((392, LANES), F32)] * 2,
        grid=(9,),
        in_specs=[
            pl.BlockSpec(memory_space=SMEM),
            pl.BlockSpec((4, ROWS, COLS), lambda i: (i, 0, 0)),
            whole((2, ROWS, COLS)),
            whole((ROWS, COLS)),
            whole((39, HALO, COLS)),
            whole((39, HALO, COLS)),
        ],
        out_specs=[whole((392, LANES))] * 2,
        compiler_params=params(32),
        name="pack_state",
    )(flags, state, motion, fictive, up, down)


def shift_of(theta, fict):
    arg = 10.0 * (theta + fict) / (theta * fict) - 20.0
    inv = jnp.exp(-arg)
    return inv, jnp.exp(arg)


def strip_body(flags, coef, first, got, heat, heat_up, heat_down, sigma, nodes, z, v, q, heat_t):
    for k in range(36):
        z[k, 0:DEEP, :] = got[DEEP * k:DEEP * k + DEEP, :]
        z[k, DEEP:2 * DEEP, :] = first[DEEP * k:DEEP * k + DEEP, :]
        z[k, 2 * DEEP:SUBS, :] = jnp.zeros((SUBS - 2 * DEEP, LANES), F32)
    for k in range(2):
        at = 360 + DEEP * k
        v[k, 0:DEEP, :] = got[at:at + DEEP, :]
        v[k, DEEP:2 * DEEP, :] = first[at:at + DEEP, :]
        v[k, 2 * DEEP:SUBS, :] = jnp.zeros((SUBS - 2 * DEEP, LANES), F32)
    f_left = jnp.where(flags[2] == 1, OUTSIDE, got[380:390, :])
    ones = jnp.ones((SUBS - 2 * DEEP, LANES), F32)
    fict0 = jnp.concatenate([f_left, first[380:390, :], ones], axis=0)
    q[...] = jnp.zeros((3, SUBS, LANES), F32)

    top, bottom = flags[0] == 1, flags[1] == 1
    side = turned(heat[:, TICKS].reshape(ROWS, COLS), jnp.where(top, OUTSIDE, heat_up[TICKS]),
                  jnp.where(bottom, OUTSIDE, heat_down[TICKS]), 1.0)

    def gathered(pick, rows):
        lane = iota((rows, COLS), 1)
        acc = jnp.full((rows, COLS), 1.0, F32)
        for n in range(TICKS):
            moved = pltpu.roll(pick(n), DEEP * n, 1) if n else pick(n)
            acc = jnp.where((lane >= DEEP * n) & (lane < DEEP * n + DEEP), moved, acc)
        return acc

    own = jnp.concatenate([gathered(lambda n: heat[s, n], 32) for s in range(PIECES)], axis=0)
    mine = turned(own, gathered(lambda n: jnp.where(top, OUTSIDE, heat_up[n]), HALO),
                  gathered(lambda n: jnp.where(bottom, OUTSIDE, heat_down[n]), HALO), 1.0)
    for n in range(TICKS):
        heat_t[n, 0:DEEP, :] = side[DEEP * n:DEEP * n + DEEP]
        heat_t[n, DEEP:2 * DEEP, :] = mine[DEEP * n:DEEP * n + DEEP]
        heat_t[n, 2 * DEEP:SUBS, :] = ones

    lane = iota((SUBS, LANES), 1)
    inside = jnp.where(bottom & (lane >= ROWS) & (lane < LANES - HALO), 0.0, 1.0)
    sum_a = coef[24]

    def tick(n, fict):
        theta = heat_t[n]
        inv, shift = shift_of(theta, fict)
        fict_next = theta + (fict - theta) * jnp.exp(inv * (-1.0 / 3.0))

        def grads(m):
            beside = pltpu.roll(m, SUBS - 1, 0)
            both, diff = m + beside, beside - m
            along = 0.5 * (pltpu.roll(both, LANES - 1, 1) - both)
            across = 0.5 * (pltpu.roll(diff, LANES - 1, 1) + diff)
            return along, across

        u, w = v[0], v[1]
        nodes[pl.ds(n, 1), :] = u[DEEP:DEEP + 1]
        nodes[pl.ds(16 + n, 1), :] = w[DEEP:DEEP + 1]
        lu, wu = grads(u)
        lw, ww = grads(w)
        now = [shift * lu, shift * ww, shift * (0.5 * (wu + lw))]
        delta = [q[c] - now[c] for c in range(3)]
        for c in range(3):
            q[c] = now[c]
        total = [sum_a * now[c] for c in range(3)]
        for k in range(MODES):
            kept = jnp.exp2(inv * coef[k])
            a = coef[12 + k]
            for c in range(3):
                new = kept * (z[3 * k + c] + a * delta[c])
                z[3 * k + c] = new
                total[c] = total[c] + new
        for c in range(3):
            sigma[pl.ds(16 * c + n, 1), :] = total[c][DEEP - 1:DEEP]

        def force(lin, cross):
            x = lin + pltpu.roll(lin, 1, 0)
            y = cross - pltpu.roll(cross, 1, 0)
            return 0.5 * ((x + y) - pltpu.roll(x - y, 1, 1))

        v[0] = (u + force(total[0], total[2])) * inside
        v[1] = (w + force(total[2], total[1])) * inside
        return fict_next

    sigma[...] = jnp.zeros((48, LANES), F32)
    nodes[...] = jnp.zeros((32, LANES), F32)
    lax.fori_loop(0, TICKS, tick, fict0)


def strip(flags, coef, first, got, heat, heat_up, heat_down):
    full = pl.BlockSpec(memory_space=VMEM)
    smem = pl.BlockSpec(memory_space=SMEM)
    return pl.pallas_call(
        strip_body,
        out_shape=[jax.ShapeDtypeStruct((48, LANES), F32), jax.ShapeDtypeStruct((32, LANES), F32)],
        in_specs=[smem, smem] + [full] * 5,
        out_specs=[full, full],
        scratch_shapes=[
            VMEM((36, SUBS, LANES), F32),
            VMEM((2, SUBS, LANES), F32),
            VMEM((3, SUBS, LANES), F32),
            VMEM((TICKS, SUBS, LANES), F32),
        ],
        compiler_params=params(40),
        name="strip",
    )(flags, coef, first, got, heat, heat_up, heat_down)


def block_body(flags, coef, state, motion, fictive, up, down, heat, heat_up, heat_down, sigma, nodes,
               f_out, v_out, s_out, z, v, q, f, th, h, carry, z_sem, th_sem, out_sem):
    copies = []
    for k in range(36):
        copies.append(pltpu.make_async_copy(state.at[k], z.at[k, pl.ds(HALO, ROWS)], z_sem.at[k]))
    for s in range(PIECES):
        copies.append(pltpu.make_async_copy(heat.at[s, pl.ds(0, TICKS)], th.at[:, s + 1], th_sem.at[s]))
    for c in copies:
        c.start()
    top, bottom = flags[0] == 1, flags[1] == 1
    for k in range(36):
        z[k, 0:HALO, :] = up[k]
        z[k, HALO + ROWS:EXT, :] = down[k]
    for c in range(2):
        v[c, 0:HALO, :] = up[36 + c]
        v[c, HALO:HALO + ROWS, :] = motion[c]
        v[c, HALO + ROWS:EXT, :] = down[36 + c]
        v[c, EXT:EXT + 8, :] = jnp.zeros((8, COLS), F32)
    f[0:HALO, :] = jnp.where(top, OUTSIDE, up[38])
    f[HALO:HALO + ROWS, :] = fictive[...]
    f[HALO + ROWS:EXT, :] = jnp.where(bottom, OUTSIDE, down[38])
    for n in range(TICKS):
        th[n, 0, HALO:BLK, :] = jnp.where(top, OUTSIDE, heat_up[n])
        th[n, PIECES + 1, 0:HALO, :] = jnp.where(bottom, OUTSIDE, heat_down[n])
    q[...] = jnp.zeros((3, EXT, COLS), F32)
    pad = jnp.zeros((COLS - 80, COLS), F32)
    for i in range(5):
        part = jnp.concatenate([sigma[:, i * COLS:(i + 1) * COLS], nodes[:, i * COLS:(i + 1) * COLS], pad], axis=0).T
        if i < 4:
            h[HALO + i * COLS:HALO + (i + 1) * COLS, :] = part
        else:
            h[HALO + ROWS:EXT, :] = part[0:HALO]
            h[0:HALO, :] = part[COLS - HALO:]
            h[EXT:EXT + 8, :] = jnp.zeros((8, COLS), F32)
    for c in copies:
        c.wait()

    lane_v = iota((BLK + 8, COLS), 1)
    lane_s = iota((BLK, COLS), 1)
    row_8 = iota((8, COLS), 0)
    sum_a = coef[24]

    def tick(n, last):
        to_right = lax.rem(127 - 48 - n + COLS, COLS)
        carry[...] = jnp.zeros((2, 8, COLS), F32)

        def rows(b, _):
            r0 = pl.multiple_of(b * BLK, BLK)
            at = pl.ds(r0, BLK)
            j = 2 * b + 1
            theta = jnp.concatenate([th[n, b, HALO:BLK, :], th[n, b + 1, 0:HALO, :]], axis=0)
            fict = f[at, :]
            inv, shift = shift_of(theta, fict)
            f[at, :] = theta + (fict - theta) * jnp.exp(inv * (-1.0 / 3.0))
            hist = h[pl.ds(r0, BLK + 8), :]

            def grads(m, to):
                beside = jnp.where(lane_v == COLS - 1, pltpu.roll(hist, to, 1), pltpu.roll(m, COLS - 1, 1))
                both, diff = m + beside, beside - m
                along = 0.5 * (both[1:BLK + 1] - both[:BLK])
                across = 0.5 * (diff[1:BLK + 1] + diff[:BLK])
                return along, across

            u, w = v[0, pl.ds(r0, BLK + 8), :], v[1, pl.ds(r0, BLK + 8), :]
            lu, wu = grads(u, to_right)
            lw, ww = grads(w, lax.rem(to_right + COLS - 16, COLS))
            now = [shift * lu, shift * ww, shift * (0.5 * (wu + lw))]
            delta = [q[c, at, :] - now[c] for c in range(3)]
            for c in range(3):
                q[c, at, :] = now[c]
            total = [sum_a * now[c] for c in range(3)]
            for k in range(MODES):
                kept = jnp.exp2(inv * coef[k])
                a = coef[12 + k]
                for c in range(3):
                    new = kept * (z[3 * k + c, at, :] + a * delta[c])
                    z[3 * k + c, at, :] = (new + a * now[c]) if last else new
                    total[c] = total[c] + new
            hist_s = hist[:BLK]

            def left(c):
                to = lax.rem(COLS - 16 * c - n + COLS, COLS)
                return jnp.where(lane_s == 0, pltpu.roll(hist_s, to, 1), pltpu.roll(total[c], 1, 1))

            xx_l, yy_l, xy_l = left(0), left(1), left(2)

            def force(lin, lin_l, cross, cross_l, c):
                x, y = lin + lin_l, cross - cross_l
                rolled = pltpu.roll(x - y, 1, 0)
                head = jnp.where(row_8 == 0, carry[c], rolled[:8])
                carry[c] = rolled[:8]
                return 0.5 * ((x + y) - jnp.concatenate([head, rolled[8:]], axis=0))

            v[0, at, :] = u[:BLK] + force(total[0], xx_l, total[2], xy_l, 0)
            v[1, at, :] = w[:BLK] + force(total[2], xy_l, total[1], yy_l, 1)
            return 0

        lax.fori_loop(0, EXT // BLK, rows, 0)

        @pl.when(bottom)
        def _():
            v[:, HALO + ROWS:EXT, :] = jnp.zeros((2, HALO, COLS), F32)

    def step(n, _):
        tick(n, False)
        return 0

    lax.fori_loop(0, TICKS - 1, step, 0)
    tick(TICKS - 1, True)
    outs = [pltpu.make_async_copy(z.at[k, pl.ds(HALO, ROWS)], s_out.at[k], out_sem.at[k]) for k in range(36)]
    for c in outs:
        c.start()
    f_out[...] = f[HALO:HALO + ROWS, :]
    for c in range(2):
        v_out[c] = v[c, HALO:HALO + ROWS, :]
    for c in outs:
        c.wait()


def block(flags, coef, state, motion, fictive, up, down, heat, heat_up, heat_down, sigma, nodes):
    full = pl.BlockSpec(memory_space=VMEM)
    smem = pl.BlockSpec(memory_space=SMEM)
    hbm = pl.BlockSpec(memory_space=ANY)
    return pl.pallas_call(
        block_body,
        out_shape=[
            jax.ShapeDtypeStruct((ROWS, COLS), F32),
            jax.ShapeDtypeStruct((2, ROWS, COLS), F32),
            jax.ShapeDtypeStruct((36, ROWS, COLS), F32),
        ],
        in_specs=[smem, smem, hbm, full, full, full, full, hbm, full, full, full, full],
        out_specs=[full, full, hbm],
        scratch_shapes=[
            VMEM((36, EXT, COLS), F32),
            VMEM((2, EXT + 8, COLS), F32),
            VMEM((3, EXT, COLS), F32),
            VMEM((EXT, COLS), F32),
            VMEM((TICKS, PIECES + 2, BLK, COLS), F32),
            VMEM((EXT + 8, COLS), F32),
            VMEM((2, 8, COLS), F32),
            pltpu.SemaphoreType.DMA((36,)),
            pltpu.SemaphoreType.DMA((PIECES,)),
            pltpu.SemaphoreType.DMA((36,)),
        ],
        compiler_params=params(48),
        name="block",
    )(flags, coef, state, motion, fictive, up, down, heat, heat_up, heat_down, sigma, nodes)


def shards(warmth_history, fictitious_warmth, vertex_velocity, branch_load_tensors, mechanism_lifetimes, branch_stiffness):
    state = branch_load_tensors.reshape(3 * MODES, ROWS, COLS)
    weight = 2.0 * branch_stiffness * mechanism_lifetimes
    coef = jnp.concatenate([-LOG2E / mechanism_lifetimes, weight, jnp.sum(weight)[None]])
    draw, wide = lax.axis_index("draw"), lax.axis_index(WIDE)
    flags = jnp.stack([draw == 0, draw == lax.axis_size("draw") - 1, wide == 0]).astype(jnp.int32)

    heat = lax.all_to_all(pack_heat(warmth_history), WIDE, split_axis=0, concat_axis=0, tiled=True)

    def rows_of(at):
        cut = lambda x: lax.slice_in_dim(x, at, at + HALO, axis=1)
        return jnp.concatenate([cut(state), cut(vertex_velocity), cut(fictitious_warmth[None])], axis=0)

    up = shifted(rows_of(ROWS - HALO), "draw", 1)
    down = shifted(rows_of(0), "draw", -1)
    first, final = pack_state(flags, state, vertex_velocity, fictitious_warmth, up, down)
    got = shifted(final, WIDE, 1)

    heat_up = shifted(heat[PIECES - 1, :, HALO:, :], "draw", 1)
    heat_down = shifted(heat[0, :, :HALO, :], "draw", -1)
    sigma, nodes = strip(flags, coef, first, got, heat, heat_up, heat_down)
    nodes = shifted(nodes, WIDE, -1)
    fict, motion, modes = block(flags, coef, state, vertex_velocity, fictitious_warmth, up, down, heat, heat_up, heat_down, sigma, nodes)
    return fict, motion, modes.reshape(branch_load_tensors.shape)


def solution(mesh):
    in_specs = (
        P(None, ("draw", "width", "cores"), None),
        P("draw", ("width", "cores")),
        P(None, "draw", ("width", "cores")),
        P(None, None, "draw", ("width", "cores")),
        P(),
        P(),
    )
    out_specs = (
        P("draw", ("width", "cores")),
        P(None, "draw", ("width", "cores")),
        P(None, None, "draw", ("width", "cores")),
    )
    return jax.shard_map(shards, mesh=mesh, in_specs=in_specs, out_specs=out_specs, check_vma=False)
```

time: 769 us -> 164 us (0.21); the launches traced: 754 us -> 163 us
  other arithmetic: 304 us -> 2.9 us
  starting transfers between devices: 263 us -> 25.9 us
  local copies, waits for them, and re-layouts: 111 us -> 11.9 us
  Pallas kernels: 0 us -> 76.3 us
  waiting for transfers between devices: 73.4 us -> 45.4 us
    ppermute x60 -> x6, starting transfers between devices: 255 us -> 17.3 us  [shifted(): return lax.ppermute(shard, axis, pairs)]
    reduce_sum x10 -> x1, other arithmetic: 118 us -> 0.6 us  [shards(): jnp.sum(weight)[None]]
    unnamed x1 -> x0, other arithmetic: 94.9 us -> none
    pallas_call x0 -> x4, Pallas kernels: none -> 76.3 us  [the longest x1 55.7 us: block(): pl.pallas_call(block_body, out_shape=[jax.ShapeDtypeStruct((ROWS, COLS),...]
    exp x20 -> x0, other arithmetic: 61.6 us -> none  [the longest x10 41.8 us: relax_mode(): kept = jnp.exp(-rate_ratio)]
    unnamed x17 -> x20, local copies, waits for them, and re-layouts: 49.7 us -> 10.1 us
    all_to_all x2 -> x0, local copies, waits for them, and re-layouts: 24.4 us -> none  [shards(): lax.all_to_all(sheet_pieces, ('width', 'cores'), split_axis=3, concat_axi...]
    all_to_all x1, waiting for transfers between devices: 41.4 us -> 20.8 us  [shards(): lax.all_to_all(pack_heat(warmth_history), WIDE, split_axis=0, concat_axis...]
  transfers between devices with their start and end apart: 61 -> 7, of which waited for: 31 -> 5; matrix products, arithmetic and copies ran while one was open for 10% -> 3% of each run, Pallas kernels for 0% -> 4%
where the time goes in v1:
time: 164 us; the launch traced here: 163 us
  Pallas kernels  76.3 us (47%)
  waiting for transfers between devices  45.4 us (28%)
  starting transfers between devices  25.9 us (16%)
  local copies, waits for them, and re-layouts  11.9 us (7%)
  other arithmetic  2.9 us (2%)
    pallas_call x1, Pallas kernels, block(): pl.pallas_call(block_body, out_shape=[jax.ShapeDtypeStruct((ROWS, COLS),...  55.7 us
    ppermute x6, waiting for transfers between devices, shifted(): return lax.ppermute(shard, axis, pairs)  24.6 us
    all_to_all x1, waiting for transfers between devices, shards(): lax.all_to_all(pack_heat(warmth_history), WIDE, split_axis=0, concat_axis...  20.8 us
    ppermute x6, starting transfers between devices, shifted(): return lax.ppermute(shard, axis, pairs)  17.3 us
    unnamed x20, local copies, waits for them, and re-layouts  10.1 us
    all_to_all x1, starting transfers between devices, shards(): lax.all_to_all(pack_heat(warmth_history), WIDE, split_axis=0, concat_axis...  8.58 us
    pallas_call x1, Pallas kernels, strip(): pl.pallas_call(strip_body, out_shape=[jax.ShapeDtypeStruct((48, LANES), F...  8.4 us
    pallas_call x1, Pallas kernels, pack_state(): pl.pallas_call(pack_state_body, out_shape=[jax.ShapeDtypeStruct((392, LAN...  6.2 us
  transfers between devices with their start and end apart: 7, of which 5 were waited for; matrix products, arithmetic and copies ran while one was open for 3% of the time, Pallas kernels for 4%

profile of v1, /device:TPU:5, one launch (start us, length us, event | category | flops | bytes accessed | tf_op | source)
XLA Modules:
  0.0 163.2 jit_solution(12951332281977375030)
XLA Ops:
  0.6 0.0 copy-start.2
  0.6 1.7 %copy-done.2 = f32[10,32,2048]{2,1,0:T(8,128)S(1)} copy-done((f32[10,32,2048]{2,1,0:T(8,128)S(1)}, f32[10,32,2048]{2,1,0:T(8,128)}, u32[]{:S(2)}) %copy-start.2) | copy-done | bytes 2621464
  2.4 6.0 %pack_heat.1 = f32[16,11,32,128]{3,2,1,0:T(8,128)S(1)} custom-call(f32[10,32,2048]{2,1,0:T(8,128)S(1)} %copy-done.2), custom_call_target="tpu_custom_call" | custom-call | tf_op jit(solution)/shard_map/pack_heat/pallas_call | solution.py:74
  8.4 0.0 copy-start.1
  8.4 1.6 copy-done.1
  9.9 0.0 copy-start.3
  9.9 8.6 %all-to-all-start = ((f32[16,11,32,128]{3,2,1,0:T(8,128)}), f32[16,11,32,128]{3,2,1,0:T(8,128)S(1)}, u32[]{:S(2)}, u32[]{:S(2)}) async-start(f32[16,11,32,128]{3,2,1,0:T(8,128)} %copy-done.1), calls=%async_computation | async-start | bytes 5767168 | tf_op jit(solution)/shard_map/all_to_all | solution.py:407
  18.5 0.7 fusion.3
  19.2 0.0 copy-done.3
  19.2 1.1 fusion.1
  20.4 0.7 pad_maximum_fusion
  21.1 3.9 %collective-permute-start = (f32[39,16,128]{2,1,0:T(8,128)}, f32[39,16,128]{2,1,0:T(8,128)}, u32[]{:S(2)}, u32[]{:S(2)}) collective-permute-start(f32[39,16,128]{2,1,0:T(8,128)} %pad_maximum_fusion), channel_id=1, source_target_pairs={{0,16},{16,32},{32,48},{48,64},{64,80},{80,96},{96,112},{1,17},{17... | collective-permute-start | bytes 958472 | tf_op jit(solution)/shard_map/ppermute | solution.py:31
  25.0 0.8 pad_maximum_fusion.1
  25.8 1.3 collective-permute-start.1
  27.1 0.0 copy-start.8
  27.1 0.0 copy-start.9
  27.1 0.1 add_convert_fusion.flags
  27.2 4.0 %collective-permute-done.up = f32[39,16,128]{2,1,0:T(8,128)} collective-permute-done((f32[39,16,128]{2,1,0:T(8,128)}, f32[39,16,128]{2,1,0:T(8,128)}, u32[]{:S(2)}, u32[]{:S(2)}) %collective-permute-start) | collective-permute-done | bytes 319520 | tf_op jit(solution)/shard_map/ppermute | solution.py:31
  31.2 5.3 %collective-permute-done.1.down = f32[39,16,128]{2,1,0:T(8,128)} collective-permute-done((f32[39,16,128]{2,1,0:T(8,128)}, f32[39,16,128]{2,1,0:T(8,128)}, u32[]{:S(2)}, u32[]{:S(2)}) %collective-permute-start.1) | collective-permute-done | bytes 319520 | tf_op jit(solution)/shard_map/ppermute | solution.py:31
  36.4 0.0 copy-start
  36.4 3.7 %copy-done = f32[12,3,512,128]{3,2,1,0:T(8,128)S(1)} copy-done((f32[12,3,512,128]{3,2,1,0:T(8,128)S(1)}, f32[12,3,512,128]{3,2,1,0:T(8,128)}, u32[]{:S(2)}) %copy-start) | copy-done | bytes 9437208
  40.1 0.0 copy-start.4
  40.1 0.9 copy-done.4
  41.0 6.2 %pack_state.1 = (f32[392,640]{1,0:T(8,128)S(1)}, f32[392,640]{1,0:T(8,128)}) custom-call(s32[3]{0:T(128)S(1)} %add_convert_fusion.flags, f32[36,512,128]{2,1,0:T(8,128)S(1)} %bitcast.13, f32[2,512,128]{2,1,0:T(8,128)S(1)} %copy-done.3, f32[512,128]{1,0:T(8,128)S(1)} %copy-done.4, f32[39,16,128]{2,1,0:T(8,128)} %collective-permute-done.up, ...), custom_call_target="tpu_custom_call" | custom-call | tf_op jit(solution)/shard_map/pack_state/pallas_call | solution.py:123
  47.2 0.0 copy-start.6
  47.2 1.0 copy-done.6
  48.2 4.6 %collective-permute-start.4 = (f32[392,640]{1,0:T(8,128)}, f32[392,640]{1,0:T(8,128)}, u32[]{:S(2)}, u32[]{:S(2)}) collective-permute-start(f32[392,640]{1,0:T(8,128)} %get-tuple-element.11), channel_id=1, source_target_pairs={{0,1},{1,2},{2,3},{3,4},{4,5},{5,6},{6,7},{7,8},{8,9},{9,10},{10,1... | collective-permute-start | bytes 3010568 | tf_op jit(solution)/shard_map/ppermute | solution.py:31
  52.8 0.0 copy-done.8
  52.8 0.0 copy-done.9
  52.8 0.6 fusion
  53.4 20.8 %all-to-all-done.heat = f32[16,11,32,128]{3,2,1,0:T(8,128)S(1)} async-done(((f32[16,11,32,128]{3,2,1,0:T(8,128)}), f32[16,11,32,128]{3,2,1,0:T(8,128)S(1)}, u32[]{:S(2)}, u32[]{:S(2)}) %all-to-all-start) | async-done | bytes 2883616 | tf_op jit(solution)/shard_map/all_to_all | solution.py:407
  74.2 0.0 copy-start.5
  74.2 1.4 collective-permute-start.3
  75.6 4.0 %collective-permute-start.2 = (f32[11,16,128]{2,1,0:T(8,128)S(1)}, f32[11,16,128]{2,1,0:T(8,128)S(1)}, u32[]{:S(2)}, u32[]{:S(2)}) collective-permute-start(f32[11,16,128]{2,1,0:T(8,128)S(1)} %get-tuple-element.22), channel_id=1, source_target_pairs={{0,16},{16,32},{32,48},{48,64},{64,80},{80,96},{96,112},{1,17},{17... | collective-permute-start | bytes 270344 | tf_op jit(solution)/shard_map/ppermute | solution.py:31
  79.6 0.7 pad_maximum_fusion.2.coef
  80.4 10.8 %collective-permute-done.4.got = f32[392,640]{1,0:T(8,128)} collective-permute-done((f32[392,640]{1,0:T(8,128)}, f32[392,640]{1,0:T(8,128)}, u32[]{:S(2)}, u32[]{:S(2)}) %collective-permute-start.4) | collective-permute-done | bytes 1003552 | tf_op jit(solution)/shard_map/ppermute | solution.py:31
  91.2 0.0 collective-permute-done.3.heat_down
  91.2 0.0 collective-permute-done.2.heat_up
  91.2 0.0 copy-start.7
  91.2 1.2 copy-done.7
  92.4 8.4 %strip.1 = (f32[48,640]{1,0:T(8,128)S(1)}, f32[32,640]{1,0:T(8,128)S(1)}) custom-call(s32[3]{0:T(128)S(1)} %add_convert_fusion.flags, f32[25]{0:T(128)S(1)} %pad_maximum_fusion.2.coef, f32[392,640]{1,0:T(8,128)S(1)} %copy-done.7, f32[392,640]{1,0:T(8,128)} %collective-permute-done.4.got, f32[16,11,32,128]{3,2,1,0:T(8,128)S(1)} %all-to-all-done.heat, ...), custom_call_target="tpu_custom_call" | custom-call | tf_op jit(solution)/shard_map/strip/pallas_call | solution.py:235
  100.8 2.1 %collective-permute-start.5 = (f32[32,640]{1,0:T(8,128)S(1)}, f32[32,640]{1,0:T(8,128)S(1)}, u32[]{:S(2)}, u32[]{:S(2)}) collective-permute-start(f32[32,640]{1,0:T(8,128)S(1)} %get-tuple-element.13), channel_id=1, source_target_pairs={{1,0},{2,1},{3,2},{4,3},{5,4},{6,5},{7,6},{8,7},{9,8},{10,9},{11,1... | collective-permute-start | bytes 245768 | tf_op jit(solution)/shard_map/ppermute | solution.py:31
  102.9 4.6 %collective-permute-done.5.nodes = f32[32,640]{1,0:T(8,128)S(1)} collective-permute-done((f32[32,640]{1,0:T(8,128)S(1)}, f32[32,640]{1,0:T(8,128)S(1)}, u32[]{:S(2)}, u32[]{:S(2)}) %collective-permute-start.5) | collective-permute-done | bytes 81952 | tf_op jit(solution)/shard_map/ppermute | solution.py:31
  107.5 0.0 copy-done.5
  107.5 55.7 %block.1 = (f32[512,128]{1,0:T(8,128)}, f32[2,512,128]{2,1,0:T(8,128)}, f32[36,512,128]{2,1,0:T(8,128)}) custom-call(s32[3]{0:T(128)S(1)} %add_convert_fusion.flags, f32[25]{0:T(128)S(1)} %pad_maximum_fusion.2.coef, f32[36,512,128]{2,1,0:T(8,128)} %bitcast.12, f32[2,512,128]{2,1,0:T(8,128)S(1)} %copy-done.3, f32[512,128]{1,0:T(8,128)S(1)} %copy-done.5, ...), custom_call_target="tpu_custom_call" | custom-call | tf_op jit(solution)/shard_map/block/pallas_call | solution.py:374
  (2 shorter events, 0.0 us)
Async XLA Ops:
  0.6 1.7 %copy-start.2 = (f32[10,32,2048]{2,1,0:T(8,128)S(1)}, f32[10,32,2048]{2,1,0:T(8,128)}, u32[]{:S(2)}) copy-start(f32[10,32,2048]{2,1,0:T(8,128)} %src.1) | copy-start | bytes 7864324
  8.4 1.6 copy-start.1
  9.9 9.3 %copy-start.3 = (f32[2,512,128]{2,1,0:T(8,128)S(1)}, f32[2,512,128]{2,1,0:T(8,128)}, u32[]{:S(2)}) copy-start(f32[2,512,128]{2,1,0:T(8,128)} %motion.1) | copy-start | bytes 1572868
  9.9 64.2 %all-to-all-start = ((f32[16,11,32,128]{3,2,1,0:T(8,128)}), f32[16,11,32,128]{3,2,1,0:T(8,128)S(1)}, u32[]{:S(2)}, u32[]{:S(2)}) async-start(f32[16,11,32,128]{3,2,1,0:T(8,128)} %copy-done.1), calls=%async_computation | async-start | bytes 5767168 | tf_op jit(solution)/shard_map/all_to_all | solution.py:407
  21.1 10.1 %collective-permute-start = (f32[39,16,128]{2,1,0:T(8,128)}, f32[39,16,128]{2,1,0:T(8,128)}, u32[]{:S(2)}, u32[]{:S(2)}) collective-permute-start(f32[39,16,128]{2,1,0:T(8,128)} %pad_maximum_fusion), channel_id=1, source_target_pairs={{0,16},{16,32},{32,48},{48,64},{64,80},{80,96},{96,112},{1,17},{17... | collective-permute-start | bytes 958472 | tf_op jit(solution)/shard_map/ppermute | solution.py:31
  25.8 10.6 %collective-permute-start.1 = (f32[39,16,128]{2,1,0:T(8,128)}, f32[39,16,128]{2,1,0:T(8,128)}, u32[]{:S(2)}, u32[]{:S(2)}) collective-permute-start(f32[39,16,128]{2,1,0:T(8,128)} %pad_maximum_fusion.1), channel_id=1, source_target_pairs={{16,0},{32,16},{48,32},{64,48},{80,64},{96,80},{112,96},{17,1},{33... | collective-permute-start | bytes 958472 | tf_op jit(solution)/shard_map/ppermute | solution.py:31
  27.1 25.7 %copy-start.8 = (f32[12]{0:T(128)S(1)}, f32[12]{0:T(128)}, u32[]{:S(2)}) copy-start(f32[12]{0:T(128)} %param.10) | copy-start | bytes 148
  27.1 25.7 %copy-start.9 = (f32[12]{0:T(128)S(1)}, f32[12]{0:T(128)}, u32[]{:S(2)}) copy-start(f32[12]{0:T(128)} %param.11) | copy-start | bytes 148
  36.4 3.7 %copy-start = (f32[12,3,512,128]{3,2,1,0:T(8,128)S(1)}, f32[12,3,512,128]{3,2,1,0:T(8,128)}, u32[]{:S(2)}) copy-start(f32[12,3,512,128]{3,2,1,0:T(8,128)} %param.9) | copy-start | bytes 28311556
  40.1 0.9 copy-start.4
  47.2 1.0 copy-start.6
  48.2 43.0 %collective-permute-start.4 = (f32[392,640]{1,0:T(8,128)}, f32[392,640]{1,0:T(8,128)}, u32[]{:S(2)}, u32[]{:S(2)}) collective-permute-start(f32[392,640]{1,0:T(8,128)} %get-tuple-element.11), channel_id=1, source_target_pairs={{0,1},{1,2},{2,3},{3,4},{4,5},{5,6},{6,7},{7,8},{8,9},{9,10},{10,1... | collective-permute-start | bytes 3010568 | tf_op jit(solution)/shard_map/ppermute | solution.py:31
  74.2 33.3 %copy-start.5 = (f32[512,128]{1,0:T(8,128)S(1)}, f32[512,128]{1,0:T(8,128)}, u32[]{:S(2)}) copy-start(f32[512,128]{1,0:T(8,128)} %fictive.1) | copy-start | bytes 786436
  74.2 17.0 %collective-permute-start.3 = (f32[11,16,128]{2,1,0:T(8,128)S(1)}, f32[11,16,128]{2,1,0:T(8,128)S(1)}, u32[]{:S(2)}, u32[]{:S(2)}) collective-permute-start(f32[11,16,128]{2,1,0:T(8,128)S(1)} %get-tuple-element.21), channel_id=1, source_target_pairs={{16,0},{32,16},{48,32},{64,48},{80,64},{96,80},{112,96},{17,1},{33... | collective-permute-start | bytes 270344 | tf_op jit(solution)/shard_map/ppermute | solution.py:31
  75.6 15.6 %collective-permute-start.2 = (f32[11,16,128]{2,1,0:T(8,128)S(1)}, f32[11,16,128]{2,1,0:T(8,128)S(1)}, u32[]{:S(2)}, u32[]{:S(2)}) collective-permute-start(f32[11,16,128]{2,1,0:T(8,128)S(1)} %get-tuple-element.22), channel_id=1, source_target_pairs={{0,16},{16,32},{32,48},{48,64},{64,80},{80,96},{96,112},{1,17},{17... | collective-permute-start | bytes 270344 | tf_op jit(solution)/shard_map/ppermute | solution.py:31
  91.2 1.2 copy-start.7
  100.8 6.7 %collective-permute-start.5 = (f32[32,640]{1,0:T(8,128)S(1)}, f32[32,640]{1,0:T(8,128)S(1)}, u32[]{:S(2)}, u32[]{:S(2)}) collective-permute-start(f32[32,640]{1,0:T(8,128)S(1)} %get-tuple-element.13), channel_id=1, source_target_pairs={{1,0},{2,1},{3,2},{4,3},{5,4},{6,5},{7,6},{8,7},{9,8},{10,9},{11,1... | collective-permute-start | bytes 245768 | tf_op jit(solution)/shard_map/ppermute | solution.py:31

commit v2 on v0

v2 whole, which is shorter than its diff:
```python
import jax
import jax.numpy as jnp
from jax import lax
from jax.experimental import pallas as pl
from jax.experimental.pallas import tpu as pltpu
from jax.sharding import PartitionSpec as P

LOG2E = 1.4426950408889634
OUTSIDE = -1.0 / 3.0
TICKS = 10
MODES = 12
PIECES = 16
ROWS = 512
COLS = 128
HALO = 16
EXT = ROWS + 2 * HALO
DEEP = 10
LANES = 640
SUBS = 24
PAD = 8
SUB = 16
FLOW = 272
F32 = jnp.float32
VMEM = pltpu.VMEM
ANY = pl.ANY
SMEM = pltpu.SMEM
WIDE = ("width", "cores")


def shifted(shard, axis, by):
    peers = lax.axis_size(axis)
    pairs = [(i, i + by) for i in range(peers) if 0 <= i + by < peers]
    return lax.ppermute(shard, axis, pairs)


def params(mb):
    return pltpu.CompilerParams(vmem_limit_bytes=mb << 20)


def iota(shape, axis):
    return lax.broadcasted_iota(jnp.int32, shape, axis)


def pinned(x):
    return pltpu.with_memory_space_constraint(x, pltpu.HBM)


def cut_body(src, state, motion, fictive, dst, above, below, buf, side, halo, in_sem, out_sem, side_sem, row_sem):
    def fetch(p):
        return pltpu.make_async_copy(src.at[:, :, pl.ds(p * COLS, COLS)], buf.at[p], in_sem.at[p])

    def put(p):
        return pltpu.make_async_copy(buf.at[p], dst.at[p, pl.ds(0, TICKS)], out_sem.at[p])

    def put_side(p):
        return pltpu.make_async_copy(side.at[p], dst.at[p, TICKS], side_sem.at[p])

    ins, outs = [], []
    for i, (to, at) in enumerate(((above, ROWS - HALO), (below, 0))):
        part = pl.ds(at, HALO)
        for x, y in ((state.at[:, part], pl.ds(0, 36)), (motion.at[:, part], pl.ds(36, 2)), (fictive.at[part], 38)):
            ins.append(pltpu.make_async_copy(x, halo.at[i, y], row_sem.at[len(ins)]))
        outs.append(pltpu.make_async_copy(halo.at[i], to, row_sem.at[6 + i]))
    for p in range(PIECES):
        fetch(p).start()
    for c in ins:
        c.start()
    lane = iota((32, COLS), 1)
    for p in range(PIECES):
        fetch(p).wait()
        put(p).start()
        if p == 0:
            side[0] = jnp.full((32, COLS), OUTSIDE, F32)
            put_side(0).start()
        if p + 1 < PIECES:
            acc = jnp.full((32, COLS), 1.0, F32)
            for n in range(TICKS):
                moved = pltpu.roll(buf[p, n], (DEEP * n + DEEP) % COLS, 1)
                acc = jnp.where((lane >= DEEP * n) & (lane < DEEP * n + DEEP), moved, acc)
            side[p + 1] = acc
            put_side(p + 1).start()
    for c in ins:
        c.wait()
    for c in outs:
        c.start()
    for p in range(PIECES):
        put(p).wait()
        put_side(p).wait()
    for c in outs:
        c.wait()


def cut(slab, state, motion, fictive):
    hbm = pl.BlockSpec(memory_space=pltpu.HBM)
    halo = pltpu.HBM((39, HALO, COLS), F32)
    return pl.pallas_call(
        cut_body,
        out_shape=[pltpu.HBM((PIECES, TICKS + 1, 32, COLS), F32), halo, halo],
        in_specs=[hbm] * 4,
        out_specs=[hbm] * 3,
        scratch_shapes=[
            VMEM((PIECES, TICKS, 32, COLS), F32),
            VMEM((PIECES, 32, COLS), F32),
            VMEM((2, 39, HALO, COLS), F32),
            pltpu.SemaphoreType.DMA((PIECES,)),
            pltpu.SemaphoreType.DMA((PIECES,)),
            pltpu.SemaphoreType.DMA((PIECES,)),
            pltpu.SemaphoreType.DMA((8,)),
        ],
        compiler_params=params(8),
        name="cut",
    )(pinned(slab), pinned(state), pinned(motion), pinned(fictive))


def corner(up, down, fill):
    return jnp.concatenate([down, jnp.full((COLS - 2 * HALO, COLS), fill, F32), up], axis=0).T


def turned(own):
    return jnp.concatenate([own[i * COLS:(i + 1) * COLS].T for i in range(4)], axis=1)


def pack_own_body(state, motion, fictive, first, last, buf, sem):
    copies = [pltpu.make_async_copy(state.at[pl.ds(4 * i, 4)], buf.at[pl.ds(4 * i, 4)], sem.at[i]) for i in range(9)]
    for c in copies:
        c.start()
    rest = [turned(motion[0]), turned(motion[1]), turned(fictive[...])]
    put_rest(rest, first, last)
    for i in range(9):
        copies[i].wait()
        put_state(i, [turned(buf[4 * i + q]) for q in range(4)], first, last)


def put_rest(rest, first, last):
    first[360:400, :] = jnp.concatenate([rest[0][:16], rest[1][:16], rest[2][:8]], axis=0)
    first[400:408, :] = rest[2][8:16]
    last[360:392, :] = jnp.concatenate([r[COLS - DEEP:] for r in rest] + [rest[0][:2]], axis=0)


def put_state(i, blocks, first, last):
    first[40 * i:40 * i + 40, :] = jnp.concatenate([b[:DEEP] for b in blocks], axis=0)
    last[40 * i:40 * i + 40, :] = jnp.concatenate([b[COLS - DEEP:] for b in blocks], axis=0)


def pack_own(state, motion, fictive):
    full = pl.BlockSpec(memory_space=VMEM)
    return pl.pallas_call(
        pack_own_body,
        out_shape=[jax.ShapeDtypeStruct((408, ROWS), F32), jax.ShapeDtypeStruct((392, ROWS), F32)],
        in_specs=[pl.BlockSpec(memory_space=pltpu.HBM), full, full],
        out_specs=[full] * 2,
        scratch_shapes=[VMEM((36, ROWS, COLS), F32), pltpu.SemaphoreType.DMA((9,))],
        compiler_params=params(20),
        name="pack_own",
    )(pinned(state), motion, fictive)


def pack_halo_body(flags, up, down, first, dense, last):
    f_up = jnp.where(flags[0] == 1, OUTSIDE, up[38])
    f_down = jnp.where(flags[1] == 1, OUTSIDE, down[38])
    put_rest([corner(up[36], down[36], 0.0), corner(up[37], down[37], 0.0), corner(f_up, f_down, 1.0)], first, last)
    for i in range(9):
        put_state(i, [corner(up[4 * i + q], down[4 * i + q], 0.0) for q in range(4)], first, last)
    last[392:416, :] = jnp.zeros((24, COLS), F32)
    lane = iota((104, COLS), 1)
    acc = jnp.zeros((104, COLS), F32)
    for g in range(4):
        moved = pltpu.roll(last[104 * g:104 * g + 104, :], (HALO + 32 * g) % COLS, 1)
        acc = jnp.where((lane >= 32 * g) & (lane < 32 * g + 32), moved, acc)
    dense[...] = acc


def spread(dense):
    return jnp.concatenate([pltpu.roll(dense, COLS - HALO - 32 * g, 1) for g in range(4)], axis=0)


def pack_halo(flags, up, down):
    full = pl.BlockSpec(memory_space=VMEM)
    return pl.pallas_call(
        pack_halo_body,
        out_shape=[jax.ShapeDtypeStruct((408, COLS), F32), jax.ShapeDtypeStruct((104, COLS), F32)],
        in_specs=[pl.BlockSpec(memory_space=SMEM), full, full],
        out_specs=[full] * 2,
        scratch_shapes=[VMEM((416, COLS), F32)],
        compiler_params=params(8),
        name="pack_halo",
    )(flags, up, down)


def shift_of(theta, fict):
    arg = 10.0 * (theta + fict) / (theta * fict) - 20.0
    inv = jnp.exp(-arg)
    return inv, jnp.exp(arg)


def work(us):
    return pl.CostEstimate(flops=0, transcendentals=0, bytes_accessed=us * 3_000_000)


def beside_each_other(pick, rows):
    lane = iota((rows, COLS), 1)
    acc = jnp.full((rows, COLS), 1.0, F32)
    for n in range(TICKS):
        moved = pltpu.roll(pick(n), DEEP * n, 1) if n else pick(n)
        acc = jnp.where((lane >= DEEP * n) & (lane < DEEP * n + DEEP), moved, acc)
    return acc


def advance(theta, fict):
    inv, shift = shift_of(theta, fict)
    return inv, 0.5 * shift, theta + (fict - theta) * jnp.exp(inv * (-1.0 / 3.0))


def ready_body(heat, fictive, inv_ref, half_ref, f_out, mine, side):
    def piece(s, _):
        at = pl.ds(pl.multiple_of(32 * s, 32), 32)
        to = pl.ds(pl.multiple_of(32 * s + HALO, 16), 32)
        fict = fictive[at, :]
        for n in range(TICKS):
            inv_ref[n, to, :], half_ref[n, to, :], fict = advance(heat[s, n], fict)
        f_out[at, :] = fict
        return 0

    lax.fori_loop(0, PIECES, piece, 0)
    own = jnp.concatenate([beside_each_other(lambda n: heat[s, n], 32) for s in range(PIECES)], axis=0)
    mine[...] = turned(own)
    side[...] = turned(jnp.concatenate([heat[s, TICKS] for s in range(PIECES)], axis=0))


def ready(heat, fictive):
    full = pl.BlockSpec(memory_space=VMEM)
    factor = jax.ShapeDtypeStruct((TICKS, EXT + PAD, COLS), F32)
    row_t = jax.ShapeDtypeStruct((COLS, ROWS), F32)
    return pl.pallas_call(
        ready_body,
        out_shape=[factor, factor, jax.ShapeDtypeStruct((ROWS, COLS), F32), row_t, row_t],
        in_specs=[full] * 2,
        out_specs=[full] * 5,
        compiler_params=params(16),
        cost_estimate=work(6),
        name="ready",
    )(heat, fictive)


def lay_body(flags, first, first_halo, got, got_dense, z, v, fict, got_halo):
    rest = SUBS - 2 * DEEP
    lane = iota((416, COLS), 1)
    blank = jnp.where((iota((416, COLS), 0) >= 380) & (iota((416, COLS), 0) < 390), 1.0, 0.0)
    got_halo[...] = jnp.where((lane < HALO) | (lane >= COLS - HALO), spread(got_dense[...]), blank)
    for lanes, own, left in ((slice(0, ROWS), first, got), (slice(ROWS, LANES), first_halo, got_halo)):
        width = lanes.stop - lanes.start
        for k in range(36):
            z[k, 0:DEEP, lanes] = left[DEEP * k:DEEP * k + DEEP, :]
            z[k, DEEP:2 * DEEP, lanes] = own[DEEP * k:DEEP * k + DEEP, :]
            z[k, 2 * DEEP:SUBS, lanes] = jnp.zeros((rest, width), F32)
        for k in range(2):
            v[k, 0:DEEP, lanes] = left[360 + DEEP * k:370 + DEEP * k, :]
            v[k, DEEP:SUBS, lanes] = own[360 + 16 * k:360 + 16 * k + SUBS - DEEP, :]
        fict[0:DEEP, lanes] = jnp.where(flags[2] == 1, OUTSIDE, left[380:390, :])
        fict[DEEP:2 * DEEP, lanes] = own[392:402, :]
        fict[2 * DEEP:SUBS, lanes] = jnp.ones((rest, width), F32)


def lay(flags, first, first_halo, got, got_halo):
    full = pl.BlockSpec(memory_space=VMEM)
    shapes = [(36, SUBS, LANES), (2, SUBS, LANES), (SUBS, LANES)]
    return pl.pallas_call(
        lay_body,
        out_shape=[jax.ShapeDtypeStruct(s, F32) for s in shapes],
        in_specs=[pl.BlockSpec(memory_space=SMEM)] + [full] * 4,
        out_specs=[full] * 3,
        scratch_shapes=[VMEM((416, COLS), F32)],
        compiler_params=params(8),
        cost_estimate=work(2),
        name="lay",
    )(flags, first, first_halo, got, got_halo)


def strip_body(flags, coef, z_in, v_in, fict_in, mine, side, heat_up, heat_down, nodes, z, v, q, heat_t):
    rest = SUBS - 2 * DEEP
    v[...] = v_in[...]
    q[...] = jnp.zeros((3, SUBS, LANES), F32)

    top, bottom = flags[0] == 1, flags[1] == 1
    last_side = corner(jnp.where(top, OUTSIDE, heat_up[TICKS]), jnp.where(bottom, OUTSIDE, heat_down[TICKS]), 1.0)
    last_mine = corner(beside_each_other(lambda n: jnp.where(top, OUTSIDE, heat_up[n]), HALO),
                       beside_each_other(lambda n: jnp.where(bottom, OUTSIDE, heat_down[n]), HALO), 1.0)
    for n in range(TICKS):
        cols = slice(DEEP * n, DEEP * n + DEEP)
        heat_t[n, 0:DEEP, 0:ROWS] = side[cols, :]
        heat_t[n, 0:DEEP, ROWS:LANES] = last_side[cols]
        heat_t[n, DEEP:2 * DEEP, 0:ROWS] = mine[cols, :]
        heat_t[n, DEEP:2 * DEEP, ROWS:LANES] = last_mine[cols]
        heat_t[n, 2 * DEEP:SUBS, :] = jnp.ones((rest, LANES), F32)

    lane = iota((SUBS, LANES), 1)
    inside = jnp.where(bottom & (lane >= ROWS) & (lane < LANES - HALO), 0.0, 1.0)
    sum_a = coef[24]
    nodes[...] = jnp.zeros((32, LANES), F32)
    nodes[31:32, :] = v[0, DEEP:DEEP + 1, :]
    nodes[0:1, :] = v[1, DEEP:DEEP + 1, :]

    def tick(n, fict):
        inv, half, fict_next = advance(heat_t[n], fict)

        def grads(m):
            beside = pltpu.roll(m, SUBS - 1, 0)
            both, diff = m + beside, beside - m
            return pltpu.roll(both, LANES - 1, 1) - both, pltpu.roll(diff, LANES - 1, 1) + diff

        u, w = v[0], v[1]
        lu, wu = grads(u)
        lw, ww = grads(w)
        now = [half * lu, half * ww, (0.5 * half) * (wu + lw)]
        delta = [q[c] - now[c] for c in range(3)]
        for c in range(3):
            q[c] = now[c]
        total = [sum_a * now[c] for c in range(3)]
        for k in range(MODES):
            kept = jnp.exp2(inv * coef[k])
            a = coef[12 + k]
            for c in range(3):
                new = kept * (z[3 * k + c] + a * delta[c])
                z[3 * k + c] = new
                total[c] = total[c] + new

        def force(lin, cross):
            a, b = lin + cross, lin - cross
            return 0.5 * ((a - pltpu.roll(b, 1, 1)) + pltpu.roll(b - pltpu.roll(a, 1, 1), 1, 0))

        u_next = (u + force(total[0], total[2])) * inside
        w_next = (w + force(total[2], total[1])) * inside
        v[0], v[1] = u_next, w_next
        nodes[pl.ds(2 * n + 1, 1), :] = u_next[DEEP:DEEP + 1]
        nodes[pl.ds(2 * n + 2, 1), :] = w_next[DEEP:DEEP + 1]
        return fict_next

    lax.fori_loop(0, TICKS, tick, fict_in[...])


def strip(flags, coef, z, v, fict, mine, side, heat_up, heat_down):
    full = pl.BlockSpec(memory_space=VMEM)
    smem = pl.BlockSpec(memory_space=SMEM)
    return pl.pallas_call(
        strip_body,
        out_shape=[jax.ShapeDtypeStruct((32, LANES), F32), jax.ShapeDtypeStruct((36, SUBS, LANES), F32)],
        in_specs=[smem, smem] + [full] * 7,
        out_specs=[full, full],
        input_output_aliases={2: 1},
        scratch_shapes=[
            VMEM((2, SUBS, LANES), F32),
            VMEM((3, SUBS, LANES), F32),
            VMEM((TICKS, SUBS, LANES), F32),
        ],
        compiler_params=params(16),
        cost_estimate=work(7),
        name="strip",
    )(flags, coef, z, v, fict, mine, side, heat_up, heat_down)[0]


def upright(nodes, i):
    part = nodes[:, i * COLS:(i + 1) * COLS]
    return jnp.concatenate([part[:24], jnp.zeros((COLS - 32, COLS), F32), part[24:]], axis=0).T


def edges_body(flags, inv_in, half_in, up, down, heat_up, heat_down, nodes, inv_ref, half_ref, left):
    top, bottom = flags[0] == 1, flags[1] == 1
    fict = jnp.concatenate([jnp.where(top, OUTSIDE, up[38]), jnp.where(bottom, OUTSIDE, down[38])], axis=0)
    for n in range(TICKS):
        theta = jnp.concatenate([jnp.where(top, OUTSIDE, heat_up[n]), jnp.where(bottom, OUTSIDE, heat_down[n])], axis=0)
        inv, half, fict = advance(theta, fict)
        inv_ref[n, 0:HALO, :] = inv[:HALO]
        half_ref[n, 0:HALO, :] = half[:HALO]
        inv_ref[n, HALO + ROWS:EXT, :] = inv[HALO:]
        half_ref[n, HALO + ROWS:EXT, :] = half[HALO:]
        inv_ref[n, EXT:EXT + PAD, :] = jnp.ones((PAD, COLS), F32)
        half_ref[n, EXT:EXT + PAD, :] = jnp.ones((PAD, COLS), F32)
    for i in range(5):
        part = upright(nodes, i)
        for n in range(TICKS):
            for c in range(2):
                moved = pltpu.roll(part, COLS - (2 * n + 1 + c), 1)
                if i < 4:
                    left[n, c, HALO + i * COLS:HALO + (i + 1) * COLS, :] = moved
                else:
                    left[n, c, HALO + ROWS:EXT, :] = moved[:HALO]
                    left[n, c, 0:HALO, :] = moved[COLS - HALO:]


def edges(flags, inv, half, up, down, heat_up, heat_down, nodes):
    full = pl.BlockSpec(memory_space=VMEM)
    factor = jax.ShapeDtypeStruct((TICKS, EXT + PAD, COLS), F32)
    return pl.pallas_call(
        edges_body,
        out_shape=[factor, factor, jax.ShapeDtypeStruct((TICKS, 2, EXT, COLS), F32)],
        in_specs=[pl.BlockSpec(memory_space=SMEM)] + [full] * 7,
        out_specs=[full] * 3,
        input_output_aliases={1: 0, 2: 1},
        compiler_params=params(18),
        cost_estimate=work(3),
        name="edges",
    )(flags, inv, half, up, down, heat_up, heat_down, nodes)


def block_body(flags, coef, state, motion, up, down, inv_ref, half_ref, left, beside_t, v_out, s_out, z, v, q, h, pairs, forces, zh, sem, in_sem):
    bottom = flags[1] == 1

    def in_copy(b):
        at = pl.ds(32 * b if isinstance(b, int) else pl.multiple_of(32 * b, 32), 32)
        return pltpu.make_async_copy(state.at[:, at], z.at[:, at], in_sem.at[b])

    for b in range(ROWS // 32):
        in_copy(b).start()

    for k in range(36):
        zh[k, 0:HALO, :] = up[k]
        zh[k, HALO:, :] = down[k]
    for c in range(2):
        v[c, 0:HALO, :] = up[36 + c]
        v[c, HALO:HALO + ROWS, :] = motion[c]
        v[c, HALO + ROWS:EXT, :] = down[36 + c]
        v[c, EXT:, :] = jnp.zeros((32, COLS), F32)
    q[...] = jnp.zeros((3, EXT + PAD, COLS), F32)
    forces[:, 0:8, :] = jnp.zeros((4, 8, COLS), F32)
    for i in range(5):
        part = upright(beside_t, i)
        if i < 4:
            h[HALO + i * COLS:HALO + (i + 1) * COLS, :] = part
        else:
            h[HALO + ROWS:EXT, :] = part[0:HALO]
            h[0:HALO, :] = part[COLS - HALO:]
            h[EXT:, :] = jnp.zeros((32, COLS), F32)

    lane = iota((FLOW, COLS), 1)
    at_right, at_left = lane == COLS - 1, lane == 0
    sum_a = coef[24]

    def out_copy(b):
        at = pl.ds(pl.multiple_of(32 * (b - 1), 32), 32)
        return pltpu.make_async_copy(z.at[:, at], s_out.at[:, at], sem.at[b - 1])

    def flow(n, forced, paired):
        for r in range(0, EXT, FLOW):
            at, here, above = pl.ds(r, FLOW), pl.ds(r + 8, FLOW), pl.ds(r + 7, FLOW)
            m = [v[c, at, :] for c in range(2)]
            if forced:
                for c in range(2):
                    lin, cross = 2 * c, 2 * c + 1
                    straight = forces[lin, here, :] - forces[cross, above, :]
                    turned_in = pltpu.roll(forces[cross, here, :] - forces[lin, above, :], 1, 1)
                    m[c] = jnp.where(at_left, left[n, c, at, :], m[c] + 0.5 * (straight + turned_in))
                    if r + FLOW == EXT:
                        m[c] = jnp.concatenate([m[c][:FLOW - HALO], jnp.where(bottom, 0.0, m[c][FLOW - HALO:])], axis=0)
                    v[c, at, :] = m[c]
            if paired:
                hist = h[at, :]
                h[at, :] = pltpu.roll(hist, COLS - 2, 1)
                beside = (jnp.where(at_right, hist, pltpu.roll(m[0], COLS - 1, 1)),
                          pltpu.roll(jnp.where(at_left, hist, m[1]), COLS - 1, 1))
                for c in range(2):
                    pairs[2 * c, at, :] = m[c] + beside[c]
                    pairs[2 * c + 1, at, :] = beside[c] - m[c]

    def relax(n, r, zs, r_z, size, final):
        at, below, at_z = pl.ds(r, size), pl.ds(r + 1, size), pl.ds(r_z, size)
        along = [pairs[2 * c, below, :] - pairs[2 * c, at, :] for c in range(2)]
        across = [pairs[2 * c + 1, below, :] + pairs[2 * c + 1, at, :] for c in range(2)]
        half, inv = half_ref[n, at, :], inv_ref[n, at, :]
        now = [half * along[0], half * across[1], (0.5 * half) * (across[0] + along[1])]
        delta = [q[c, at, :] - now[c] for c in range(3)]
        for c in range(3):
            q[c, at, :] = now[c]
        total = [sum_a * x for x in now]
        for k in range(MODES):
            kept = jnp.exp2(inv * coef[k])
            a = coef[12 + k]
            for c in range(3):
                new = kept * (zs[3 * k + c, at_z, :] + a * delta[c])
                zs[3 * k + c, at_z, :] = (new + a * now[c]) if final else new
                total[c] = total[c] + new
        xx, yy, xy = total
        for i, part in enumerate((xx + xy, xx - xy, xy + yy, xy - yy)):
            forces[i, pl.ds(r + 8, size), :] = part

    def relax_group(n, b, final):
        fixed = isinstance(b, int)
        size = HALO if fixed else SUB
        for t in range(0, 32, size):
            r = 32 * b + t
            if not fixed:
                r = pl.multiple_of(r, 8)
            if fixed and b == 0 and t < HALO:
                relax(n, r, zh, t, size, final)
            elif fixed and b > 0 and t >= HALO:
                relax(n, r, zh, t, size, final)
            else:
                relax(n, r, z, r - HALO, size, final)

    def tick(n, starting, final):
        if starting:
            in_copy(0).wait()
        relax_group(n, 0, final)

        def body(b, _):
            if starting:
                in_copy(b).wait()
            relax_group(n, b, final)
            if final:
                out_copy(b).start()
            return 0

        last = EXT // 32 - 1
        lax.fori_loop(1, last, body, 0)
        relax_group(n, last, final)
        if final:
            out_copy(last).start()
        flow(n, True, not final)

    def step(n, _):
        tick(n, False, False)
        return 0

    flow(0, False, True)
    tick(0, True, False)
    lax.fori_loop(1, TICKS - 1, step, 0)
    tick(TICKS - 1, False, True)
    for c in range(2):
        v_out[c] = v[c, HALO:HALO + ROWS, :]
    for b in range(1, EXT // 32):
        out_copy(b).wait()


def block(flags, coef, state, motion, up, down, inv, half, left, beside):
    full = pl.BlockSpec(memory_space=VMEM)
    smem = pl.BlockSpec(memory_space=SMEM)
    return pl.pallas_call(
        block_body,
        out_shape=[
            jax.ShapeDtypeStruct((2, ROWS, COLS), F32),
            pltpu.HBM((36, ROWS, COLS), F32),
        ],
        in_specs=[smem, smem, pl.BlockSpec(memory_space=pltpu.HBM)] + [full] * 7,
        out_specs=[full, pl.BlockSpec(memory_space=pltpu.HBM)],
        scratch_shapes=[
            VMEM((36, ROWS, COLS), F32),
            VMEM((2, EXT + 32, COLS), F32),
            VMEM((3, EXT + PAD, COLS), F32),
            VMEM((EXT + 32, COLS), F32),
            VMEM((4, EXT + 32, COLS), F32),
            VMEM((4, EXT + 8, COLS), F32),
            VMEM((36, 2 * HALO, COLS), F32),
            pltpu.SemaphoreType.DMA((EXT // 32 - 1,)),
            pltpu.SemaphoreType.DMA((ROWS // 32,)),
        ],
        compiler_params=params(26),
        cost_estimate=work(28),
        name="block",
    )(flags, coef, pinned(state), motion, up, down, inv, half, left, beside)


def shards(warmth_history, fictitious_warmth, vertex_velocity, branch_load_tensors, mechanism_lifetimes, branch_stiffness):
    state = branch_load_tensors.reshape(3 * MODES, ROWS, COLS)
    weight = 2.0 * branch_stiffness * mechanism_lifetimes
    coef = jnp.concatenate([-LOG2E / mechanism_lifetimes, weight, jnp.sum(weight)[None]])
    draw, wide = lax.axis_index("draw"), lax.axis_index(WIDE)
    flags = jnp.stack([draw == 0, draw == lax.axis_size("draw") - 1, wide == 0]).astype(jnp.int32)

    slab, above, below = cut(warmth_history, state, vertex_velocity, fictitious_warmth)
    heat = lax.all_to_all(slab, WIDE, split_axis=0, concat_axis=0, tiled=True)
    up = shifted(above, "draw", 1)
    down = shifted(below, "draw", -1)
    first, final = pack_own(state, vertex_velocity, fictitious_warmth)
    got = shifted(final, WIDE, 1)
    first_halo, final_halo = pack_halo(flags, up, down)
    got_halo = shifted(final_halo, WIDE, 1)
    heat_up = shifted(heat[PIECES - 1, :, HALO:, :], "draw", 1)
    heat_down = shifted(heat[0, :, :HALO, :], "draw", -1)
    inv, half, fict, mine, side = ready(heat, fictitious_warmth)
    got, got_halo, mine = lax.optimization_barrier((got, got_halo, mine))
    strip_state = lay(flags, first, first_halo, got, got_halo)
    nodes = strip(flags, coef, *strip_state, mine, side, heat_up, heat_down)
    beside = shifted(nodes, WIDE, -1)
    inv, half, left = edges(flags, inv, half, up, down, heat_up, heat_down, nodes)
    motion, modes = block(flags, coef, state, vertex_velocity, up, down, inv, half, left, beside)
    return fict, motion, modes.reshape(branch_load_tensors.shape)


def solution(mesh):
    in_specs = (
        P(None, ("draw", "width", "cores"), None),
        P("draw", ("width", "cores")),
        P(None, "draw", ("width", "cores")),
        P(None, None, "draw", ("width", "cores")),
        P(),
        P(),
    )
    out_specs = (
        P("draw", ("width", "cores")),
        P(None, "draw", ("width", "cores")),
        P(None, None, "draw", ("width", "cores")),
    )
    return jax.shard_map(shards, mesh=mesh, in_specs=in_specs, out_specs=out_specs, check_vma=False)
```

time: 769 us -> 128 us (0.17); the launches traced: 754 us -> 128 us
  other arithmetic: 304 us -> 1.4 us
  starting transfers between devices: 263 us -> 29.9 us
  local copies, waits for them, and re-layouts: 111 us -> 3.51 us
  Pallas kernels: 0 us -> 57.3 us
  waiting for transfers between devices: 73.4 us -> 34.9 us
    ppermute x60 -> x7, starting transfers between devices: 255 us -> 21.3 us  [shifted(): return lax.ppermute(shard, axis, pairs)]
    reduce_sum x10 -> x1, other arithmetic: 118 us -> 0.6 us  [shards(): jnp.sum(weight)[None]]
    unnamed x1 -> x0, other arithmetic: 94.9 us -> none
    exp x20 -> x0, other arithmetic: 61.6 us -> none  [the longest x10 41.8 us: relax_mode(): kept = jnp.exp(-rate_ratio)]
    pallas_call x0 -> x8, Pallas kernels: none -> 57.3 us  [the longest x1 29.6 us: block(): pl.pallas_call(block_body, out_shape=[jax.ShapeDtypeStruct((2, ROWS, COLS...]
    unnamed x17 -> x18, local copies, waits for them, and re-layouts: 49.7 us -> 3.5 us
    all_to_all x2 -> x0, local copies, waits for them, and re-layouts: 24.4 us -> none  [shards(): lax.all_to_all(sheet_pieces, ('width', 'cores'), split_axis=3, concat_axi...]
    ppermute x60 -> x7, waiting for transfers between devices: 32 us -> 10.4 us  [shifted(): return lax.ppermute(shard, axis, pairs)]
  transfers between devices with their start and end apart: 61 -> 8, of which waited for: 31 -> 4; matrix products, arithmetic and copies ran while one was open for 10% -> 1% of each run, Pallas kernels for 0% -> 13%
where the time goes in v2:
time: 128 us
  Pallas kernels  57.3 us (45%)
  waiting for transfers between devices  34.9 us (27%)
  starting transfers between devices  29.9 us (23%)
  local copies, waits for them, and re-layouts  3.51 us (3%)
  other arithmetic  1.4 us (1%)
    pallas_call x1, Pallas kernels, block(): pl.pallas_call(block_body, out_shape=[jax.ShapeDtypeStruct((2, ROWS, COLS...  29.6 us
    all_to_all x1, waiting for transfers between devices, shards(): heat = lax.all_to_all(slab, WIDE, split_axis=0, concat_axis=0, tiled=True)  24.5 us
    ppermute x7, starting transfers between devices, shifted(): return lax.ppermute(shard, axis, pairs)  21.3 us
    ppermute x7, waiting for transfers between devices, shifted(): return lax.ppermute(shard, axis, pairs)  10.4 us
    all_to_all x1, starting transfers between devices, shards(): heat = lax.all_to_all(slab, WIDE, split_axis=0, concat_axis=0, tiled=True)  8.59 us
    pallas_call x1, Pallas kernels, strip(): pl.pallas_call(strip_body, out_shape=[jax.ShapeDtypeStruct((32, LANES), F...  6.49 us
    pallas_call x1, Pallas kernels, ready(): pl.pallas_call(ready_body, out_shape=[factor, factor, jax.ShapeDtypeStruc...  5.8 us
    pallas_call x1, Pallas kernels, pack_own(): pl.pallas_call(pack_own_body, out_shape=[jax.ShapeDtypeStruct((408, ROWS)...  5.31 us
  transfers between devices with their start and end apart: 8, of which 4 were waited for; matrix products, arithmetic and copies ran while one was open for 1% of the time, Pallas kernels for 13%

profile of v2, /device:TPU:5, one launch (start us, length us, event | category | flops | bytes accessed | tf_op | source)
XLA Modules:
  0.0 127.8 jit_solution(8867152752450225767)
XLA Ops:
  0.6 4.0 %cut.1 = (f32[16,11,32,128]{3,2,1,0:T(8,128)}, f32[39,16,128]{2,1,0:T(8,128)}, f32[39,16,128]{2,1,0:T(8,128)}) custom-call(f32[10,32,2048]{2,1,0:T(8,128)} %src.1, f32[36,512,128]{2,1,0:T(8,128)} %bitcast.10, f32[2,512,128]{2,1,0:T(8,128)} %motion.5, f32[512,128]{1,0:T(8,128)} %fictive.5), custom_call_target="tpu_custom_call" | custom-call | tf_op jit(solution)/shard_map/cut/pallas_call | solution.py:96
  4.6 0.0 copy-start
  4.6 8.6 %all-to-all-start = ((f32[16,11,32,128]{3,2,1,0:T(8,128)}), f32[16,11,32,128]{3,2,1,0:T(8,128)S(1)}, u32[]{:S(2)}, u32[]{:S(2)}) async-start(f32[16,11,32,128]{3,2,1,0:T(8,128)} %get-tuple-element.27), calls=%async_computation | async-start | bytes 5767168 | tf_op jit(solution)/shard_map/all_to_all | solution.py:569
  13.2 0.0 copy-done
  13.2 0.0 copy-start.1
  13.2 0.9 copy-done.1
  14.2 0.0 copy-start.7
  14.2 0.0 copy-start.8
  14.2 5.3 %pack_own.1 = (f32[408,512]{1,0:T(8,128)S(1)}, f32[392,512]{1,0:T(8,128)}) custom-call(f32[36,512,128]{2,1,0:T(8,128)} %bitcast.11, f32[2,512,128]{2,1,0:T(8,128)S(1)} %copy-done, f32[512,128]{1,0:T(8,128)S(1)} %copy-done.1), custom_call_target="tpu_custom_call" | custom-call | tf_op jit(solution)/shard_map/pack_own/pallas_call | solution.py:147
  19.5 0.0 copy-start.3
  19.5 0.9 copy-done.3
  20.4 4.6 %collective-permute-start.4 = (f32[392,512]{1,0:T(8,128)}, f32[392,512]{1,0:T(8,128)}, u32[]{:S(2)}, u32[]{:S(2)}) collective-permute-start(f32[392,512]{1,0:T(8,128)} %get-tuple-element.35), channel_id=1, source_target_pairs={{0,1},{1,2},{2,3},{3,4},{4,5},{5,6},{6,7},{7,8},{8,9},{9,10},{10,1... | collective-permute-start | bytes 2408456 | tf_op jit(solution)/shard_map/ppermute | solution.py:33
  25.0 3.9 %collective-permute-start = (f32[39,16,128]{2,1,0:T(8,128)}, f32[39,16,128]{2,1,0:T(8,128)}, u32[]{:S(2)}, u32[]{:S(2)}) collective-permute-start(f32[39,16,128]{2,1,0:T(8,128)} %get-tuple-element.29), channel_id=1, source_target_pairs={{0,16},{16,32},{32,48},{48,64},{64,80},{80,96},{96,112},{1,17},{17... | collective-permute-start | bytes 958472 | tf_op jit(solution)/shard_map/ppermute | solution.py:33
  28.9 1.3 %collective-permute-start.1 = (f32[39,16,128]{2,1,0:T(8,128)}, f32[39,16,128]{2,1,0:T(8,128)}, u32[]{:S(2)}, u32[]{:S(2)}) collective-permute-start(f32[39,16,128]{2,1,0:T(8,128)} %get-tuple-element.30), channel_id=1, source_target_pairs={{16,0},{32,16},{48,32},{64,48},{80,64},{96,80},{112,96},{17,1},{33... | collective-permute-start | bytes 958472 | tf_op jit(solution)/shard_map/ppermute | solution.py:33
  30.2 0.1 add_convert_fusion.flags
  30.3 0.0 copy-done.7
  30.3 0.0 copy-done.8
  30.3 0.6 fusion
  30.9 3.8 %collective-permute-done.up = f32[39,16,128]{2,1,0:T(8,128)} collective-permute-done((f32[39,16,128]{2,1,0:T(8,128)}, f32[39,16,128]{2,1,0:T(8,128)}, u32[]{:S(2)}, u32[]{:S(2)}) %collective-permute-start) | collective-permute-done | bytes 319520 | tf_op jit(solution)/shard_map/ppermute | solution.py:33
  34.8 4.5 %collective-permute-done.1.down = f32[39,16,128]{2,1,0:T(8,128)} collective-permute-done((f32[39,16,128]{2,1,0:T(8,128)}, f32[39,16,128]{2,1,0:T(8,128)}, u32[]{:S(2)}, u32[]{:S(2)}) %collective-permute-start.1) | collective-permute-done | bytes 319520 | tf_op jit(solution)/shard_map/ppermute | solution.py:33
  39.2 1.9 %pack_halo.1 = (f32[408,128]{1,0:T(8,128)S(1)}, f32[104,128]{1,0:T(8,128)S(1)}) custom-call(s32[3]{0:T(128)S(1)} %add_convert_fusion.flags, f32[39,16,128]{2,1,0:T(8,128)} %collective-permute-done.up, f32[39,16,128]{2,1,0:T(8,128)} %collective-permute-done.1.down), custom_call_target="tpu_custom_call" | custom-call | tf_op jit(solution)/shard_map/pack_halo/pallas_call | solution.py:179
  41.1 0.0 copy-start.5
  41.2 0.7 copy-done.5
  41.8 4.2 %collective-permute-start.5 = (f32[104,128]{1,0:T(8,128)S(1)}, f32[104,128]{1,0:T(8,128)S(1)}, u32[]{:S(2)}, u32[]{:S(2)}) collective-permute-start(f32[104,128]{1,0:T(8,128)S(1)} %get-tuple-element.36), channel_id=1, source_target_pairs={{0,1},{1,2},{2,3},{3,4},{4,5},{5,6},{6,7},{7,8},{8,9},{9,10},{10,1... | collective-permute-start | bytes 159752 | tf_op jit(solution)/shard_map/ppermute | solution.py:33
  46.0 24.5 %all-to-all-done.heat = f32[16,11,32,128]{3,2,1,0:T(8,128)S(1)} async-done(((f32[16,11,32,128]{3,2,1,0:T(8,128)}), f32[16,11,32,128]{3,2,1,0:T(8,128)S(1)}, u32[]{:S(2)}, u32[]{:S(2)}) %all-to-all-start) | async-done | bytes 2883616 | tf_op jit(solution)/shard_map/all_to_all | solution.py:569
  70.5 0.0 copy-start.6
  70.5 1.4 %collective-permute-start.3 = (f32[11,16,128]{2,1,0:T(8,128)S(1)}, f32[11,16,128]{2,1,0:T(8,128)S(1)}, u32[]{:S(2)}, u32[]{:S(2)}) collective-permute-start(f32[11,16,128]{2,1,0:T(8,128)S(1)} %get-tuple-element.53), channel_id=1, source_target_pairs={{16,0},{32,16},{48,32},{64,48},{80,64},{96,80},{112,96},{17,1},{33... | collective-permute-start | bytes 270344 | tf_op jit(solution)/shard_map/ppermute | solution.py:33
  71.9 4.0 %collective-permute-start.2 = (f32[11,16,128]{2,1,0:T(8,128)S(1)}, f32[11,16,128]{2,1,0:T(8,128)S(1)}, u32[]{:S(2)}, u32[]{:S(2)}) collective-permute-start(f32[11,16,128]{2,1,0:T(8,128)S(1)} %get-tuple-element.54), channel_id=1, source_target_pairs={{0,16},{16,32},{32,48},{48,64},{64,80},{80,96},{96,112},{1,17},{17... | collective-permute-start | bytes 270344 | tf_op jit(solution)/shard_map/ppermute | solution.py:33
  75.9 0.7 pad_maximum_fusion.coef
  76.7 0.0 copy-start.2
  76.7 0.9 copy-done.2
  77.6 0.0 copy-start.4
  77.6 5.8 %ready.1 = (f32[10,552,128]{2,1,0:T(8,128)S(1)}, f32[10,552,128]{2,1,0:T(8,128)S(1)}, f32[512,128]{1,0:T(8,128)}, f32[128,512]{1,0:T(8,128)S(1)}, f32[128,512]{1,0:T(8,128)S(1)}) custom-call(f32[16,11,32,128]{3,2,1,0:T(8,128)S(1)} %all-to-all-done.heat, f32[512,128]{1,0:T(8,128)S(1)} %copy-done.2), custom_call_target="tpu_custom_call" | custom-call | bytes 18000000 | tf_op jit(solution)/shard_map/ready/pallas_call | solution.py:234
  83.4 0.0 collective-permute-done.5.got_dense
  83.4 0.0 collective-permute-done.4.got
  83.4 0.0 copy-done.6
  83.4 0.0 copy-done.4
  83.4 1.5 %lay.1 = (f32[36,24,640]{2,1,0:T(8,128)S(1)}, f32[2,24,640]{2,1,0:T(8,128)S(1)}, f32[24,640]{1,0:T(8,128)S(1)}) custom-call(s32[3]{0:T(128)S(1)} %add_convert_fusion.flags, f32[408,512]{1,0:T(8,128)S(1)} %copy-done.4, f32[408,128]{1,0:T(8,128)S(1)} %copy-done.6, f32[392,512]{1,0:T(8,128)} %collective-permute-done.4.got, ...), custom_call_target="tpu_custom_call" | custom-call | bytes 6000000 | tf_op jit(solution)/shard_map/lay/pallas_call | solution.py:267
  84.9 0.0 collective-permute-done.3.heat_down
  84.9 0.0 collective-permute-done.2.heat_up
  85.0 6.5 %strip.1 = (f32[32,640]{1,0:T(8,128)S(1)}, f32[36,24,640]{2,1,0:T(8,128)S(1)}) custom-call(s32[3]{0:T(128)S(1)} %add_convert_fusion.flags, f32[25]{0:T(128)S(1)} %pad_maximum_fusion.coef, f32[36,24,640]{2,1,0:T(8,128)S(1)} %get-tuple-element.40.z_in, f32[2,24,640]{2,1,0:T(8,128)S(1)} %get-tuple-element.41.v_in, ...), custom_call_target="tpu_custom_call", output_to_operand_aliasing={{1}: (2, {})} | custom-call | bytes 21000000 | tf_op jit(solution)/shard_map/strip/pallas_call | solution.py:344
  91.5 1.9 %collective-permute-start.6 = (f32[32,640]{1,0:T(8,128)S(1)}, f32[32,640]{1,0:T(8,128)S(1)}, u32[]{:S(2)}, u32[]{:S(2)}) collective-permute-start(f32[32,640]{1,0:T(8,128)S(1)} %get-tuple-element.45.nodes), channel_id=1, source_target_pairs={{1,0},{2,1},{3,2},{4,3},{5,4},{6,5},{7,6},{8,7},{9,8},{10,9},{11,1... | collective-permute-start | bytes 245768 | tf_op jit(solution)/shard_map/ppermute | solution.py:33
  93.4 2.7 %edges.1 = (f32[10,552,128]{2,1,0:T(8,128)S(1)}, f32[10,552,128]{2,1,0:T(8,128)S(1)}, f32[10,2,544,128]{3,2,1,0:T(8,128)S(1)}) custom-call(s32[3]{0:T(128)S(1)} %add_convert_fusion.flags, f32[10,552,128]{2,1,0:T(8,128)S(1)} %get-tuple-element.31.inv_in, f32[10,552,128]{2,1,0:T(8,128)S(1)} %get-tuple-element.32.half_in, ...), custom_call_target="tpu_custom_call", output_to_operand_aliasing={{0}: (1, {}), {1}: (2, {})} | custom-call | bytes 9000000 | tf_op jit(solution)/shard_map/edges/pallas_call | solution.py:393
  96.1 2.1 %collective-permute-done.6.beside_t = f32[32,640]{1,0:T(8,128)S(1)} collective-permute-done((f32[32,640]{1,0:T(8,128)S(1)}, f32[32,640]{1,0:T(8,128)S(1)}, u32[]{:S(2)}, u32[]{:S(2)}) %collective-permute-start.6) | collective-permute-done | bytes 81952 | tf_op jit(solution)/shard_map/ppermute | solution.py:33
  98.1 29.6 %block.1 = (f32[2,512,128]{2,1,0:T(8,128)}, f32[36,512,128]{2,1,0:T(8,128)}) custom-call(s32[3]{0:T(128)S(1)} %add_convert_fusion.flags, f32[25]{0:T(128)S(1)} %pad_maximum_fusion.coef, f32[36,512,128]{2,1,0:T(8,128)} %bitcast.12, f32[2,512,128]{2,1,0:T(8,128)S(1)} %copy-done, f32[39,16,128]{2,1,0:T(8,128)} %collective-permute-done.up, ...), custom_call_target="tpu_custom_call" | custom-call | bytes 84000000 | tf_op jit(solution)/shard_map/block/pallas_call | solution.py:536
  (1 shorter events, 0.0 us)
Async XLA Ops:
  4.6 8.6 %copy-start = (f32[2,512,128]{2,1,0:T(8,128)S(1)}, f32[2,512,128]{2,1,0:T(8,128)}, u32[]{:S(2)}) copy-start(f32[2,512,128]{2,1,0:T(8,128)} %motion.5) | copy-start | bytes 1572868
  4.6 65.9 %all-to-all-start = ((f32[16,11,32,128]{3,2,1,0:T(8,128)}), f32[16,11,32,128]{3,2,1,0:T(8,128)S(1)}, u32[]{:S(2)}, u32[]{:S(2)}) async-start(f32[16,11,32,128]{3,2,1,0:T(8,128)} %get-tuple-element.27), calls=%async_computation | async-start | bytes 5767168 | tf_op jit(solution)/shard_map/all_to_all | solution.py:569
  13.2 1.0 copy-start.1
  14.2 16.1 %copy-start.7 = (f32[12]{0:T(128)S(1)}, f32[12]{0:T(128)}, u32[]{:S(2)}) copy-start(f32[12]{0:T(128)} %param.10) | copy-start | bytes 148
  14.2 16.1 %copy-start.8 = (f32[12]{0:T(128)S(1)}, f32[12]{0:T(128)}, u32[]{:S(2)}) copy-start(f32[12]{0:T(128)} %param.11) | copy-start | bytes 148
  19.5 0.9 copy-start.3
  20.4 63.0 %collective-permute-start.4 = (f32[392,512]{1,0:T(8,128)}, f32[392,512]{1,0:T(8,128)}, u32[]{:S(2)}, u32[]{:S(2)}) collective-permute-start(f32[392,512]{1,0:T(8,128)} %get-tuple-element.35), channel_id=1, source_target_pairs={{0,1},{1,2},{2,3},{3,4},{4,5},{5,6},{6,7},{7,8},{8,9},{9,10},{10,1... | collective-permute-start | bytes 2408456 | tf_op jit(solution)/shard_map/ppermute | solution.py:33
  25.0 9.7 %collective-permute-start = (f32[39,16,128]{2,1,0:T(8,128)}, f32[39,16,128]{2,1,0:T(8,128)}, u32[]{:S(2)}, u32[]{:S(2)}) collective-permute-start(f32[39,16,128]{2,1,0:T(8,128)} %get-tuple-element.29), channel_id=1, source_target_pairs={{0,16},{16,32},{32,48},{48,64},{64,80},{80,96},{96,112},{1,17},{17... | collective-permute-start | bytes 958472 | tf_op jit(solution)/shard_map/ppermute | solution.py:33
  28.9 10.3 %collective-permute-start.1 = (f32[39,16,128]{2,1,0:T(8,128)}, f32[39,16,128]{2,1,0:T(8,128)}, u32[]{:S(2)}, u32[]{:S(2)}) collective-permute-start(f32[39,16,128]{2,1,0:T(8,128)} %get-tuple-element.30), channel_id=1, source_target_pairs={{16,0},{32,16},{48,32},{64,48},{80,64},{96,80},{112,96},{17,1},{33... | collective-permute-start | bytes 958472 | tf_op jit(solution)/shard_map/ppermute | solution.py:33
  41.1 0.7 copy-start.5
  41.8 41.6 %collective-permute-start.5 = (f32[104,128]{1,0:T(8,128)S(1)}, f32[104,128]{1,0:T(8,128)S(1)}, u32[]{:S(2)}, u32[]{:S(2)}) collective-permute-start(f32[104,128]{1,0:T(8,128)S(1)} %get-tuple-element.36), channel_id=1, source_target_pairs={{0,1},{1,2},{2,3},{3,4},{4,5},{5,6},{6,7},{7,8},{8,9},{9,10},{10,1... | collective-permute-start | bytes 159752 | tf_op jit(solution)/shard_map/ppermute | solution.py:33
  70.5 12.9 %copy-start.6 = (f32[408,128]{1,0:T(8,128)S(1)}, f32[408,128]{1,0:T(8,128)}, u32[]{:S(2)}) copy-start(f32[408,128]{1,0:T(8,128)} %copy-done.5) | copy-start | bytes 626692
  70.5 14.4 %collective-permute-start.3 = (f32[11,16,128]{2,1,0:T(8,128)S(1)}, f32[11,16,128]{2,1,0:T(8,128)S(1)}, u32[]{:S(2)}, u32[]{:S(2)}) collective-permute-start(f32[11,16,128]{2,1,0:T(8,128)S(1)} %get-tuple-element.53), channel_id=1, source_target_pairs={{16,0},{32,16},{48,32},{64,48},{80,64},{96,80},{112,96},{17,1},{33... | collective-permute-start | bytes 270344 | tf_op jit(solution)/shard_map/ppermute | solution.py:33
  71.9 13.0 %collective-permute-start.2 = (f32[11,16,128]{2,1,0:T(8,128)S(1)}, f32[11,16,128]{2,1,0:T(8,128)S(1)}, u32[]{:S(2)}, u32[]{:S(2)}) collective-permute-start(f32[11,16,128]{2,1,0:T(8,128)S(1)} %get-tuple-element.54), channel_id=1, source_target_pairs={{0,16},{16,32},{32,48},{48,64},{64,80},{80,96},{96,112},{1,17},{17... | collective-permute-start | bytes 270344 | tf_op jit(solution)/shard_map/ppermute | solution.py:33
  76.7 1.0 copy-start.2
  77.6 5.8 %copy-start.4 = (f32[408,512]{1,0:T(8,128)S(1)}, f32[408,512]{1,0:T(8,128)}, u32[]{:S(2)}) copy-start(f32[408,512]{1,0:T(8,128)} %copy-done.3) | copy-start | bytes 2506756
  91.5 6.7 %collective-permute-start.6 = (f32[32,640]{1,0:T(8,128)S(1)}, f32[32,640]{1,0:T(8,128)S(1)}, u32[]{:S(2)}, u32[]{:S(2)}) collective-permute-start(f32[32,640]{1,0:T(8,128)S(1)} %get-tuple-element.45.nodes), channel_id=1, source_target_pairs={{1,0},{2,1},{3,2},{4,3},{5,4},{6,5},{7,6},{8,7},{9,8},{10,9},{11,1... | collective-permute-start | bytes 245768 | tf_op jit(solution)/shard_map/ppermute | solution.py:33

commit v3 on v2

--- a/solution.py
+++ b/solution.py
@@ -18,6 +18,8 @@
 LANES = 640
 SUBS = 24
 PAD = 8
+EDGE = 392
+SPAN = 3
 SUB = 16
 FLOW = 272
 F32 = jnp.float32
@@ -120,71 +122,70 @@
     return jnp.concatenate([own[i * COLS:(i + 1) * COLS].T for i in range(4)], axis=1)
 
 
-def pack_own_body(state, motion, fictive, first, last, buf, sem):
+def pack_body(flags, state, motion, fictive, up, down, first_out, send, buf, tail, first, more, sem, more_sem):
     copies = [pltpu.make_async_copy(state.at[pl.ds(4 * i, 4)], buf.at[pl.ds(4 * i, 4)], sem.at[i]) for i in range(9)]
-    for c in copies:
+    rest = [pltpu.make_async_copy(motion, more.at[pl.ds(0, 2)], more_sem.at[0]), pltpu.make_async_copy(fictive, more.at[2], more_sem.at[1])]
+    for c in rest + copies:
         c.start()
-    rest = [turned(motion[0]), turned(motion[1]), turned(fictive[...])]
-    put_rest(rest, first, last)
+
+    def put(at, blocks, corners, widths):
+        for i in range(5):
+            parts = corners if i == 4 else [b[i * COLS:(i + 1) * COLS].T for b in blocks]
+            lanes = slice(i * COLS, (i + 1) * COLS)
+            own = jnp.concatenate([p[:w] for p, w in zip(parts, widths)], axis=0)
+            first[at:at + own.shape[0], lanes] = own
+            gone = [p[COLS - DEEP:] for p in parts]
+            if len(gone) == 3:
+                gone.append(jnp.zeros((2, COLS), F32))
+            gone = jnp.concatenate(gone, axis=0)
+            if i < 4:
+                send[EDGE * i + at:EDGE * i + at + gone.shape[0], :] = gone
+            else:
+                tail[at:at + gone.shape[0], :] = gone
+
+    f_up = jnp.where(flags[0] == 1, OUTSIDE, up[38])
+    f_down = jnp.where(flags[1] == 1, OUTSIDE, down[38])
+    for c in rest:
+        c.wait()
+    put(360, [more[0], more[1], more[2]], [corner(up[36], down[36], 0.0), corner(up[37], down[37], 0.0), corner(f_up, f_down, 1.0)], (16, 16, 16))
     for i in range(9):
         copies[i].wait()
-        put_state(i, [turned(buf[4 * i + q]) for q in range(4)], first, last)
-
-
-def put_rest(rest, first, last):
-    first[360:400, :] = jnp.concatenate([rest[0][:16], rest[1][:16], rest[2][:8]], axis=0)
-    first[400:408, :] = rest[2][8:16]
-    last[360:392, :] = jnp.concatenate([r[COLS - DEEP:] for r in rest] + [rest[0][:2]], axis=0)
-
-
-def put_state(i, blocks, first, last):
-    first[40 * i:40 * i + 40, :] = jnp.concatenate([b[:DEEP] for b in blocks], axis=0)
-    last[40 * i:40 * i + 40, :] = jnp.concatenate([b[COLS - DEEP:] for b in blocks], axis=0)
-
-
-def pack_own(state, motion, fictive):
-    full = pl.BlockSpec(memory_space=VMEM)
-    return pl.pallas_call(
-        pack_own_body,
-        out_shape=[jax.ShapeDtypeStruct((408, ROWS), F32), jax.ShapeDtypeStruct((392, ROWS), F32)],
-        in_specs=[pl.BlockSpec(memory_space=pltpu.HBM), full, full],
-        out_specs=[full] * 2,
-        scratch_shapes=[VMEM((36, ROWS, COLS), F32), pltpu.SemaphoreType.DMA((9,))],
-        compiler_params=params(20),
-        name="pack_own",
-    )(pinned(state), motion, fictive)
-
-
-def pack_halo_body(flags, up, down, first, dense, last):
-    f_up = jnp.where(flags[0] == 1, OUTSIDE, up[38])
-    f_down = jnp.where(flags[1] == 1, OUTSIDE, down[38])
-    put_rest([corner(up[36], down[36], 0.0), corner(up[37], down[37], 0.0), corner(f_up, f_down, 1.0)], first, last)
-    for i in range(9):
-        put_state(i, [corner(up[4 * i + q], down[4 * i + q], 0.0) for q in range(4)], first, last)
-    last[392:416, :] = jnp.zeros((24, COLS), F32)
+        put(40 * i, [buf[4 * i + j] for j in range(4)], [corner(up[4 * i + j], down[4 * i + j], 0.0) for j in range(4)], (DEEP,) * 4)
+    keep = pltpu.make_async_copy(first, first_out, more_sem.at[2])
+    keep.start()
+    tail[EDGE:416, :] = jnp.zeros((416 - EDGE, COLS), F32)
     lane = iota((104, COLS), 1)
     acc = jnp.zeros((104, COLS), F32)
-    for g in range(4):
-        moved = pltpu.roll(last[104 * g:104 * g + 104, :], (HALO + 32 * g) % COLS, 1)
-        acc = jnp.where((lane >= 32 * g) & (lane < 32 * g + 32), moved, acc)
-    dense[...] = acc
+    for j in range(4):
+        moved = pltpu.roll(tail[104 * j:104 * j + 104, :], (HALO + 32 * j) % COLS, 1)
+        acc = jnp.where((lane >= 32 * j) & (lane < 32 * j + 32), moved, acc)
+    send[4 * EDGE:, :] = acc
+    keep.wait()
 
 
 def spread(dense):
-    return jnp.concatenate([pltpu.roll(dense, COLS - HALO - 32 * g, 1) for g in range(4)], axis=0)
-
-
-def pack_halo(flags, up, down):
+    return jnp.concatenate([pltpu.roll(dense, COLS - HALO - 32 * j, 1) for j in range(4)], axis=0)
+
+
+def pack(flags, state, motion, fictive, up, down):
     full = pl.BlockSpec(memory_space=VMEM)
+    hbm = pl.BlockSpec(memory_space=pltpu.HBM)
     return pl.pallas_call(
-        pack_halo_body,
-        out_shape=[jax.ShapeDtypeStruct((408, COLS), F32), jax.ShapeDtypeStruct((104, COLS), F32)],
-        in_specs=[pl.BlockSpec(memory_space=SMEM), full, full],
-        out_specs=[full] * 2,
-        scratch_shapes=[VMEM((416, COLS), F32)],
-        compiler_params=params(8),
-        name="pack_halo",
-    )(flags, up, down)
+        pack_body,
+        out_shape=[pltpu.HBM((408, LANES), F32), jax.ShapeDtypeStruct((4 * EDGE + 104, COLS), F32)],
+        in_specs=[pl.BlockSpec(memory_space=SMEM)] + [hbm] * 3 + [full] * 2,
+        out_specs=[hbm, full],
+        scratch_shapes=[
+            VMEM((36, ROWS, COLS), F32),
+            VMEM((416, COLS), F32),
+            VMEM((408, LANES), F32),
+            VMEM((3, ROWS, COLS), F32),
+            pltpu.SemaphoreType.DMA((9,)),
+            pltpu.SemaphoreType.DMA((3,)),
+        ],
+        compiler_params=params(20),
+        name="pack",
+    )(flags, pinned(state), pinned(motion), pinned(fictive), up, down)
 
 
 def shift_of(theta, fict):
@@ -211,69 +212,61 @@
     return inv, 0.5 * shift, theta + (fict - theta) * jnp.exp(inv * (-1.0 / 3.0))
 
 
-def ready_body(heat, fictive, inv_ref, half_ref, f_out, mine, side):
-    def piece(s, _):
-        at = pl.ds(pl.multiple_of(32 * s, 32), 32)
-        to = pl.ds(pl.multiple_of(32 * s + HALO, 16), 32)
-        fict = fictive[at, :]
-        for n in range(TICKS):
-            inv_ref[n, to, :], half_ref[n, to, :], fict = advance(heat[s, n], fict)
-        f_out[at, :] = fict
-        return 0
-
-    lax.fori_loop(0, PIECES, piece, 0)
+def ready_body(heat, mine, side):
     own = jnp.concatenate([beside_each_other(lambda n: heat[s, n], 32) for s in range(PIECES)], axis=0)
     mine[...] = turned(own)
     side[...] = turned(jnp.concatenate([heat[s, TICKS] for s in range(PIECES)], axis=0))
 
 
-def ready(heat, fictive):
+def ready(heat):
     full = pl.BlockSpec(memory_space=VMEM)
-    factor = jax.ShapeDtypeStruct((TICKS, EXT + PAD, COLS), F32)
     row_t = jax.ShapeDtypeStruct((COLS, ROWS), F32)
     return pl.pallas_call(
         ready_body,
-        out_shape=[factor, factor, jax.ShapeDtypeStruct((ROWS, COLS), F32), row_t, row_t],
-        in_specs=[full] * 2,
-        out_specs=[full] * 5,
-        compiler_params=params(16),
-        cost_estimate=work(6),
+        out_shape=[row_t, row_t],
+        in_specs=[full],
+        out_specs=[full] * 2,
+        compiler_params=params(8),
+        cost_estimate=work(3),
         name="ready",
-    )(heat, fictive)
-
-
-def lay_body(flags, first, first_halo, got, got_dense, z, v, fict, got_halo):
+    )(heat)
+
+
+def lay_body(flags, first, got, z, v, fict, got_halo):
     rest = SUBS - 2 * DEEP
     lane = iota((416, COLS), 1)
     blank = jnp.where((iota((416, COLS), 0) >= 380) & (iota((416, COLS), 0) < 390), 1.0, 0.0)
-    got_halo[...] = jnp.where((lane < HALO) | (lane >= COLS - HALO), spread(got_dense[...]), blank)
-    for lanes, own, left in ((slice(0, ROWS), first, got), (slice(ROWS, LANES), first_halo, got_halo)):
-        width = lanes.stop - lanes.start
+    got_halo[...] = jnp.where((lane < HALO) | (lane >= COLS - HALO), spread(got[4 * EDGE:, :]), blank)
+    for k in range(36):
+        z[k, DEEP:2 * DEEP, :] = first[DEEP * k:DEEP * k + DEEP, :]
+        z[k, 2 * DEEP:SUBS, :] = jnp.zeros((rest, LANES), F32)
+    for k in range(2):
+        v[k, DEEP:SUBS, :] = first[360 + 16 * k:360 + 16 * k + SUBS - DEEP, :]
+    fict[DEEP:2 * DEEP, :] = first[392:402, :]
+    fict[2 * DEEP:SUBS, :] = jnp.ones((rest, LANES), F32)
+    for i in range(5):
+        lanes = slice(i * COLS, (i + 1) * COLS)
+        left = got_halo if i == 4 else got.at[pl.ds(EDGE * i, EDGE)]
         for k in range(36):
             z[k, 0:DEEP, lanes] = left[DEEP * k:DEEP * k + DEEP, :]
-            z[k, DEEP:2 * DEEP, lanes] = own[DEEP * k:DEEP * k + DEEP, :]
-            z[k, 2 * DEEP:SUBS, lanes] = jnp.zeros((rest, width), F32)
         for k in range(2):
             v[k, 0:DEEP, lanes] = left[360 + DEEP * k:370 + DEEP * k, :]
-            v[k, DEEP:SUBS, lanes] = own[360 + 16 * k:360 + 16 * k + SUBS - DEEP, :]
         fict[0:DEEP, lanes] = jnp.where(flags[2] == 1, OUTSIDE, left[380:390, :])
-        fict[DEEP:2 * DEEP, lanes] = own[392:402, :]
-        fict[2 * DEEP:SUBS, lanes] = jnp.ones((rest, width), F32)
-
-
-def lay(flags, first, first_halo, got, got_halo):
+
+
+def lay(flags, first, got):
     full = pl.BlockSpec(memory_space=VMEM)
     shapes = [(36, SUBS, LANES), (2, SUBS, LANES), (SUBS, LANES)]
     return pl.pallas_call(
         lay_body,
         out_shape=[jax.ShapeDtypeStruct(s, F32) for s in shapes],
-        in_specs=[pl.BlockSpec(memory_space=SMEM)] + [full] * 4,
+        in_specs=[pl.BlockSpec(memory_space=SMEM)] + [full] * 2,
         out_specs=[full] * 3,
         scratch_shapes=[VMEM((416, COLS), F32)],
         compiler_params=params(8),
         cost_estimate=work(2),
         name="lay",
-    )(flags, first, first_halo, got, got_halo)
+    )(flags, first, got)
 
 
 def strip_body(flags, coef, z_in, v_in, fict_in, mine, side, heat_up, heat_down, nodes, z, v, q, heat_t):
@@ -293,49 +286,52 @@
         heat_t[n, DEEP:2 * DEEP, ROWS:LANES] = last_mine[cols]
         heat_t[n, 2 * DEEP:SUBS, :] = jnp.ones((rest, LANES), F32)
 
-    lane = iota((SUBS, LANES), 1)
-    inside = jnp.where(bottom & (lane >= ROWS) & (lane < LANES - HALO), 0.0, 1.0)
+    inside = jnp.where(bottom & (iota((8, LANES), 1) >= ROWS) & (iota((8, LANES), 1) < LANES - HALO), 0.0, 1.0)
     sum_a = coef[24]
     nodes[...] = jnp.zeros((32, LANES), F32)
     nodes[31:32, :] = v[0, DEEP:DEEP + 1, :]
     nodes[0:1, :] = v[1, DEEP:DEEP + 1, :]
 
-    def tick(n, fict):
-        inv, half, fict_next = advance(heat_t[n], fict)
+    def tick(n, fict, lo, hi):
+        at, size = slice(lo, hi), hi - lo
+        inv, half, fict_next = advance(heat_t[n, at], fict)
+        keep = jnp.concatenate([inside] * (size // 8), axis=0)
 
         def grads(m):
-            beside = pltpu.roll(m, SUBS - 1, 0)
+            beside = pltpu.roll(m, size - 1, 0)
             both, diff = m + beside, beside - m
             return pltpu.roll(both, LANES - 1, 1) - both, pltpu.roll(diff, LANES - 1, 1) + diff
 
-        u, w = v[0], v[1]
+        u, w = v[0, at], v[1, at]
         lu, wu = grads(u)
         lw, ww = grads(w)
         now = [half * lu, half * ww, (0.5 * half) * (wu + lw)]
-        delta = [q[c] - now[c] for c in range(3)]
+        delta = [q[c, at] - now[c] for c in range(3)]
         for c in range(3):
-            q[c] = now[c]
+            q[c, at] = now[c]
         total = [sum_a * now[c] for c in range(3)]
         for k in range(MODES):
             kept = jnp.exp2(inv * coef[k])
             a = coef[12 + k]
             for c in range(3):
-                new = kept * (z[3 * k + c] + a * delta[c])
-                z[3 * k + c] = new
+                new = kept * (z[3 * k + c, at] + a * delta[c])
+                z[3 * k + c, at] = new
                 total[c] = total[c] + new
 
         def force(lin, cross):
             a, b = lin + cross, lin - cross
             return 0.5 * ((a - pltpu.roll(b, 1, 1)) + pltpu.roll(b - pltpu.roll(a, 1, 1), 1, 0))
 
-        u_next = (u + force(total[0], total[2])) * inside
-        w_next = (w + force(total[2], total[1])) * inside
-        v[0], v[1] = u_next, w_next
-        nodes[pl.ds(2 * n + 1, 1), :] = u_next[DEEP:DEEP + 1]
-        nodes[pl.ds(2 * n + 2, 1), :] = w_next[DEEP:DEEP + 1]
+        u_next = (u + force(total[0], total[2])) * keep
+        w_next = (w + force(total[2], total[1])) * keep
+        v[0, at], v[1, at] = u_next, w_next
+        nodes[pl.ds(2 * n + 1, 1), :] = u_next[DEEP - lo:DEEP - lo + 1]
+        nodes[pl.ds(2 * n + 2, 1), :] = w_next[DEEP - lo:DEEP - lo + 1]
         return fict_next
 
-    lax.fori_loop(0, TICKS, tick, fict_in[...])
+    fict = lax.fori_loop(0, 5, lambda n, f: tick(n, f, 0, SUBS), fict_in[...])
+    fict = lax.fori_loop(5, 8, lambda n, f: tick(n, f, 0, 16), fict[:16])
+    lax.fori_loop(8, TICKS, lambda n, f: tick(n, f, 8, 16), fict[8:16])
 
 
 def strip(flags, coef, z, v, fict, mine, side, heat_up, heat_down):
@@ -363,7 +359,13 @@
     return jnp.concatenate([part[:24], jnp.zeros((COLS - 32, COLS), F32), part[24:]], axis=0).T
 
 
-def edges_body(flags, inv_in, half_in, up, down, heat_up, heat_down, nodes, inv_ref, half_ref, left):
+def edges_body(flags, heat, fictive, up, down, heat_up, heat_down, nodes, inv_ref, half_ref, f_out, left):
+    for s in range(0, PIECES, 8):
+        at, to = slice(32 * s, 32 * s + 256), slice(32 * s + HALO, 32 * s + HALO + 256)
+        own = fictive[at, :]
+        for n in range(TICKS):
+            inv_ref[n, to, :], half_ref[n, to, :], own = advance(heat[s:s + 8, n].reshape(256, COLS), own)
+        f_out[at, :] = own
     top, bottom = flags[0] == 1, flags[1] == 1
     fict = jnp.concatenate([jnp.where(top, OUTSIDE, up[38]), jnp.where(bottom, OUTSIDE, down[38])], axis=0)
     for n in range(TICKS):
@@ -387,19 +389,18 @@
                     left[n, c, 0:HALO, :] = moved[COLS - HALO:]
 
 
-def edges(flags, inv, half, up, down, heat_up, heat_down, nodes):
+def edges(flags, heat, fictive, up, down, heat_up, heat_down, nodes):
     full = pl.BlockSpec(memory_space=VMEM)
     factor = jax.ShapeDtypeStruct((TICKS, EXT + PAD, COLS), F32)
     return pl.pallas_call(
         edges_body,
-        out_shape=[factor, factor, jax.ShapeDtypeStruct((TICKS, 2, EXT, COLS), F32)],
+        out_shape=[factor, factor, jax.ShapeDtypeStruct((ROWS, COLS), F32), jax.ShapeDtypeStruct((TICKS, 2, EXT, COLS), F32)],
         in_specs=[pl.BlockSpec(memory_space=SMEM)] + [full] * 7,
-        out_specs=[full] * 3,
-        input_output_aliases={1: 0, 2: 1},
-        compiler_params=params(18),
-        cost_estimate=work(3),
+        out_specs=[full] * 4,
+        compiler_params=params(12),
+        cost_estimate=work(6),
         name="edges",
-    )(flags, inv, half, up, down, heat_up, heat_down, nodes)
+    )(flags, heat, fictive, up, down, heat_up, heat_down, nodes)
 
 
 def block_body(flags, coef, state, motion, up, down, inv_ref, half_ref, left, beside_t, v_out, s_out, z, v, q, h, pairs, forces, zh, sem, in_sem):
@@ -501,16 +502,18 @@
             in_copy(0).wait()
         relax_group(n, 0, final)
 
-        def body(b, _):
-            if starting:
-                in_copy(b).wait()
-            relax_group(n, b, final)
-            if final:
-                out_copy(b).start()
+        def body(i, _):
+            for j in range(SPAN):
+                b = SPAN * i + j + 1
+                if starting:
+                    in_copy(b).wait()
+                relax_group(n, b, final)
+                if final:
+                    out_copy(b).start()
             return 0
 
         last = EXT // 32 - 1
-        lax.fori_loop(1, last, body, 0)
+        lax.fori_loop(0, (last - 1) // SPAN, body, 0)
         relax_group(n, last, final)
         if final:
             out_copy(last).start()
@@ -569,18 +572,17 @@
     heat = lax.all_to_all(slab, WIDE, split_axis=0, concat_axis=0, tiled=True)
     up = shifted(above, "draw", 1)
     down = shifted(below, "draw", -1)
-    first, final = pack_own(state, vertex_velocity, fictitious_warmth)
+    up, down, coef = lax.optimization_barrier((up, down, coef))
+    first, final = pack(flags, state, vertex_velocity, fictitious_warmth, up, down)
     got = shifted(final, WIDE, 1)
-    first_halo, final_halo = pack_halo(flags, up, down)
-    got_halo = shifted(final_halo, WIDE, 1)
     heat_up = shifted(heat[PIECES - 1, :, HALO:, :], "draw", 1)
     heat_down = shifted(heat[0, :, :HALO, :], "draw", -1)
-    inv, half, fict, mine, side = ready(heat, fictitious_warmth)
-    got, got_halo, mine = lax.optimization_barrier((got, got_halo, mine))
-    strip_state = lay(flags, first, first_halo, got, got_halo)
+    mine, side = ready(heat)
+    got, mine = lax.optimization_barrier((got, mine))
+    strip_state = lay(flags, first, got)
     nodes = strip(flags, coef, *strip_state, mine, side, heat_up, heat_down)
     beside = shifted(nodes, WIDE, -1)
-    inv, half, left = edges(flags, inv, half, up, down, heat_up, heat_down, nodes)
+    inv, half, fict, left = edges(flags, heat, fictitious_warmth, up, down, heat_up, heat_down, nodes)
     motion, modes = block(flags, coef, state, vertex_velocity, up, down, inv, half, left, beside)
     return fict, motion, modes.reshape(branch_load_tensors.shape)
 

time: 128 us -> 124 us (0.969); the launches traced: 128 us -> 122 us
  starting transfers between devices: 29.9 us -> 25.9 us
  local copies, waits for them, and re-layouts: 3.51 us -> 0.04 us
  waiting for transfers between devices: 34.9 us -> 38.1 us
  Pallas kernels: 57.3 us -> 55.2 us
    ppermute x7 -> x6, starting transfers between devices: 21.3 us -> 17.4 us  [shifted(): return lax.ppermute(shard, axis, pairs)]
    unnamed x18 -> x10, local copies, waits for them, and re-layouts: 3.5 us -> 0.03 us
    ppermute x7 -> x6, waiting for transfers between devices: 10.4 us -> 13.3 us  [shifted(): return lax.ppermute(shard, axis, pairs)]
    pallas_call x3 -> x2, Pallas kernels: 13 us -> 11 us  [the longest x1 10.2 us: pack(): pl.pallas_call(pack_body, out_shape=[pltpu.HBM((408, LANES), F32), jax.Sh...]
    pallas_call x1, Pallas kernels: 2.68 us -> 4.46 us  [edges(): pl.pallas_call(edges_body, out_shape=[factor, factor, jax.ShapeDtypeStruc...]
  transfers between devices with their start and end apart: 8 -> 7, of which waited for: 4 -> 4; matrix products, arithmetic and copies ran while one was open for 1% -> 1% of each run, Pallas kernels for 13% -> 14%
where the time goes in v3:
time: 124 us; the launch traced here: 122 us
  Pallas kernels  55.2 us (45%)
  waiting for transfers between devices  38.1 us (31%)
  starting transfers between devices  25.9 us (21%)
  other arithmetic  1.4 us (1%)
    pallas_call x1, Pallas kernels, block(): pl.pallas_call(block_body, out_shape=[jax.ShapeDtypeStruct((2, ROWS, COLS...  28.5 us
    all_to_all x1, waiting for transfers between devices, shards(): heat = lax.all_to_all(slab, WIDE, split_axis=0, concat_axis=0, tiled=True)  24.8 us
    ppermute x6, starting transfers between devices, shifted(): return lax.ppermute(shard, axis, pairs)  17.4 us
    ppermute x6, waiting for transfers between devices, shifted(): return lax.ppermute(shard, axis, pairs)  13.3 us
    pallas_call x1, Pallas kernels, pack(): pl.pallas_call(pack_body, out_shape=[pltpu.HBM((408, LANES), F32), jax.Sh...  10.2 us
    all_to_all x1, starting transfers between devices, shards(): heat = lax.all_to_all(slab, WIDE, split_axis=0, concat_axis=0, tiled=True)  8.46 us
    pallas_call x1, Pallas kernels, strip(): pl.pallas_call(strip_body, out_shape=[jax.ShapeDtypeStruct((32, LANES), F...  5.78 us
    pallas_call x1, Pallas kernels, edges(): pl.pallas_call(edges_body, out_shape=[factor, factor, jax.ShapeDtypeStruc...  4.46 us
  transfers between devices with their start and end apart: 7, of which 4 were waited for; matrix products, arithmetic and copies ran while one was open for 1% of the time, Pallas kernels for 14%

profile of v3, /device:TPU:5, one launch (start us, length us, event | category | flops | bytes accessed | tf_op | source)
XLA Modules:
  0.0 121.6 jit_solution(14148678904173324505)
XLA Ops:
  0.6 4.0 %cut.1 = (f32[16,11,32,128]{3,2,1,0:T(8,128)}, f32[39,16,128]{2,1,0:T(8,128)}, f32[39,16,128]{2,1,0:T(8,128)}) custom-call(f32[10,32,2048]{2,1,0:T(8,128)} %src.1, f32[36,512,128]{2,1,0:T(8,128)} %bitcast.10, f32[2,512,128]{2,1,0:T(8,128)} %motion.5, f32[512,128]{1,0:T(8,128)} %fictive.5), custom_call_target="tpu_custom_call" | custom-call | tf_op jit(solution)/shard_map/cut/pallas_call | solution.py:98
  4.6 0.0 copy-start.3
  4.6 0.0 copy-start.4
  4.6 8.5 %all-to-all-start = ((f32[16,11,32,128]{3,2,1,0:T(8,128)}), f32[16,11,32,128]{3,2,1,0:T(8,128)S(1)}, u32[]{:S(2)}, u32[]{:S(2)}) async-start(f32[16,11,32,128]{3,2,1,0:T(8,128)} %get-tuple-element.25), calls=%async_computation | async-start | bytes 5767168 | tf_op jit(solution)/shard_map/all_to_all | solution.py:572
  13.1 3.2 %collective-permute-start = (f32[39,16,128]{2,1,0:T(8,128)}, f32[39,16,128]{2,1,0:T(8,128)S(1)}, u32[]{:S(2)}, u32[]{:S(2)}) collective-permute-start(f32[39,16,128]{2,1,0:T(8,128)} %get-tuple-element.26), channel_id=1, source_target_pairs={{0,16},{16,32},{32,48},{48,64},{64,80},{80,96},{96,112},{1,17},{17... | collective-permute-start | bytes 958472 | tf_op jit(solution)/shard_map/ppermute | solution.py:35
  16.3 1.3 %collective-permute-start.1 = (f32[39,16,128]{2,1,0:T(8,128)}, f32[39,16,128]{2,1,0:T(8,128)S(1)}, u32[]{:S(2)}, u32[]{:S(2)}) collective-permute-start(f32[39,16,128]{2,1,0:T(8,128)} %get-tuple-element.27), channel_id=1, source_target_pairs={{16,0},{32,16},{48,32},{64,48},{80,64},{96,80},{112,96},{17,1},{33... | collective-permute-start | bytes 958472 | tf_op jit(solution)/shard_map/ppermute | solution.py:35
  17.6 0.1 add_convert_fusion.flags
  17.7 0.0 copy-done.3
  17.7 0.0 copy-done.4
  17.7 0.6 fusion
  18.3 0.7 pad_maximum_fusion.coef
  19.0 4.1 %collective-permute-done.up = f32[39,16,128]{2,1,0:T(8,128)S(1)} collective-permute-done((f32[39,16,128]{2,1,0:T(8,128)}, f32[39,16,128]{2,1,0:T(8,128)S(1)}, u32[]{:S(2)}, u32[]{:S(2)}) %collective-permute-start) | collective-permute-done | bytes 319520 | tf_op jit(solution)/shard_map/ppermute | solution.py:35
  23.1 3.7 %collective-permute-done.1.down = f32[39,16,128]{2,1,0:T(8,128)S(1)} collective-permute-done((f32[39,16,128]{2,1,0:T(8,128)}, f32[39,16,128]{2,1,0:T(8,128)S(1)}, u32[]{:S(2)}, u32[]{:S(2)}) %collective-permute-start.1) | collective-permute-done | bytes 319520 | tf_op jit(solution)/shard_map/ppermute | solution.py:35
  26.8 10.2 %pack.1 = (f32[408,640]{1,0:T(8,128)}, f32[1672,128]{1,0:T(8,128)}) custom-call(s32[3]{0:T(128)S(1)} %add_convert_fusion.flags, f32[36,512,128]{2,1,0:T(8,128)} %bitcast.11, f32[2,512,128]{2,1,0:T(8,128)} %motion.5, f32[512,128]{1,0:T(8,128)} %fictive.5, f32[39,16,128]{2,1,0:T(8,128)S(1)} %collective-permute-done.up, ...), custom_call_target="tpu_custom_call" | custom-call | tf_op jit(solution)/shard_map/pack/pallas_call | solution.py:173
  37.0 4.6 %collective-permute-start.4 = (f32[1672,128]{1,0:T(8,128)}, f32[1672,128]{1,0:T(8,128)}, u32[]{:S(2)}, u32[]{:S(2)}) collective-permute-start(f32[1672,128]{1,0:T(8,128)} %get-tuple-element.32), channel_id=1, source_target_pairs={{0,1},{1,2},{2,3},{3,4},{4,5},{5,6},{6,7},{7,8},{8,9},{9,10},{10,1... | collective-permute-start | bytes 2568200 | tf_op jit(solution)/shard_map/ppermute | solution.py:35
  41.6 24.8 %all-to-all-done.heat = f32[16,11,32,128]{3,2,1,0:T(8,128)S(1)} async-done(((f32[16,11,32,128]{3,2,1,0:T(8,128)}), f32[16,11,32,128]{3,2,1,0:T(8,128)S(1)}, u32[]{:S(2)}, u32[]{:S(2)}) %all-to-all-start) | async-done | bytes 2883616 | tf_op jit(solution)/shard_map/all_to_all | solution.py:572
  66.5 0.0 copy-start.2
  66.5 1.4 %collective-permute-start.3 = (f32[11,16,128]{2,1,0:T(8,128)S(1)}, f32[11,16,128]{2,1,0:T(8,128)S(1)}, u32[]{:S(2)}, u32[]{:S(2)}) collective-permute-start(f32[11,16,128]{2,1,0:T(8,128)S(1)} %get-tuple-element.49), channel_id=1, source_target_pairs={{16,0},{32,16},{48,32},{64,48},{80,64},{96,80},{112,96},{17,1},{33... | collective-permute-start | bytes 270344 | tf_op jit(solution)/shard_map/ppermute | solution.py:35
  67.9 4.0 %collective-permute-start.2 = (f32[11,16,128]{2,1,0:T(8,128)S(1)}, f32[11,16,128]{2,1,0:T(8,128)S(1)}, u32[]{:S(2)}, u32[]{:S(2)}) collective-permute-start(f32[11,16,128]{2,1,0:T(8,128)S(1)} %get-tuple-element.50), channel_id=1, source_target_pairs={{0,16},{16,32},{32,48},{48,64},{64,80},{80,96},{96,112},{1,17},{17... | collective-permute-start | bytes 270344 | tf_op jit(solution)/shard_map/ppermute | solution.py:35
  72.0 0.8 ready.1
  72.8 0.0 copy-start.1
  72.8 5.5 %collective-permute-done.4.got = f32[1672,128]{1,0:T(8,128)} collective-permute-done((f32[1672,128]{1,0:T(8,128)}, f32[1672,128]{1,0:T(8,128)}, u32[]{:S(2)}, u32[]{:S(2)}) %collective-permute-start.4) | collective-permute-done | bytes 856096 | tf_op jit(solution)/shard_map/ppermute | solution.py:35
  78.3 0.0 copy-done.2
  78.3 1.5 %lay.1 = (f32[36,24,640]{2,1,0:T(8,128)S(1)}, f32[2,24,640]{2,1,0:T(8,128)S(1)}, f32[24,640]{1,0:T(8,128)S(1)}) custom-call(s32[3]{0:T(128)S(1)} %add_convert_fusion.flags, f32[408,640]{1,0:T(8,128)S(1)} %copy-done.2, f32[1672,128]{1,0:T(8,128)} %collective-permute-done.4.got), custom_call_target="tpu_custom_call" | custom-call | bytes 6000000 | tf_op jit(solution)/shard_map/lay/pallas_call | solution.py:260
  79.8 0.0 collective-permute-done.3.heat_down
  79.8 0.0 collective-permute-done.2.heat_up
  79.8 0.0 copy-start
  79.8 5.8 %strip.1 = (f32[32,640]{1,0:T(8,128)S(1)}, f32[36,24,640]{2,1,0:T(8,128)S(1)}) custom-call(s32[3]{0:T(128)S(1)} %add_convert_fusion.flags, f32[25]{0:T(128)S(1)} %pad_maximum_fusion.coef, f32[36,24,640]{2,1,0:T(8,128)S(1)} %get-tuple-element.35.z_in, f32[2,24,640]{2,1,0:T(8,128)S(1)} %get-tuple-element.36.v_in, ...), custom_call_target="tpu_custom_call", output_to_operand_aliasing={{1}: (2, {})} | custom-call | bytes 21000000 | tf_op jit(solution)/shard_map/strip/pallas_call | solution.py:340
  85.6 2.9 %collective-permute-start.5 = (f32[32,640]{1,0:T(8,128)S(1)}, f32[32,640]{1,0:T(8,128)S(1)}, u32[]{:S(2)}, u32[]{:S(2)}) collective-permute-start(f32[32,640]{1,0:T(8,128)S(1)} %get-tuple-element.40.nodes), channel_id=1, source_target_pairs={{1,0},{2,1},{3,2},{4,3},{5,4},{6,5},{7,6},{8,7},{9,8},{10,9},{11,1... | collective-permute-start | bytes 245768 | tf_op jit(solution)/shard_map/ppermute | solution.py:35
  88.5 0.0 copy-done.1
  88.5 4.5 %edges.1 = (f32[10,552,128]{2,1,0:T(8,128)S(1)}, f32[10,552,128]{2,1,0:T(8,128)S(1)}, f32[512,128]{1,0:T(8,128)}, f32[10,2,544,128]{3,2,1,0:T(8,128)S(1)}) custom-call(s32[3]{0:T(128)S(1)} %add_convert_fusion.flags, f32[16,11,32,128]{3,2,1,0:T(8,128)S(1)} %all-to-all-done.heat, f32[512,128]{1,0:T(8,128)S(1)} %copy-done.1, ...), custom_call_target="tpu_custom_call" | custom-call | bytes 18000000 | tf_op jit(solution)/shard_map/edges/pallas_call | solution.py:395
  93.0 0.0 collective-permute-done.5.beside_t
  93.0 0.0 copy-done
  93.0 28.5 %block.1 = (f32[2,512,128]{2,1,0:T(8,128)}, f32[36,512,128]{2,1,0:T(8,128)}) custom-call(s32[3]{0:T(128)S(1)} %add_convert_fusion.flags, f32[25]{0:T(128)S(1)} %pad_maximum_fusion.coef, f32[36,512,128]{2,1,0:T(8,128)} %bitcast.12, f32[2,512,128]{2,1,0:T(8,128)S(1)} %copy-done, f32[39,16,128]{2,1,0:T(8,128)S(1)} %collective-permute-done.up, ...), custom_call_target="tpu_custom_call" | custom-call | bytes 84000000 | tf_op jit(solution)/shard_map/block/pallas_call | solution.py:539
  (1 shorter events, 0.0 us)
Async XLA Ops:
  4.6 13.1 %copy-start.3 = (f32[12]{0:T(128)S(1)}, f32[12]{0:T(128)}, u32[]{:S(2)}) copy-start(f32[12]{0:T(128)} %param.10) | copy-start | bytes 148
  4.6 13.1 %copy-start.4 = (f32[12]{0:T(128)S(1)}, f32[12]{0:T(128)}, u32[]{:S(2)}) copy-start(f32[12]{0:T(128)} %param.11) | copy-start | bytes 148
  4.6 61.8 %all-to-all-start = ((f32[16,11,32,128]{3,2,1,0:T(8,128)}), f32[16,11,32,128]{3,2,1,0:T(8,128)S(1)}, u32[]{:S(2)}, u32[]{:S(2)}) async-start(f32[16,11,32,128]{3,2,1,0:T(8,128)} %get-tuple-element.25), calls=%async_computation | async-start | bytes 5767168 | tf_op jit(solution)/shard_map/all_to_all | solution.py:572
  13.1 10.1 %collective-permute-start = (f32[39,16,128]{2,1,0:T(8,128)}, f32[39,16,128]{2,1,0:T(8,128)S(1)}, u32[]{:S(2)}, u32[]{:S(2)}) collective-permute-start(f32[39,16,128]{2,1,0:T(8,128)} %get-tuple-element.26), channel_id=1, source_target_pairs={{0,16},{16,32},{32,48},{48,64},{64,80},{80,96},{96,112},{1,17},{17... | collective-permute-start | bytes 958472 | tf_op jit(solution)/shard_map/ppermute | solution.py:35
  16.3 10.5 %collective-permute-start.1 = (f32[39,16,128]{2,1,0:T(8,128)}, f32[39,16,128]{2,1,0:T(8,128)S(1)}, u32[]{:S(2)}, u32[]{:S(2)}) collective-permute-start(f32[39,16,128]{2,1,0:T(8,128)} %get-tuple-element.27), channel_id=1, source_target_pairs={{16,0},{32,16},{48,32},{64,48},{80,64},{96,80},{112,96},{17,1},{33... | collective-permute-start | bytes 958472 | tf_op jit(solution)/shard_map/ppermute | solution.py:35
  37.0 41.3 %collective-permute-start.4 = (f32[1672,128]{1,0:T(8,128)}, f32[1672,128]{1,0:T(8,128)}, u32[]{:S(2)}, u32[]{:S(2)}) collective-permute-start(f32[1672,128]{1,0:T(8,128)} %get-tuple-element.32), channel_id=1, source_target_pairs={{0,1},{1,2},{2,3},{3,4},{4,5},{5,6},{6,7},{7,8},{8,9},{9,10},{10,1... | collective-permute-start | bytes 2568200 | tf_op jit(solution)/shard_map/ppermute | solution.py:35
  66.5 11.8 %copy-start.2 = (f32[408,640]{1,0:T(8,128)S(1)}, f32[408,640]{1,0:T(8,128)}, u32[]{:S(2)}) copy-start(f32[408,640]{1,0:T(8,128)} %get-tuple-element.31.first) | copy-start | bytes 3133444
  66.5 13.3 %collective-permute-start.3 = (f32[11,16,128]{2,1,0:T(8,128)S(1)}, f32[11,16,128]{2,1,0:T(8,128)S(1)}, u32[]{:S(2)}, u32[]{:S(2)}) collective-permute-start(f32[11,16,128]{2,1,0:T(8,128)S(1)} %get-tuple-element.49), channel_id=1, source_target_pairs={{16,0},{32,16},{48,32},{64,48},{80,64},{96,80},{112,96},{17,1},{33... | collective-permute-start | bytes 270344 | tf_op jit(solution)/shard_map/ppermute | solution.py:35
  67.9 11.9 %collective-permute-start.2 = (f32[11,16,128]{2,1,0:T(8,128)S(1)}, f32[11,16,128]{2,1,0:T(8,128)S(1)}, u32[]{:S(2)}, u32[]{:S(2)}) collective-permute-start(f32[11,16,128]{2,1,0:T(8,128)S(1)} %get-tuple-element.50), channel_id=1, source_target_pairs={{0,16},{16,32},{32,48},{48,64},{64,80},{80,96},{96,112},{1,17},{17... | collective-permute-start | bytes 270344 | tf_op jit(solution)/shard_map/ppermute | solution.py:35
  72.8 15.7 %copy-start.1 = (f32[512,128]{1,0:T(8,128)S(1)}, f32[512,128]{1,0:T(8,128)}, u32[]{:S(2)}) copy-start(f32[512,128]{1,0:T(8,128)} %fictive.5) | copy-start | bytes 786436
  79.8 13.2 %copy-start = (f32[2,512,128]{2,1,0:T(8,128)S(1)}, f32[2,512,128]{2,1,0:T(8,128)}, u32[]{:S(2)}) copy-start(f32[2,512,128]{2,1,0:T(8,128)} %motion.5) | copy-start | bytes 1572868
  85.6 7.4 %collective-permute-start.5 = (f32[32,640]{1,0:T(8,128)S(1)}, f32[32,640]{1,0:T(8,128)S(1)}, u32[]{:S(2)}, u32[]{:S(2)}) collective-permute-start(f32[32,640]{1,0:T(8,128)S(1)} %get-tuple-element.40.nodes), channel_id=1, source_target_pairs={{1,0},{2,1},{3,2},{4,3},{5,4},{6,5},{7,6},{8,7},{9,8},{10,9},{11,1... | collective-permute-start | bytes 245768 | tf_op jit(solution)/shard_map/ppermute | solution.py:35

commit v4 on v3

--- a/solution.py
+++ b/solution.py
@@ -232,18 +232,10 @@
     )(heat)
 
 
-def lay_body(flags, first, got, z, v, fict, got_halo):
-    rest = SUBS - 2 * DEEP
+def lay_body(flags, got, z_in, v_in, fict_in, z, v, fict, got_halo):
     lane = iota((416, COLS), 1)
     blank = jnp.where((iota((416, COLS), 0) >= 380) & (iota((416, COLS), 0) < 390), 1.0, 0.0)
     got_halo[...] = jnp.where((lane < HALO) | (lane >= COLS - HALO), spread(got[4 * EDGE:, :]), blank)
-    for k in range(36):
-        z[k, DEEP:2 * DEEP, :] = first[DEEP * k:DEEP * k + DEEP, :]
-        z[k, 2 * DEEP:SUBS, :] = jnp.zeros((rest, LANES), F32)
-    for k in range(2):
-        v[k, DEEP:SUBS, :] = first[360 + 16 * k:360 + 16 * k + SUBS - DEEP, :]
-    fict[DEEP:2 * DEEP, :] = first[392:402, :]
-    fict[2 * DEEP:SUBS, :] = jnp.ones((rest, LANES), F32)
     for i in range(5):
         lanes = slice(i * COLS, (i + 1) * COLS)
         left = got_halo if i == 4 else got.at[pl.ds(EDGE * i, EDGE)]
@@ -254,27 +246,41 @@
         fict[0:DEEP, lanes] = jnp.where(flags[2] == 1, OUTSIDE, left[380:390, :])
 
 
-def lay(flags, first, got):
+def lay(flags, got, z, v, fict):
     full = pl.BlockSpec(memory_space=VMEM)
     shapes = [(36, SUBS, LANES), (2, SUBS, LANES), (SUBS, LANES)]
     return pl.pallas_call(
         lay_body,
         out_shape=[jax.ShapeDtypeStruct(s, F32) for s in shapes],
-        in_specs=[pl.BlockSpec(memory_space=SMEM)] + [full] * 2,
+        in_specs=[pl.BlockSpec(memory_space=SMEM)] + [full] * 4,
         out_specs=[full] * 3,
+        input_output_aliases={2: 0, 3: 1, 4: 2},
         scratch_shapes=[VMEM((416, COLS), F32)],
         compiler_params=params(8),
         cost_estimate=work(2),
         name="lay",
-    )(flags, first, got)
-
-
-def strip_body(flags, coef, z_in, v_in, fict_in, mine, side, heat_up, heat_down, nodes, z, v, q, heat_t):
+    )(flags, got, z, v, fict)
+
+
+def prepare_body(flags, first, heat, fictive, up, down, heat_up, heat_down, mine, side, inv_ref, half_ref, f_out, heat_t, z, v, fict_t):
     rest = SUBS - 2 * DEEP
-    v[...] = v_in[...]
-    q[...] = jnp.zeros((3, SUBS, LANES), F32)
-
     top, bottom = flags[0] == 1, flags[1] == 1
+    for s in range(0, PIECES, 8):
+        at, to = slice(32 * s, 32 * s + 256), slice(32 * s + HALO, 32 * s + HALO + 256)
+        own = fictive[at, :]
+        for n in range(TICKS):
+            inv_ref[n, to, :], half_ref[n, to, :], own = advance(heat[s:s + 8, n].reshape(256, COLS), own)
+        f_out[at, :] = own
+    fict = jnp.concatenate([jnp.where(top, OUTSIDE, up[38]), jnp.where(bottom, OUTSIDE, down[38])], axis=0)
+    for n in range(TICKS):
+        theta = jnp.concatenate([jnp.where(top, OUTSIDE, heat_up[n]), jnp.where(bottom, OUTSIDE, heat_down[n])], axis=0)
+        inv, half, fict = advance(theta, fict)
+        inv_ref[n, 0:HALO, :] = inv[:HALO]
+        half_ref[n, 0:HALO, :] = half[:HALO]
+        inv_ref[n, HALO + ROWS:EXT, :] = inv[HALO:]
+        half_ref[n, HALO + ROWS:EXT, :] = half[HALO:]
+        inv_ref[n, EXT:EXT + PAD, :] = jnp.ones((PAD, COLS), F32)
+        half_ref[n, EXT:EXT + PAD, :] = jnp.ones((PAD, COLS), F32)
     last_side = corner(jnp.where(top, OUTSIDE, heat_up[TICKS]), jnp.where(bottom, OUTSIDE, heat_down[TICKS]), 1.0)
     last_mine = corner(beside_each_other(lambda n: jnp.where(top, OUTSIDE, heat_up[n]), HALO),
                        beside_each_other(lambda n: jnp.where(bottom, OUTSIDE, heat_down[n]), HALO), 1.0)
@@ -285,7 +291,35 @@
         heat_t[n, DEEP:2 * DEEP, 0:ROWS] = mine[cols, :]
         heat_t[n, DEEP:2 * DEEP, ROWS:LANES] = last_mine[cols]
         heat_t[n, 2 * DEEP:SUBS, :] = jnp.ones((rest, LANES), F32)
-
+    for k in range(36):
+        z[k, DEEP:2 * DEEP, :] = first[DEEP * k:DEEP * k + DEEP, :]
+        z[k, 2 * DEEP:SUBS, :] = jnp.zeros((rest, LANES), F32)
+    for k in range(2):
+        v[k, DEEP:SUBS, :] = first[360 + 16 * k:360 + 16 * k + SUBS - DEEP, :]
+    fict_t[DEEP:2 * DEEP, :] = first[392:402, :]
+    fict_t[2 * DEEP:SUBS, :] = jnp.ones((rest, LANES), F32)
+
+
+def prepare(flags, first, heat, fictive, up, down, heat_up, heat_down, mine, side):
+    full = pl.BlockSpec(memory_space=VMEM)
+    factor = (TICKS, EXT + PAD, COLS)
+    shapes = [factor, factor, (ROWS, COLS), (TICKS, SUBS, LANES), (36, SUBS, LANES), (2, SUBS, LANES), (SUBS, LANES)]
+    return pl.pallas_call(
+        prepare_body,
+        out_shape=[jax.ShapeDtypeStruct(s, F32) for s in shapes],
+        in_specs=[pl.BlockSpec(memory_space=SMEM)] + [full] * 9,
+        out_specs=[full] * 7,
+        compiler_params=params(8),
+        cost_estimate=work(5),
+        name="prepare",
+    )(flags, first, heat, fictive, up, down, heat_up, heat_down, mine, side)
+
+
+def strip_body(flags, coef, z_in, v_in, fict_in, heat_t, nodes, z, v, q):
+    v[...] = v_in[...]
+    q[...] = jnp.zeros((3, SUBS, LANES), F32)
+
+    bottom = flags[1] == 1
     inside = jnp.where(bottom & (iota((8, LANES), 1) >= ROWS) & (iota((8, LANES), 1) < LANES - HALO), 0.0, 1.0)
     sum_a = coef[24]
     nodes[...] = jnp.zeros((32, LANES), F32)
@@ -334,24 +368,23 @@
     lax.fori_loop(8, TICKS, lambda n, f: tick(n, f, 8, 16), fict[8:16])
 
 
-def strip(flags, coef, z, v, fict, mine, side, heat_up, heat_down):
+def strip(flags, coef, z, v, fict, heat_t):
     full = pl.BlockSpec(memory_space=VMEM)
     smem = pl.BlockSpec(memory_space=SMEM)
     return pl.pallas_call(
         strip_body,
         out_shape=[jax.ShapeDtypeStruct((32, LANES), F32), jax.ShapeDtypeStruct((36, SUBS, LANES), F32)],
-        in_specs=[smem, smem] + [full] * 7,
+        in_specs=[smem, smem] + [full] * 4,
         out_specs=[full, full],
         input_output_aliases={2: 1},
         scratch_shapes=[
             VMEM((2, SUBS, LANES), F32),
             VMEM((3, SUBS, LANES), F32),
-            VMEM((TICKS, SUBS, LANES), F32),
         ],
-        compiler_params=params(16),
+        compiler_params=params(8),
         cost_estimate=work(7),
         name="strip",
-    )(flags, coef, z, v, fict, mine, side, heat_up, heat_down)[0]
+    )(flags, coef, z, v, fict, heat_t)[0]
 
 
 def upright(nodes, i):
@@ -359,24 +392,7 @@
     return jnp.concatenate([part[:24], jnp.zeros((COLS - 32, COLS), F32), part[24:]], axis=0).T
 
 
-def edges_body(flags, heat, fictive, up, down, heat_up, heat_down, nodes, inv_ref, half_ref, f_out, left):
-    for s in range(0, PIECES, 8):
-        at, to = slice(32 * s, 32 * s + 256), slice(32 * s + HALO, 32 * s + HALO + 256)
-        own = fictive[at, :]
-        for n in range(TICKS):
-            inv_ref[n, to, :], half_ref[n, to, :], own = advance(heat[s:s + 8, n].reshape(256, COLS), own)
-        f_out[at, :] = own
-    top, bottom = flags[0] == 1, flags[1] == 1
-    fict = jnp.concatenate([jnp.where(top, OUTSIDE, up[38]), jnp.where(bottom, OUTSIDE, down[38])], axis=0)
-    for n in range(TICKS):
-        theta = jnp.concatenate([jnp.where(top, OUTSIDE, heat_up[n]), jnp.where(bottom, OUTSIDE, heat_down[n])], axis=0)
-        inv, half, fict = advance(theta, fict)
-        inv_ref[n, 0:HALO, :] = inv[:HALO]
-        half_ref[n, 0:HALO, :] = half[:HALO]
-        inv_ref[n, HALO + ROWS:EXT, :] = inv[HALO:]
-        half_ref[n, HALO + ROWS:EXT, :] = half[HALO:]
-        inv_ref[n, EXT:EXT + PAD, :] = jnp.ones((PAD, COLS), F32)
-        half_ref[n, EXT:EXT + PAD, :] = jnp.ones((PAD, COLS), F32)
+def edges_body(nodes, left):
     for i in range(5):
         part = upright(nodes, i)
         for n in range(TICKS):
@@ -389,18 +405,17 @@
                     left[n, c, 0:HALO, :] = moved[COLS - HALO:]
 
 
-def edges(flags, heat, fictive, up, down, heat_up, heat_down, nodes):
+def edges(nodes):
     full = pl.BlockSpec(memory_space=VMEM)
-    factor = jax.ShapeDtypeStruct((TICKS, EXT + PAD, COLS), F32)
     return pl.pallas_call(
         edges_body,
-        out_shape=[factor, factor, jax.ShapeDtypeStruct((ROWS, COLS), F32), jax.ShapeDtypeStruct((TICKS, 2, EXT, COLS), F32)],
-        in_specs=[pl.BlockSpec(memory_space=SMEM)] + [full] * 7,
-        out_specs=[full] * 4,
-        compiler_params=params(12),
-        cost_estimate=work(6),
+        out_shape=jax.ShapeDtypeStruct((TICKS, 2, EXT, COLS), F32),
+        in_specs=[full],
+        out_specs=full,
+        compiler_params=params(8),
+        cost_estimate=work(3),
         name="edges",
-    )(flags, heat, fictive, up, down, heat_up, heat_down, nodes)
+    )(nodes)
 
 
 def block_body(flags, coef, state, motion, up, down, inv_ref, half_ref, left, beside_t, v_out, s_out, z, v, q, h, pairs, forces, zh, sem, in_sem):
@@ -578,11 +593,11 @@
     heat_up = shifted(heat[PIECES - 1, :, HALO:, :], "draw", 1)
     heat_down = shifted(heat[0, :, :HALO, :], "draw", -1)
     mine, side = ready(heat)
-    got, mine = lax.optimization_barrier((got, mine))
-    strip_state = lay(flags, first, got)
-    nodes = strip(flags, coef, *strip_state, mine, side, heat_up, heat_down)
+    inv, half, fict, heat_t, z, v, fict_t = prepare(flags, first, heat, fictitious_warmth, up, down, heat_up, heat_down, mine, side)
+    got, fict_t = lax.optimization_barrier((got, fict_t))
+    nodes = strip(flags, coef, *lay(flags, got, z, v, fict_t), heat_t)
     beside = shifted(nodes, WIDE, -1)
-    inv, half, fict, left = edges(flags, heat, fictitious_warmth, up, down, heat_up, heat_down, nodes)
+    left = edges(nodes)
     motion, modes = block(flags, coef, state, vertex_velocity, up, down, inv, half, left, beside)
     return fict, motion, modes.reshape(branch_load_tensors.shape)
 

time: 124 us -> 125 us (level)
  the two profiles are of different devices: /device:TPU:5 before, /device:TPU:37 now
where the time goes in v4:
time: 125 us; the launch traced here: 124 us
  Pallas kernels  55.7 us (45%)
  waiting for transfers between devices  37.4 us (30%)
  starting transfers between devices  28.9 us (23%)
  other arithmetic  1.4 us (1%)
    pallas_call x1, Pallas kernels, block(): pl.pallas_call(block_body, out_shape=[jax.ShapeDtypeStruct((2, ROWS, COLS...  28.5 us
    all_to_all x1, waiting for transfers between devices, shards(): heat = lax.all_to_all(slab, WIDE, split_axis=0, concat_axis=0, tiled=True)  24.5 us
    ppermute x6, starting transfers between devices, shifted(): return lax.ppermute(shard, axis, pairs)  21.4 us
    ppermute x6, waiting for transfers between devices, shifted(): return lax.ppermute(shard, axis, pairs)  13 us
    pallas_call x1, Pallas kernels, pack(): pl.pallas_call(pack_body, out_shape=[pltpu.HBM((408, LANES), F32), jax.Sh...  10.2 us
    all_to_all x1, starting transfers between devices, shards(): heat = lax.all_to_all(slab, WIDE, split_axis=0, concat_axis=0, tiled=True)  7.56 us
    pallas_call x1, Pallas kernels, strip(): pl.pallas_call(strip_body, out_shape=[jax.ShapeDtypeStruct((32, LANES), F...  5.63 us
    pallas_call x1, Pallas kernels, cut(): pl.pallas_call(cut_body, out_shape=[pltpu.HBM((PIECES, TICKS + 1, 32, COL...  3.96 us
  transfers between devices with their start and end apart: 7, of which 5 were waited for; matrix products, arithmetic and copies ran while one was open for 1% of the time, Pallas kernels for 13%

profile of v4, /device:TPU:37, one launch (start us, length us, event | category | flops | bytes accessed | tf_op | source)
XLA Modules:
  0.0 124.4 jit_solution(7727561765815863421)
XLA Ops:
  0.6 4.0 %cut.1 = (f32[16,11,32,128]{3,2,1,0:T(8,128)}, f32[39,16,128]{2,1,0:T(8,128)}, f32[39,16,128]{2,1,0:T(8,128)}) custom-call(f32[10,32,2048]{2,1,0:T(8,128)} %src.1, f32[36,512,128]{2,1,0:T(8,128)} %bitcast.10, f32[2,512,128]{2,1,0:T(8,128)} %motion.5, f32[512,128]{1,0:T(8,128)} %fictive.5), custom_call_target="tpu_custom_call" | custom-call | tf_op jit(solution)/shard_map/cut/pallas_call | solution.py:98
  4.6 0.0 copy-start.3
  4.6 0.0 copy-start.4
  4.6 7.6 %all-to-all-start = ((f32[16,11,32,128]{3,2,1,0:T(8,128)}), f32[16,11,32,128]{3,2,1,0:T(8,128)S(1)}, u32[]{:S(2)}, u32[]{:S(2)}) async-start(f32[16,11,32,128]{3,2,1,0:T(8,128)} %get-tuple-element.33), calls=%async_computation | async-start | bytes 5767168 | tf_op jit(solution)/shard_map/all_to_all | solution.py:587
  12.2 3.2 %collective-permute-start = (f32[39,16,128]{2,1,0:T(8,128)}, f32[39,16,128]{2,1,0:T(8,128)S(1)}, u32[]{:S(2)}, u32[]{:S(2)}) collective-permute-start(f32[39,16,128]{2,1,0:T(8,128)} %get-tuple-element.28), channel_id=1, source_target_pairs={{0,16},{16,32},{32,48},{48,64},{64,80},{80,96},{96,112},{1,17},{17... | collective-permute-start | bytes 958472 | tf_op jit(solution)/shard_map/ppermute | solution.py:35
  15.4 4.2 %collective-permute-start.1 = (f32[39,16,128]{2,1,0:T(8,128)}, f32[39,16,128]{2,1,0:T(8,128)S(1)}, u32[]{:S(2)}, u32[]{:S(2)}) collective-permute-start(f32[39,16,128]{2,1,0:T(8,128)} %get-tuple-element.29), channel_id=1, source_target_pairs={{16,0},{32,16},{48,32},{64,48},{80,64},{96,80},{112,96},{17,1},{33... | collective-permute-start | bytes 958472 | tf_op jit(solution)/shard_map/ppermute | solution.py:35
  19.6 0.1 add_convert_fusion.flags
  19.7 0.0 copy-done.3
  19.7 0.0 copy-done.4
  19.7 0.6 fusion
  20.3 0.7 pad_maximum_fusion.coef
  21.0 5.0 %collective-permute-done.up = f32[39,16,128]{2,1,0:T(8,128)S(1)} collective-permute-done((f32[39,16,128]{2,1,0:T(8,128)}, f32[39,16,128]{2,1,0:T(8,128)S(1)}, u32[]{:S(2)}, u32[]{:S(2)}) %collective-permute-start) | collective-permute-done | bytes 319520 | tf_op jit(solution)/shard_map/ppermute | solution.py:35
  26.0 0.4 collective-permute-done.1.down
  26.4 10.2 %pack.1 = (f32[408,640]{1,0:T(8,128)}, f32[1672,128]{1,0:T(8,128)}) custom-call(s32[3]{0:T(128)S(1)} %add_convert_fusion.flags, f32[36,512,128]{2,1,0:T(8,128)} %bitcast.11, f32[2,512,128]{2,1,0:T(8,128)} %motion.5, f32[512,128]{1,0:T(8,128)} %fictive.5, f32[39,16,128]{2,1,0:T(8,128)S(1)} %collective-permute-done.up, ...), custom_call_target="tpu_custom_call" | custom-call | tf_op jit(solution)/shard_map/pack/pallas_call | solution.py:173
  36.6 4.7 %collective-permute-start.4 = (f32[1672,128]{1,0:T(8,128)}, f32[1672,128]{1,0:T(8,128)}, u32[]{:S(2)}, u32[]{:S(2)}) collective-permute-start(f32[1672,128]{1,0:T(8,128)} %get-tuple-element.40), channel_id=1, source_target_pairs={{0,1},{1,2},{2,3},{3,4},{4,5},{5,6},{6,7},{7,8},{8,9},{9,10},{10,1... | collective-permute-start | bytes 2568200 | tf_op jit(solution)/shard_map/ppermute | solution.py:35
  41.3 24.5 %all-to-all-done.heat = f32[16,11,32,128]{3,2,1,0:T(8,128)S(1)} async-done(((f32[16,11,32,128]{3,2,1,0:T(8,128)}), f32[16,11,32,128]{3,2,1,0:T(8,128)S(1)}, u32[]{:S(2)}, u32[]{:S(2)}) %all-to-all-start) | async-done | bytes 2883616 | tf_op jit(solution)/shard_map/all_to_all | solution.py:587
  65.8 0.0 copy-start.1
  65.8 0.0 copy-start.2
  65.8 5.1 %collective-permute-start.3 = (f32[11,16,128]{2,1,0:T(8,128)S(1)}, f32[11,16,128]{2,1,0:T(8,128)S(1)}, u32[]{:S(2)}, u32[]{:S(2)}) collective-permute-start(f32[11,16,128]{2,1,0:T(8,128)S(1)} %get-tuple-element.55), channel_id=1, source_target_pairs={{16,0},{32,16},{48,32},{64,48},{80,64},{96,80},{112,96},{17,1},{33... | collective-permute-start | bytes 270344 | tf_op jit(solution)/shard_map/ppermute | solution.py:35
  70.9 1.9 %collective-permute-start.2 = (f32[11,16,128]{2,1,0:T(8,128)S(1)}, f32[11,16,128]{2,1,0:T(8,128)S(1)}, u32[]{:S(2)}, u32[]{:S(2)}) collective-permute-start(f32[11,16,128]{2,1,0:T(8,128)S(1)} %get-tuple-element.56), channel_id=1, source_target_pairs={{0,16},{16,32},{32,48},{48,64},{64,80},{80,96},{96,112},{1,17},{17... | collective-permute-start | bytes 270344 | tf_op jit(solution)/shard_map/ppermute | solution.py:35
  72.8 0.8 ready.1
  73.7 0.0 collective-permute-done.3.heat_down
  73.7 4.6 %collective-permute-done.2.heat_up = f32[11,16,128]{2,1,0:T(8,128)S(1)} collective-permute-done((f32[11,16,128]{2,1,0:T(8,128)S(1)}, f32[11,16,128]{2,1,0:T(8,128)S(1)}, u32[]{:S(2)}, u32[]{:S(2)}) %collective-permute-start.2) | collective-permute-done | bytes 90144 | tf_op jit(solution)/shard_map/ppermute | solution.py:35
  78.3 0.0 copy-done.1
  78.3 0.0 copy-done.2
  78.3 3.7 %prepare.1 = (f32[10,552,128]{2,1,0:T(8,128)S(1)}, f32[10,552,128]{2,1,0:T(8,128)S(1)}, f32[512,128]{1,0:T(8,128)}, f32[10,24,640]{2,1,0:T(8,128)S(1)}, f32[36,2...) custom-call(s32[3]{0:T(128)S(1)} %add_convert_fusion.flags, f32[408,640]{1,0:T(8,128)S(1)} %copy-done.2, ...), custom_call_target="tpu_custom_call" | custom-call | bytes 15000000 | tf_op jit(solution)/shard_map/prepare/pallas_call | solution.py:307
  82.0 0.0 collective-permute-done.4.got
  82.0 1.3 %lay.1 = (f32[36,24,640]{2,1,0:T(8,128)S(1)}, f32[2,24,640]{2,1,0:T(8,128)S(1)}, f32[24,640]{1,0:T(8,128)S(1)}) custom-call(s32[3]{0:T(128)S(1)} %add_convert_fusion.flags, f32[1672,128]{1,0:T(8,128)} %collective-permute-done.4.got, f32[36,24,640]{2,1,0:T(8,128)S(1)} %get-tuple-element.43.z_in, ...), custom_call_target="tpu_custom_call", output_to_operand_aliasing={{0}: (2, {}), {1}: (3, {}), {2}: (4, {})} | custom-call | bytes 6000000 | tf_op jit(solution)/shard_map/lay/pallas_call | solution.py:252
  83.3 5.6 %strip.1 = (f32[32,640]{1,0:T(8,128)S(1)}, f32[36,24,640]{2,1,0:T(8,128)S(1)}) custom-call(s32[3]{0:T(128)S(1)} %add_convert_fusion.flags, f32[25]{0:T(128)S(1)} %pad_maximum_fusion.coef, f32[36,24,640]{2,1,0:T(8,128)S(1)} %get-tuple-element.46.z_in, f32[2,24,640]{2,1,0:T(8,128)S(1)} %get-tuple-element.47.v_in, ...), custom_call_target="tpu_custom_call", output_to_operand_aliasing={{1}: (2, {})} | custom-call | bytes 21000000 | tf_op jit(solution)/shard_map/strip/pallas_call | solution.py:374
  88.9 0.0 copy-start
  89.0 2.2 %collective-permute-start.5 = (f32[32,640]{1,0:T(8,128)S(1)}, f32[32,640]{1,0:T(8,128)S(1)}, u32[]{:S(2)}, u32[]{:S(2)}) collective-permute-start(f32[32,640]{1,0:T(8,128)S(1)} %get-tuple-element.50.nodes), channel_id=1, source_target_pairs={{1,0},{2,1},{3,2},{4,3},{5,4},{6,5},{7,6},{8,7},{9,8},{10,9},{11,1... | collective-permute-start | bytes 245768 | tf_op jit(solution)/shard_map/ppermute | solution.py:35
  91.2 1.6 %edges.1.left = f32[10,2,544,128]{3,2,1,0:T(8,128)S(1)} custom-call(f32[32,640]{1,0:T(8,128)S(1)} %get-tuple-element.50.nodes), custom_call_target="tpu_custom_call" | custom-call | bytes 9000000 | tf_op jit(solution)/shard_map/edges/pallas_call | solution.py:410
  92.8 3.0 %collective-permute-done.5.beside_t = f32[32,640]{1,0:T(8,128)S(1)} collective-permute-done((f32[32,640]{1,0:T(8,128)S(1)}, f32[32,640]{1,0:T(8,128)S(1)}, u32[]{:S(2)}, u32[]{:S(2)}) %collective-permute-start.5) | collective-permute-done | bytes 81952 | tf_op jit(solution)/shard_map/ppermute | solution.py:35
  95.8 0.0 copy-done
  95.8 28.5 %block.1 = (f32[2,512,128]{2,1,0:T(8,128)}, f32[36,512,128]{2,1,0:T(8,128)}) custom-call(s32[3]{0:T(128)S(1)} %add_convert_fusion.flags, f32[25]{0:T(128)S(1)} %pad_maximum_fusion.coef, f32[36,512,128]{2,1,0:T(8,128)} %bitcast.12, f32[2,512,128]{2,1,0:T(8,128)S(1)} %copy-done, f32[39,16,128]{2,1,0:T(8,128)S(1)} %collective-permute-done.up, ...), custom_call_target="tpu_custom_call" | custom-call | bytes 84000000 | tf_op jit(solution)/shard_map/block/pallas_call | solution.py:554
  (1 shorter events, 0.0 us)
Async XLA Ops:
  4.6 15.1 %copy-start.3 = (f32[12]{0:T(128)S(1)}, f32[12]{0:T(128)}, u32[]{:S(2)}) copy-start(f32[12]{0:T(128)} %param.10) | copy-start | bytes 148
  4.6 15.1 %copy-start.4 = (f32[12]{0:T(128)S(1)}, f32[12]{0:T(128)}, u32[]{:S(2)}) copy-start(f32[12]{0:T(128)} %param.11) | copy-start | bytes 148
  4.6 61.1 %all-to-all-start = ((f32[16,11,32,128]{3,2,1,0:T(8,128)}), f32[16,11,32,128]{3,2,1,0:T(8,128)S(1)}, u32[]{:S(2)}, u32[]{:S(2)}) async-start(f32[16,11,32,128]{3,2,1,0:T(8,128)} %get-tuple-element.33), calls=%async_computation | async-start | bytes 5767168 | tf_op jit(solution)/shard_map/all_to_all | solution.py:587
  12.2 13.8 %collective-permute-start = (f32[39,16,128]{2,1,0:T(8,128)}, f32[39,16,128]{2,1,0:T(8,128)S(1)}, u32[]{:S(2)}, u32[]{:S(2)}) collective-permute-start(f32[39,16,128]{2,1,0:T(8,128)} %get-tuple-element.28), channel_id=1, source_target_pairs={{0,16},{16,32},{32,48},{48,64},{64,80},{80,96},{96,112},{1,17},{17... | collective-permute-start | bytes 958472 | tf_op jit(solution)/shard_map/ppermute | solution.py:35
  15.4 11.0 %collective-permute-start.1 = (f32[39,16,128]{2,1,0:T(8,128)}, f32[39,16,128]{2,1,0:T(8,128)S(1)}, u32[]{:S(2)}, u32[]{:S(2)}) collective-permute-start(f32[39,16,128]{2,1,0:T(8,128)} %get-tuple-element.29), channel_id=1, source_target_pairs={{16,0},{32,16},{48,32},{64,48},{80,64},{96,80},{112,96},{17,1},{33... | collective-permute-start | bytes 958472 | tf_op jit(solution)/shard_map/ppermute | solution.py:35
  36.6 45.4 %collective-permute-start.4 = (f32[1672,128]{1,0:T(8,128)}, f32[1672,128]{1,0:T(8,128)}, u32[]{:S(2)}, u32[]{:S(2)}) collective-permute-start(f32[1672,128]{1,0:T(8,128)} %get-tuple-element.40), channel_id=1, source_target_pairs={{0,1},{1,2},{2,3},{3,4},{4,5},{5,6},{6,7},{7,8},{8,9},{9,10},{10,1... | collective-permute-start | bytes 2568200 | tf_op jit(solution)/shard_map/ppermute | solution.py:35
  65.8 12.5 %copy-start.1 = (f32[512,128]{1,0:T(8,128)S(1)}, f32[512,128]{1,0:T(8,128)}, u32[]{:S(2)}) copy-start(f32[512,128]{1,0:T(8,128)} %fictive.5) | copy-start | bytes 786436
  65.8 12.5 %copy-start.2 = (f32[408,640]{1,0:T(8,128)S(1)}, f32[408,640]{1,0:T(8,128)}, u32[]{:S(2)}) copy-start(f32[408,640]{1,0:T(8,128)} %get-tuple-element.32.first) | copy-start | bytes 3133444
  65.8 7.9 %collective-permute-start.3 = (f32[11,16,128]{2,1,0:T(8,128)S(1)}, f32[11,16,128]{2,1,0:T(8,128)S(1)}, u32[]{:S(2)}, u32[]{:S(2)}) collective-permute-start(f32[11,16,128]{2,1,0:T(8,128)S(1)} %get-tuple-element.55), channel_id=1, source_target_pairs={{16,0},{32,16},{48,32},{64,48},{80,64},{96,80},{112,96},{17,1},{33... | collective-permute-start | bytes 270344 | tf_op jit(solution)/shard_map/ppermute | solution.py:35
  70.9 7.4 %collective-permute-start.2 = (f32[11,16,128]{2,1,0:T(8,128)S(1)}, f32[11,16,128]{2,1,0:T(8,128)S(1)}, u32[]{:S(2)}, u32[]{:S(2)}) collective-permute-start(f32[11,16,128]{2,1,0:T(8,128)S(1)} %get-tuple-element.56), channel_id=1, source_target_pairs={{0,16},{16,32},{32,48},{48,64},{64,80},{80,96},{96,112},{1,17},{17... | collective-permute-start | bytes 270344 | tf_op jit(solution)/shard_map/ppermute | solution.py:35
  88.9 6.8 %copy-start = (f32[2,512,128]{2,1,0:T(8,128)S(1)}, f32[2,512,128]{2,1,0:T(8,128)}, u32[]{:S(2)}) copy-start(f32[2,512,128]{2,1,0:T(8,128)} %motion.5) | copy-start | bytes 1572868
  89.0 6.8 %collective-permute-start.5 = (f32[32,640]{1,0:T(8,128)S(1)}, f32[32,640]{1,0:T(8,128)S(1)}, u32[]{:S(2)}, u32[]{:S(2)}) collective-permute-start(f32[32,640]{1,0:T(8,128)S(1)} %get-tuple-element.50.nodes), channel_id=1, source_target_pairs={{1,0},{2,1},{3,2},{4,3},{5,4},{6,5},{7,6},{8,7},{9,8},{10,9},{11,1... | collective-permute-start | bytes 245768 | tf_op jit(solution)/shard_map/ppermute | solution.py:35

commit v5 on v4

--- a/solution.py
+++ b/solution.py
@@ -125,7 +125,7 @@
 def pack_body(flags, state, motion, fictive, up, down, first_out, send, buf, tail, first, more, sem, more_sem):
     copies = [pltpu.make_async_copy(state.at[pl.ds(4 * i, 4)], buf.at[pl.ds(4 * i, 4)], sem.at[i]) for i in range(9)]
     rest = [pltpu.make_async_copy(motion, more.at[pl.ds(0, 2)], more_sem.at[0]), pltpu.make_async_copy(fictive, more.at[2], more_sem.at[1])]
-    for c in rest + copies:
+    for c in copies + rest:
         c.start()
 
     def put(at, blocks, corners, widths):
@@ -145,12 +145,12 @@
 
     f_up = jnp.where(flags[0] == 1, OUTSIDE, up[38])
     f_down = jnp.where(flags[1] == 1, OUTSIDE, down[38])
+    for i in range(9):
+        copies[i].wait()
+        put(40 * i, [buf[4 * i + j] for j in range(4)], [corner(up[4 * i + j], down[4 * i + j], 0.0) for j in range(4)], (DEEP,) * 4)
     for c in rest:
         c.wait()
     put(360, [more[0], more[1], more[2]], [corner(up[36], down[36], 0.0), corner(up[37], down[37], 0.0), corner(f_up, f_down, 1.0)], (16, 16, 16))
-    for i in range(9):
-        copies[i].wait()
-        put(40 * i, [buf[4 * i + j] for j in range(4)], [corner(up[4 * i + j], down[4 * i + j], 0.0) for j in range(4)], (DEEP,) * 4)
     keep = pltpu.make_async_copy(first, first_out, more_sem.at[2])
     keep.start()
     tail[EDGE:416, :] = jnp.zeros((416 - EDGE, COLS), F32)

time: 125 us -> 125 us (level)
  Pallas kernels: 55.7 us -> 53.3 us
  waiting for transfers between devices: 37.4 us -> 39.8 us
    pallas_call x1, Pallas kernels: 10.2 us -> 7.77 us  [pack(): pl.pallas_call(pack_body, out_shape=[pltpu.HBM((408, LANES), F32), jax.Sh...]
    all_to_all x1, waiting for transfers between devices: 24.5 us -> 26.8 us  [shards(): heat = lax.all_to_all(slab, WIDE, split_axis=0, concat_axis=0, tiled=True)]
  transfers between devices with their start and end apart: 7 -> 7, of which waited for: 5 -> 5; matrix products, arithmetic and copies ran while one was open for 1% -> 1% of each run, Pallas kernels for 13% -> 11%
where the time goes in v5:
time: 125 us
  Pallas kernels  53.3 us (43%)
  waiting for transfers between devices  39.8 us (32%)
  starting transfers between devices  29.1 us (23%)
  other arithmetic  1.4 us (1%)
    pallas_call x1, Pallas kernels, block(): pl.pallas_call(block_body, out_shape=[jax.ShapeDtypeStruct((2, ROWS, COLS...  28.5 us
    all_to_all x1, waiting for transfers between devices, shards(): heat = lax.all_to_all(slab, WIDE, split_axis=0, concat_axis=0, tiled=True)  26.8 us
    ppermute x6, starting transfers between devices, shifted(): return lax.ppermute(shard, axis, pairs)  21.5 us
    ppermute x6, waiting for transfers between devices, shifted(): return lax.ppermute(shard, axis, pairs)  13 us
    pallas_call x1, Pallas kernels, pack(): pl.pallas_call(pack_body, out_shape=[pltpu.HBM((408, LANES), F32), jax.Sh...  7.77 us
    all_to_all x1, starting transfers between devices, shards(): heat = lax.all_to_all(slab, WIDE, split_axis=0, concat_axis=0, tiled=True)  7.56 us
    pallas_call x1, Pallas kernels, strip(): pl.pallas_call(strip_body, out_shape=[jax.ShapeDtypeStruct((32, LANES), F...  5.63 us
    pallas_call x1, Pallas kernels, cut(): pl.pallas_call(cut_body, out_shape=[pltpu.HBM((PIECES, TICKS + 1, 32, COL...  3.96 us
  transfers between devices with their start and end apart: 7, of which 5 were waited for; matrix products, arithmetic and copies ran while one was open for 1% of the time, Pallas kernels for 11%

profile of v5, /device:TPU:37, one launch (start us, length us, event | category | flops | bytes accessed | tf_op | source)
XLA Modules:
  0.0 124.5 jit_solution(15194035756398592785)
XLA Ops:
  0.6 4.0 %cut.1 = (f32[16,11,32,128]{3,2,1,0:T(8,128)}, f32[39,16,128]{2,1,0:T(8,128)}, f32[39,16,128]{2,1,0:T(8,128)}) custom-call(f32[10,32,2048]{2,1,0:T(8,128)} %src.1, f32[36,512,128]{2,1,0:T(8,128)} %bitcast.10, f32[2,512,128]{2,1,0:T(8,128)} %motion.5, f32[512,128]{1,0:T(8,128)} %fictive.5), custom_call_target="tpu_custom_call" | custom-call | tf_op jit(solution)/shard_map/cut/pallas_call | solution.py:98
  4.6 0.0 copy-start.3
  4.6 0.0 copy-start.4
  4.6 7.6 %all-to-all-start = ((f32[16,11,32,128]{3,2,1,0:T(8,128)}), f32[16,11,32,128]{3,2,1,0:T(8,128)S(1)}, u32[]{:S(2)}, u32[]{:S(2)}) async-start(f32[16,11,32,128]{3,2,1,0:T(8,128)} %get-tuple-element.33), calls=%async_computation | async-start | bytes 5767168 | tf_op jit(solution)/shard_map/all_to_all | solution.py:587
  12.2 3.2 %collective-permute-start = (f32[39,16,128]{2,1,0:T(8,128)}, f32[39,16,128]{2,1,0:T(8,128)S(1)}, u32[]{:S(2)}, u32[]{:S(2)}) collective-permute-start(f32[39,16,128]{2,1,0:T(8,128)} %get-tuple-element.28), channel_id=1, source_target_pairs={{0,16},{16,32},{32,48},{48,64},{64,80},{80,96},{96,112},{1,17},{17... | collective-permute-start | bytes 958472 | tf_op jit(solution)/shard_map/ppermute | solution.py:35
  15.4 4.2 %collective-permute-start.1 = (f32[39,16,128]{2,1,0:T(8,128)}, f32[39,16,128]{2,1,0:T(8,128)S(1)}, u32[]{:S(2)}, u32[]{:S(2)}) collective-permute-start(f32[39,16,128]{2,1,0:T(8,128)} %get-tuple-element.29), channel_id=1, source_target_pairs={{16,0},{32,16},{48,32},{64,48},{80,64},{96,80},{112,96},{17,1},{33... | collective-permute-start | bytes 958472 | tf_op jit(solution)/shard_map/ppermute | solution.py:35
  19.6 0.1 add_convert_fusion.flags
  19.7 0.0 copy-done.3
  19.7 0.0 copy-done.4
  19.7 0.6 fusion
  20.3 0.7 pad_maximum_fusion.coef
  21.0 5.0 %collective-permute-done.up = f32[39,16,128]{2,1,0:T(8,128)S(1)} collective-permute-done((f32[39,16,128]{2,1,0:T(8,128)}, f32[39,16,128]{2,1,0:T(8,128)S(1)}, u32[]{:S(2)}, u32[]{:S(2)}) %collective-permute-start) | collective-permute-done | bytes 319520 | tf_op jit(solution)/shard_map/ppermute | solution.py:35
  26.0 0.4 collective-permute-done.1.down
  26.4 7.8 %pack.1 = (f32[408,640]{1,0:T(8,128)}, f32[1672,128]{1,0:T(8,128)}) custom-call(s32[3]{0:T(128)S(1)} %add_convert_fusion.flags, f32[36,512,128]{2,1,0:T(8,128)} %bitcast.11, f32[2,512,128]{2,1,0:T(8,128)} %motion.5, f32[512,128]{1,0:T(8,128)} %fictive.5, f32[39,16,128]{2,1,0:T(8,128)S(1)} %collective-permute-done.up, ...), custom_call_target="tpu_custom_call" | custom-call | tf_op jit(solution)/shard_map/pack/pallas_call | solution.py:173
  34.2 4.7 %collective-permute-start.4 = (f32[1672,128]{1,0:T(8,128)}, f32[1672,128]{1,0:T(8,128)}, u32[]{:S(2)}, u32[]{:S(2)}) collective-permute-start(f32[1672,128]{1,0:T(8,128)} %get-tuple-element.40), channel_id=1, source_target_pairs={{0,1},{1,2},{2,3},{3,4},{4,5},{5,6},{6,7},{7,8},{8,9},{9,10},{10,1... | collective-permute-start | bytes 2568200 | tf_op jit(solution)/shard_map/ppermute | solution.py:35
  38.9 26.8 %all-to-all-done.heat = f32[16,11,32,128]{3,2,1,0:T(8,128)S(1)} async-done(((f32[16,11,32,128]{3,2,1,0:T(8,128)}), f32[16,11,32,128]{3,2,1,0:T(8,128)S(1)}, u32[]{:S(2)}, u32[]{:S(2)}) %all-to-all-start) | async-done | bytes 2883616 | tf_op jit(solution)/shard_map/all_to_all | solution.py:587
  65.7 0.0 copy-start.1
  65.7 0.0 copy-start.2
  65.7 5.3 %collective-permute-start.3 = (f32[11,16,128]{2,1,0:T(8,128)S(1)}, f32[11,16,128]{2,1,0:T(8,128)S(1)}, u32[]{:S(2)}, u32[]{:S(2)}) collective-permute-start(f32[11,16,128]{2,1,0:T(8,128)S(1)} %get-tuple-element.55), channel_id=1, source_target_pairs={{16,0},{32,16},{48,32},{64,48},{80,64},{96,80},{112,96},{17,1},{33... | collective-permute-start | bytes 270344 | tf_op jit(solution)/shard_map/ppermute | solution.py:35
  71.0 1.9 %collective-permute-start.2 = (f32[11,16,128]{2,1,0:T(8,128)S(1)}, f32[11,16,128]{2,1,0:T(8,128)S(1)}, u32[]{:S(2)}, u32[]{:S(2)}) collective-permute-start(f32[11,16,128]{2,1,0:T(8,128)S(1)} %get-tuple-element.56), channel_id=1, source_target_pairs={{0,16},{16,32},{32,48},{48,64},{64,80},{80,96},{96,112},{1,17},{17... | collective-permute-start | bytes 270344 | tf_op jit(solution)/shard_map/ppermute | solution.py:35
  72.9 0.8 ready.1
  73.8 0.0 collective-permute-done.3.heat_down
  73.8 4.6 %collective-permute-done.2.heat_up = f32[11,16,128]{2,1,0:T(8,128)S(1)} collective-permute-done((f32[11,16,128]{2,1,0:T(8,128)S(1)}, f32[11,16,128]{2,1,0:T(8,128)S(1)}, u32[]{:S(2)}, u32[]{:S(2)}) %collective-permute-start.2) | collective-permute-done | bytes 90144 | tf_op jit(solution)/shard_map/ppermute | solution.py:35
  78.4 0.0 copy-done.1
  78.4 0.0 copy-done.2
  78.4 3.7 %prepare.1 = (f32[10,552,128]{2,1,0:T(8,128)S(1)}, f32[10,552,128]{2,1,0:T(8,128)S(1)}, f32[512,128]{1,0:T(8,128)}, f32[10,24,640]{2,1,0:T(8,128)S(1)}, f32[36,2...) custom-call(s32[3]{0:T(128)S(1)} %add_convert_fusion.flags, f32[408,640]{1,0:T(8,128)S(1)} %copy-done.2, ...), custom_call_target="tpu_custom_call" | custom-call | bytes 15000000 | tf_op jit(solution)/shard_map/prepare/pallas_call | solution.py:307
  82.0 0.0 collective-permute-done.4.got
  82.0 1.3 %lay.1 = (f32[36,24,640]{2,1,0:T(8,128)S(1)}, f32[2,24,640]{2,1,0:T(8,128)S(1)}, f32[24,640]{1,0:T(8,128)S(1)}) custom-call(s32[3]{0:T(128)S(1)} %add_convert_fusion.flags, f32[1672,128]{1,0:T(8,128)} %collective-permute-done.4.got, f32[36,24,640]{2,1,0:T(8,128)S(1)} %get-tuple-element.43.z_in, ...), custom_call_target="tpu_custom_call", output_to_operand_aliasing={{0}: (2, {}), {1}: (3, {}), {2}: (4, {})} | custom-call | bytes 6000000 | tf_op jit(solution)/shard_map/lay/pallas_call | solution.py:252
  83.4 5.6 %strip.1 = (f32[32,640]{1,0:T(8,128)S(1)}, f32[36,24,640]{2,1,0:T(8,128)S(1)}) custom-call(s32[3]{0:T(128)S(1)} %add_convert_fusion.flags, f32[25]{0:T(128)S(1)} %pad_maximum_fusion.coef, f32[36,24,640]{2,1,0:T(8,128)S(1)} %get-tuple-element.46.z_in, f32[2,24,640]{2,1,0:T(8,128)S(1)} %get-tuple-element.47.v_in, ...), custom_call_target="tpu_custom_call", output_to_operand_aliasing={{1}: (2, {})} | custom-call | bytes 21000000 | tf_op jit(solution)/shard_map/strip/pallas_call | solution.py:374
  89.0 0.0 copy-start
  89.0 2.2 %collective-permute-start.5 = (f32[32,640]{1,0:T(8,128)S(1)}, f32[32,640]{1,0:T(8,128)S(1)}, u32[]{:S(2)}, u32[]{:S(2)}) collective-permute-start(f32[32,640]{1,0:T(8,128)S(1)} %get-tuple-element.50.nodes), channel_id=1, source_target_pairs={{1,0},{2,1},{3,2},{4,3},{5,4},{6,5},{7,6},{8,7},{9,8},{10,9},{11,1... | collective-permute-start | bytes 245768 | tf_op jit(solution)/shard_map/ppermute | solution.py:35
  91.3 1.6 %edges.1.left = f32[10,2,544,128]{3,2,1,0:T(8,128)S(1)} custom-call(f32[32,640]{1,0:T(8,128)S(1)} %get-tuple-element.50.nodes), custom_call_target="tpu_custom_call" | custom-call | bytes 9000000 | tf_op jit(solution)/shard_map/edges/pallas_call | solution.py:410
  92.9 3.0 %collective-permute-done.5.beside_t = f32[32,640]{1,0:T(8,128)S(1)} collective-permute-done((f32[32,640]{1,0:T(8,128)S(1)}, f32[32,640]{1,0:T(8,128)S(1)}, u32[]{:S(2)}, u32[]{:S(2)}) %collective-permute-start.5) | collective-permute-done | bytes 81952 | tf_op jit(solution)/shard_map/ppermute | solution.py:35
  95.9 0.0 copy-done
  95.9 28.5 %block.1 = (f32[2,512,128]{2,1,0:T(8,128)}, f32[36,512,128]{2,1,0:T(8,128)}) custom-call(s32[3]{0:T(128)S(1)} %add_convert_fusion.flags, f32[25]{0:T(128)S(1)} %pad_maximum_fusion.coef, f32[36,512,128]{2,1,0:T(8,128)} %bitcast.12, f32[2,512,128]{2,1,0:T(8,128)S(1)} %copy-done, f32[39,16,128]{2,1,0:T(8,128)S(1)} %collective-permute-done.up, ...), custom_call_target="tpu_custom_call" | custom-call | bytes 84000000 | tf_op jit(solution)/shard_map/block/pallas_call | solution.py:554
  (1 shorter events, 0.0 us)
Async XLA Ops:
  4.6 15.1 %copy-start.3 = (f32[12]{0:T(128)S(1)}, f32[12]{0:T(128)}, u32[]{:S(2)}) copy-start(f32[12]{0:T(128)} %param.10) | copy-start | bytes 148
  4.6 15.1 %copy-start.4 = (f32[12]{0:T(128)S(1)}, f32[12]{0:T(128)}, u32[]{:S(2)}) copy-start(f32[12]{0:T(128)} %param.11) | copy-start | bytes 148
  4.6 61.1 %all-to-all-start = ((f32[16,11,32,128]{3,2,1,0:T(8,128)}), f32[16,11,32,128]{3,2,1,0:T(8,128)S(1)}, u32[]{:S(2)}, u32[]{:S(2)}) async-start(f32[16,11,32,128]{3,2,1,0:T(8,128)} %get-tuple-element.33), calls=%async_computation | async-start | bytes 5767168 | tf_op jit(solution)/shard_map/all_to_all | solution.py:587
  12.2 13.8 %collective-permute-start = (f32[39,16,128]{2,1,0:T(8,128)}, f32[39,16,128]{2,1,0:T(8,128)S(1)}, u32[]{:S(2)}, u32[]{:S(2)}) collective-permute-start(f32[39,16,128]{2,1,0:T(8,128)} %get-tuple-element.28), channel_id=1, source_target_pairs={{0,16},{16,32},{32,48},{48,64},{64,80},{80,96},{96,112},{1,17},{17... | collective-permute-start | bytes 958472 | tf_op jit(solution)/shard_map/ppermute | solution.py:35
  15.4 11.0 %collective-permute-start.1 = (f32[39,16,128]{2,1,0:T(8,128)}, f32[39,16,128]{2,1,0:T(8,128)S(1)}, u32[]{:S(2)}, u32[]{:S(2)}) collective-permute-start(f32[39,16,128]{2,1,0:T(8,128)} %get-tuple-element.29), channel_id=1, source_target_pairs={{16,0},{32,16},{48,32},{64,48},{80,64},{96,80},{112,96},{17,1},{33... | collective-permute-start | bytes 958472 | tf_op jit(solution)/shard_map/ppermute | solution.py:35
  34.2 47.9 %collective-permute-start.4 = (f32[1672,128]{1,0:T(8,128)}, f32[1672,128]{1,0:T(8,128)}, u32[]{:S(2)}, u32[]{:S(2)}) collective-permute-start(f32[1672,128]{1,0:T(8,128)} %get-tuple-element.40), channel_id=1, source_target_pairs={{0,1},{1,2},{2,3},{3,4},{4,5},{5,6},{6,7},{7,8},{8,9},{9,10},{10,1... | collective-permute-start | bytes 2568200 | tf_op jit(solution)/shard_map/ppermute | solution.py:35
  65.7 12.7 %copy-start.1 = (f32[512,128]{1,0:T(8,128)S(1)}, f32[512,128]{1,0:T(8,128)}, u32[]{:S(2)}) copy-start(f32[512,128]{1,0:T(8,128)} %fictive.5) | copy-start | bytes 786436
  65.7 12.7 %copy-start.2 = (f32[408,640]{1,0:T(8,128)S(1)}, f32[408,640]{1,0:T(8,128)}, u32[]{:S(2)}) copy-start(f32[408,640]{1,0:T(8,128)} %get-tuple-element.32.first) | copy-start | bytes 3133444
  65.7 8.1 %collective-permute-start.3 = (f32[11,16,128]{2,1,0:T(8,128)S(1)}, f32[11,16,128]{2,1,0:T(8,128)S(1)}, u32[]{:S(2)}, u32[]{:S(2)}) collective-permute-start(f32[11,16,128]{2,1,0:T(8,128)S(1)} %get-tuple-element.55), channel_id=1, source_target_pairs={{16,0},{32,16},{48,32},{64,48},{80,64},{96,80},{112,96},{17,1},{33... | collective-permute-start | bytes 270344 | tf_op jit(solution)/shard_map/ppermute | solution.py:35
  71.0 7.4 %collective-permute-start.2 = (f32[11,16,128]{2,1,0:T(8,128)S(1)}, f32[11,16,128]{2,1,0:T(8,128)S(1)}, u32[]{:S(2)}, u32[]{:S(2)}) collective-permute-start(f32[11,16,128]{2,1,0:T(8,128)S(1)} %get-tuple-element.56), channel_id=1, source_target_pairs={{0,16},{16,32},{32,48},{48,64},{64,80},{80,96},{96,112},{1,17},{17... | collective-permute-start | bytes 270344 | tf_op jit(solution)/shard_map/ppermute | solution.py:35
  89.0 6.8 %copy-start = (f32[2,512,128]{2,1,0:T(8,128)S(1)}, f32[2,512,128]{2,1,0:T(8,128)}, u32[]{:S(2)}) copy-start(f32[2,512,128]{2,1,0:T(8,128)} %motion.5) | copy-start | bytes 1572868
  89.0 6.8 %collective-permute-start.5 = (f32[32,640]{1,0:T(8,128)S(1)}, f32[32,640]{1,0:T(8,128)S(1)}, u32[]{:S(2)}, u32[]{:S(2)}) collective-permute-start(f32[32,640]{1,0:T(8,128)S(1)} %get-tuple-element.50.nodes), channel_id=1, source_target_pairs={{1,0},{2,1},{3,2},{4,3},{5,4},{6,5},{7,6},{8,7},{9,8},{10,9},{11,1... | collective-permute-start | bytes 245768 | tf_op jit(solution)/shard_map/ppermute | solution.py:35
